TPU v7x, 128 devices: a whole 4x4x4 slice. The times are simulated.
128 devices in a mesh: seq: 32 (over x, y, core), head: 4 (over z).
Axes of the slice: x: 4, y: 4, z: 4, core: 2. Of those that a mesh axis runs over, the one named last changes fastest.
Arguments:
- tokens: bfloat16 [8192, 2560], P(('seq', 'head')), may hold values from -6 to 6
- input_gain: float32 [2560], replicated, may hold values from 0.5 to 1.5
- gate_weight: bfloat16 [2560, 5120], P(None, 'head'), may hold values from -0.125 to 0.125
- inner_weight: bfloat16 [2560, 5120], P(None, 'head'), may hold values from -0.125 to 0.125
- state_weight: bfloat16 [2560, 256], replicated, may hold values from -0.125 to 0.125
- step_weight: bfloat16 [2560, 80], P(None, 'head'), may hold values from -0.125 to 0.125
- step_bias: float32 [80], P('head'), may hold values from -1 to 1
- decay_exponent: int32 [80], P('head'), may hold values from 64 to 65024
- conv_inner: float32 [4, 5120], P(None, 'head'), may hold values from -3 to 3
- conv_state: float32 [4, 256], replicated, may hold values from -3 to 3
- skip_gain: float32 [80], P('head'), may hold values from 0.5 to 1.5
- norm_gain: float32 [5120], P('head'), may hold values from 0.5 to 1.5
- out_weight: bfloat16 [5120, 2560], P('head'), may hold values from -0.078125 to 0.078125
- passage_lengths: int32 [64], replicated, may hold values from 1 to 4096, 8192 in all
Outputs:
- mixed: bfloat16 [8192, 2560], P(('seq', 'head'))
Inputs may be any that keep to these rules, and one draw needn't show every extreme that they name: `passage_lengths`: the 64 passages lie end to end and fill all 8192 tokens; the longest has exactly 4096 tokens.
All inputs are finite; a program needn't handle non-finite values.
Results may differ from a plain program's by a relative error of at most 0.017.
Values may be sent and summed in bfloat16 or wider, within the bound.
No kernel may reach another device: no remote copies, remote signals or barrier semaphores. Data moves between devices by JAX's collectives and lax.ppermute only.
A program may use at most 128 MiB of HBM per device.

v0:
```python
import jax
import jax.numpy as jnp
from jax import lax
from jax.sharding import PartitionSpec as P

H = 80
P_SIZE = 64
N = 128
K = 4
Q = 256


PRECISE = lax.Precision.HIGHEST


def from_behind(block, axis, distance):
    devices = range(lax.axis_size(axis))
    route = [(i - distance, i) for i in devices if i - distance in devices]
    return lax.ppermute(block, axis, route)


def passage_ids(lengths, positions):
    starts = jnp.cumsum(lengths) - lengths
    return jnp.sum((positions[:, None] >= starts[None, :]).astype(jnp.int32), axis=1) - 1


def causal_conv(padded, weights, ids, padded_ids):
    length = ids.shape[0]
    total = jnp.zeros((length, padded.shape[1]), jnp.float32)
    for offset in range(K):
        first = K - 1 - offset
        shifted = padded[first : first + length]
        agrees = (padded_ids[first : first + length] == ids).astype(jnp.float32)
        total = total + weights[offset][None, :] * shifted * agrees[:, None]
    return jax.nn.silu(total)


def ssd_group(state, block):
    inner_part, step_part, log_part, in_part, out_part, ids_part, prev_id = block
    cumulative = jnp.cumsum(log_part, axis=0)
    count = ids_part.shape[0]
    order = jnp.arange(count)
    pairs_mask = (ids_part[:, None] == ids_part[None, :]) & (order[:, None] >= order[None, :])
    cum_heads = cumulative.T
    gaps = cum_heads[:, :, None] - cum_heads[:, None, :]
    decay_mat = jnp.exp(jnp.where(pairs_mask[None, :, :], gaps, -1e30))
    scores = jnp.dot(out_part, in_part.T, preferred_element_type=jnp.float32)
    weighted = (decay_mat * scores[None, :, :]).astype(jnp.bfloat16)
    scaled_in = (
        (inner_part.astype(jnp.float32) * step_part[:, :, None])
        .transpose(1, 0, 2)
        .astype(jnp.bfloat16)
    )
    intra = jnp.einsum(
        "hts,hsp->htp", weighted, scaled_in, preferred_element_type=jnp.float32
    ).transpose(1, 0, 2)
    keep_first = (ids_part == prev_id).astype(jnp.float32)
    decay_first = jnp.exp(cumulative) * keep_first[:, None]
    inter = (
        jnp.einsum("tn,hnp->thp", out_part.astype(jnp.float32), state, precision=PRECISE)
        * decay_first[:, :, None]
    )
    tail_decay = (
        jnp.exp(cumulative[-1][None, :] - cumulative)
        * (ids_part == ids_part[-1]).astype(jnp.float32)[:, None]
    )
    carry_keep = jnp.exp(cumulative[-1]) * (ids_part[-1] == prev_id).astype(jnp.float32)
    tail_in = (tail_decay.T[:, :, None] * scaled_in.astype(jnp.float32)).astype(jnp.bfloat16)
    new_state = state * carry_keep[:, None, None] + jnp.einsum(
        "sn,hsp->hnp", in_part, tail_in, preferred_element_type=jnp.float32
    )
    return (new_state, intra + inter)


def on_device(
    tokens,
    input_gain,
    gate_weight,
    inner_weight,
    state_weight,
    step_weight,
    step_bias,
    decay_exponent,
    conv_inner,
    conv_state,
    skip_gain,
    norm_gain,
    out_weight,
    passage_lengths,
):
    tok_float = tokens.astype(jnp.float32)
    normed = (
        tok_float
        * lax.rsqrt(jnp.mean(tok_float * tok_float, axis=-1, keepdims=True) + 1e-05)
        * input_gain
    ).astype(jnp.bfloat16)
    gathered = lax.all_gather(normed, "head", axis=0, tiled=True)
    gate_vals = jnp.dot(gathered, gate_weight, preferred_element_type=jnp.float32).astype(
        jnp.bfloat16
    )
    inner_raw = jnp.dot(gathered, inner_weight, preferred_element_type=jnp.float32).astype(
        jnp.bfloat16
    )
    state_raw = jnp.dot(gathered, state_weight, preferred_element_type=jnp.float32).astype(
        jnp.bfloat16
    )
    step_raw = jnp.dot(gathered, step_weight, preferred_element_type=jnp.float32)
    length = gathered.shape[0]
    heads_here = step_weight.shape[1]
    rim = from_behind((inner_raw[length - (K - 1) :], state_raw[length - (K - 1) :]), "seq", 1)
    first_pos = lax.axis_index("seq") * length
    padded_pos = first_pos + jnp.arange(-(K - 1), length, dtype=jnp.int32)
    padded_ids = passage_ids(passage_lengths, padded_pos)
    ids = padded_ids[K - 1 :]
    prior_id = padded_ids[K - 2]
    inner_pad = jnp.concatenate([rim[0], inner_raw]).astype(jnp.float32)
    state_pad = jnp.concatenate([rim[1], state_raw]).astype(jnp.float32)
    inner_conv = causal_conv(inner_pad, conv_inner, ids, padded_ids).astype(jnp.bfloat16)
    state_conv = causal_conv(state_pad, conv_state, ids, padded_ids).astype(jnp.bfloat16)
    state_in = state_conv[:, :N]
    state_out = state_conv[:, N:]
    step_size = jax.nn.softplus(step_raw + step_bias)
    log_decay = -step_size * (decay_exponent.astype(jnp.float32) * 2.0 ** (-21))
    groups = length // Q
    heads_x = inner_conv.reshape(length, heads_here, P_SIZE)
    id_groups = ids.reshape(groups, Q)
    prev_ids = jnp.concatenate([jnp.reshape(prior_id, (1,)), id_groups[:-1, -1]])
    start_state = jnp.zeros((heads_here, N, P_SIZE), jnp.float32)
    blocks = (
        heads_x.reshape(groups, Q, heads_here, P_SIZE),
        step_size.reshape(groups, Q, heads_here),
        log_decay.reshape(groups, Q, heads_here),
        state_in.reshape(groups, Q, N),
        state_out.reshape(groups, Q, N),
        id_groups,
        prev_ids,
    )
    local_state, pieces = lax.scan(ssd_group, start_state, blocks)
    cumulative = jnp.cumsum(log_decay, axis=0)
    keep_first = (ids == prior_id).astype(jnp.float32)
    decay_first = jnp.exp(cumulative) * keep_first[:, None]
    total_decay = decay_first[-1]

    def pass_state(turn, incoming):
        outgoing = total_decay[:, None, None] * incoming + local_state
        return from_behind(outgoing, "seq", 1)

    incoming = lax.fori_loop(0, lax.axis_size("seq") - 1, pass_state, jnp.zeros_like(local_state))
    carried = (
        jnp.einsum("tn,hnp->thp", state_out.astype(jnp.float32), incoming, precision=PRECISE)
        * decay_first[:, :, None]
    )
    ssd_out = (
        pieces.reshape(length, heads_here, P_SIZE)
        + carried
        + skip_gain[None, :, None] * heads_x.astype(jnp.float32)
    )
    gated = ssd_out.reshape(length, heads_here * P_SIZE) * jax.nn.silu(
        gate_vals.astype(jnp.float32)
    )
    squares = lax.psum(jnp.sum(gated * gated, axis=1), "head")
    normed_out = (gated * lax.rsqrt(squares / (H * P_SIZE) + 1e-05)[:, None] * norm_gain).astype(
        jnp.bfloat16
    )
    return lax.psum_scatter(
        jnp.dot(normed_out, out_weight, preferred_element_type=jnp.float32),
        "head",
        scatter_dimension=0,
        tiled=True,
    ).astype(jnp.bfloat16)


def solution(mesh):
    in_specs = (
        P(("seq", "head"), None),
        P(),
        P(None, "head"),
        P(None, "head"),
        P(),
        P(None, "head"),
        P("head"),
        P("head"),
        P(None, "head"),
        P(),
        P("head"),
        P("head"),
        P("head", None),
        P(),
    )
    out_specs = P(("seq", "head"), None)
    return jax.shard_map(
        on_device, mesh=mesh, in_specs=in_specs, out_specs=out_specs, check_vma=False
    )
```

profile of v0, /device:TPU:1, one launch (start us, length us, event | category | flops | bytes accessed | tf_op | source)
XLA Modules:
  0.0 571.4 jit_solution(14266911771963980730)
XLA Ops:
  15.8 21.3 %all-gather.2.cloned.1.call-done = bf16[256,2560]{1,0:T(8,128)(2,1)} async-done(((bf16[64,2560]{1,0:T(8,128)(2,1)}), bf16[256,2560]{1,0:T(8,128)(2,1)}) %all-gather.2.cloned.1.call-update) | async-done | bytes 1310736 | tf_op jit(solution)/shard_map/all_gather | solution.py:97
  62.9 395.1 %while.2 = (s32[]{:T(128)}, f32[20,128,64]{1,2,0:T(8,128)S(1)}, f32[1,20]{1,0:T(1,128)S(1)}, f32[20,128,64]{1,2,0:T(8,128)S(1)}, s32[]{:T(128)}) while((s32[]{:T(128)}, f32[20,128,64]{1,2,0:T(8,128)S(1)}, f32[1,20]{1,0:T(1,128)S(1)}, f32[20,128,64]{1,2,0:T(8,128)S(1)}, s32[]{:T(128)}) %tuple.45), condition=%wide.region_6.7_spmd, body=%wide.region_5.6_spmd.sunk | while | flops 327682 | bytes 4587701 | solution.py:148
  78.6 7.5 %collective-permute-done = f32[20,128,64]{1,2,0:T(8,128)S(1)} collective-permute-done((f32[20,128,64]{1,2,0:T(8,128)S(1)}, f32[20,128,64]{1,2,0:T(8,128)S(1)}, u32[]{:S(2)}, u32[]{:S(2)}) %collective-permute-start) | collective-permute-done | bytes 655392 | tf_op jit(solution)/shard_map/while/body/eval_jaxpr/ppermute | solution.py:19
  90.6 7.5 %collective-permute-done = f32[20,128,64]{1,2,0:T(8,128)S(1)} collective-permute-done((f32[20,128,64]{1,2,0:T(8,128)S(1)}, f32[20,128,64]{1,2,0:T(8,128)S(1)}, u32[]{:S(2)}, u32[]{:S(2)}) %collective-permute-start) | collective-permute-done | bytes 655392 | tf_op jit(solution)/shard_map/while/body/eval_jaxpr/ppermute | solution.py:19
  102.7 7.5 %collective-permute-done = f32[20,128,64]{1,2,0:T(8,128)S(1)} collective-permute-done((f32[20,128,64]{1,2,0:T(8,128)S(1)}, f32[20,128,64]{1,2,0:T(8,128)S(1)}, u32[]{:S(2)}, u32[]{:S(2)}) %collective-permute-start) | collective-permute-done | bytes 655392 | tf_op jit(solution)/shard_map/while/body/eval_jaxpr/ppermute | solution.py:19
  114.7 7.5 %collective-permute-done = f32[20,128,64]{1,2,0:T(8,128)S(1)} collective-permute-done((f32[20,128,64]{1,2,0:T(8,128)S(1)}, f32[20,128,64]{1,2,0:T(8,128)S(1)}, u32[]{:S(2)}, u32[]{:S(2)}) %collective-permute-start) | collective-permute-done | bytes 655392 | tf_op jit(solution)/shard_map/while/body/eval_jaxpr/ppermute | solution.py:19
  126.8 7.5 %collective-permute-done = f32[20,128,64]{1,2,0:T(8,128)S(1)} collective-permute-done((f32[20,128,64]{1,2,0:T(8,128)S(1)}, f32[20,128,64]{1,2,0:T(8,128)S(1)}, u32[]{:S(2)}, u32[]{:S(2)}) %collective-permute-start) | collective-permute-done | bytes 655392 | tf_op jit(solution)/shard_map/while/body/eval_jaxpr/ppermute | solution.py:19
  138.8 7.5 %collective-permute-done = f32[20,128,64]{1,2,0:T(8,128)S(1)} collective-permute-done((f32[20,128,64]{1,2,0:T(8,128)S(1)}, f32[20,128,64]{1,2,0:T(8,128)S(1)}, u32[]{:S(2)}, u32[]{:S(2)}) %collective-permute-start) | collective-permute-done | bytes 655392 | tf_op jit(solution)/shard_map/while/body/eval_jaxpr/ppermute | solution.py:19
  150.8 7.5 %collective-permute-done = f32[20,128,64]{1,2,0:T(8,128)S(1)} collective-permute-done((f32[20,128,64]{1,2,0:T(8,128)S(1)}, f32[20,128,64]{1,2,0:T(8,128)S(1)}, u32[]{:S(2)}, u32[]{:S(2)}) %collective-permute-start) | collective-permute-done | bytes 655392 | tf_op jit(solution)/shard_map/while/body/eval_jaxpr/ppermute | solution.py:19
  162.9 7.5 %collective-permute-done = f32[20,128,64]{1,2,0:T(8,128)S(1)} collective-permute-done((f32[20,128,64]{1,2,0:T(8,128)S(1)}, f32[20,128,64]{1,2,0:T(8,128)S(1)}, u32[]{:S(2)}, u32[]{:S(2)}) %collective-permute-start) | collective-permute-done | bytes 655392 | tf_op jit(solution)/shard_map/while/body/eval_jaxpr/ppermute | solution.py:19
  174.9 7.5 %collective-permute-done = f32[20,128,64]{1,2,0:T(8,128)S(1)} collective-permute-done((f32[20,128,64]{1,2,0:T(8,128)S(1)}, f32[20,128,64]{1,2,0:T(8,128)S(1)}, u32[]{:S(2)}, u32[]{:S(2)}) %collective-permute-start) | collective-permute-done | bytes 655392 | tf_op jit(solution)/shard_map/while/body/eval_jaxpr/ppermute | solution.py:19
  187.0 7.5 %collective-permute-done = f32[20,128,64]{1,2,0:T(8,128)S(1)} collective-permute-done((f32[20,128,64]{1,2,0:T(8,128)S(1)}, f32[20,128,64]{1,2,0:T(8,128)S(1)}, u32[]{:S(2)}, u32[]{:S(2)}) %collective-permute-start) | collective-permute-done | bytes 655392 | tf_op jit(solution)/shard_map/while/body/eval_jaxpr/ppermute | solution.py:19
  199.0 7.5 %collective-permute-done = f32[20,128,64]{1,2,0:T(8,128)S(1)} collective-permute-done((f32[20,128,64]{1,2,0:T(8,128)S(1)}, f32[20,128,64]{1,2,0:T(8,128)S(1)}, u32[]{:S(2)}, u32[]{:S(2)}) %collective-permute-start) | collective-permute-done | bytes 655392 | tf_op jit(solution)/shard_map/while/body/eval_jaxpr/ppermute | solution.py:19
  211.0 7.5 %collective-permute-done = f32[20,128,64]{1,2,0:T(8,128)S(1)} collective-permute-done((f32[20,128,64]{1,2,0:T(8,128)S(1)}, f32[20,128,64]{1,2,0:T(8,128)S(1)}, u32[]{:S(2)}, u32[]{:S(2)}) %collective-permute-start) | collective-permute-done | bytes 655392 | tf_op jit(solution)/shard_map/while/body/eval_jaxpr/ppermute | solution.py:19
  223.1 7.5 %collective-permute-done = f32[20,128,64]{1,2,0:T(8,128)S(1)} collective-permute-done((f32[20,128,64]{1,2,0:T(8,128)S(1)}, f32[20,128,64]{1,2,0:T(8,128)S(1)}, u32[]{:S(2)}, u32[]{:S(2)}) %collective-permute-start) | collective-permute-done | bytes 655392 | tf_op jit(solution)/shard_map/while/body/eval_jaxpr/ppermute | solution.py:19
  235.1 7.5 %collective-permute-done = f32[20,128,64]{1,2,0:T(8,128)S(1)} collective-permute-done((f32[20,128,64]{1,2,0:T(8,128)S(1)}, f32[20,128,64]{1,2,0:T(8,128)S(1)}, u32[]{:S(2)}, u32[]{:S(2)}) %collective-permute-start) | collective-permute-done | bytes 655392 | tf_op jit(solution)/shard_map/while/body/eval_jaxpr/ppermute | solution.py:19
  247.1 7.5 %collective-permute-done = f32[20,128,64]{1,2,0:T(8,128)S(1)} collective-permute-done((f32[20,128,64]{1,2,0:T(8,128)S(1)}, f32[20,128,64]{1,2,0:T(8,128)S(1)}, u32[]{:S(2)}, u32[]{:S(2)}) %collective-permute-start) | collective-permute-done | bytes 655392 | tf_op jit(solution)/shard_map/while/body/eval_jaxpr/ppermute | solution.py:19
  259.2 7.5 %collective-permute-done = f32[20,128,64]{1,2,0:T(8,128)S(1)} collective-permute-done((f32[20,128,64]{1,2,0:T(8,128)S(1)}, f32[20,128,64]{1,2,0:T(8,128)S(1)}, u32[]{:S(2)}, u32[]{:S(2)}) %collective-permute-start) | collective-permute-done | bytes 655392 | tf_op jit(solution)/shard_map/while/body/eval_jaxpr/ppermute | solution.py:19
  309.0 7.5 %collective-permute-done = f32[20,128,64]{1,2,0:T(8,128)S(1)} collective-permute-done((f32[20,128,64]{1,2,0:T(8,128)S(1)}, f32[20,128,64]{1,2,0:T(8,128)S(1)}, u32[]{:S(2)}, u32[]{:S(2)}) %collective-permute-start) | collective-permute-done | bytes 655392 | tf_op jit(solution)/shard_map/while/body/eval_jaxpr/ppermute | solution.py:19
  337.3 7.5 %collective-permute-done = f32[20,128,64]{1,2,0:T(8,128)S(1)} collective-permute-done((f32[20,128,64]{1,2,0:T(8,128)S(1)}, f32[20,128,64]{1,2,0:T(8,128)S(1)}, u32[]{:S(2)}, u32[]{:S(2)}) %collective-permute-start) | collective-permute-done | bytes 655392 | tf_op jit(solution)/shard_map/while/body/eval_jaxpr/ppermute | solution.py:19
  351.4 7.5 %collective-permute-done = f32[20,128,64]{1,2,0:T(8,128)S(1)} collective-permute-done((f32[20,128,64]{1,2,0:T(8,128)S(1)}, f32[20,128,64]{1,2,0:T(8,128)S(1)}, u32[]{:S(2)}, u32[]{:S(2)}) %collective-permute-start) | collective-permute-done | bytes 655392 | tf_op jit(solution)/shard_map/while/body/eval_jaxpr/ppermute | solution.py:19
  365.6 7.5 %collective-permute-done = f32[20,128,64]{1,2,0:T(8,128)S(1)} collective-permute-done((f32[20,128,64]{1,2,0:T(8,128)S(1)}, f32[20,128,64]{1,2,0:T(8,128)S(1)}, u32[]{:S(2)}, u32[]{:S(2)}) %collective-permute-start) | collective-permute-done | bytes 655392 | tf_op jit(solution)/shard_map/while/body/eval_jaxpr/ppermute | solution.py:19
  379.7 7.5 %collective-permute-done = f32[20,128,64]{1,2,0:T(8,128)S(1)} collective-permute-done((f32[20,128,64]{1,2,0:T(8,128)S(1)}, f32[20,128,64]{1,2,0:T(8,128)S(1)}, u32[]{:S(2)}, u32[]{:S(2)}) %collective-permute-start) | collective-permute-done | bytes 655392 | tf_op jit(solution)/shard_map/while/body/eval_jaxpr/ppermute | solution.py:19
  486.4 76.3 %reduce-scatter.2.cloned.1.call-done = f32[64,2560]{1,0:T(8,128)} async-done(((f32[256,2560]{1,0:T(8,128)}), f32[64,2560]{1,0:T(8,128)}) %reduce-scatter.2.cloned.1.call-update) | async-done | bytes 655376 | tf_op jit(solution)/shard_map/reduce_scatter | solution.py:165
  (181 shorter events, 300.4 us)
Async XLA Ops:
  6.6 30.5 %all-gather.2.cloned.1.call-start = ((), (), s32[]{:S(2)}) async-start(), calls=%async_computation.1 | async-start | bytes 1638400 | tf_op jit(solution)/shard_map/all_gather | solution.py:97
  9.8 552.9 %reduce-scatter.2.cloned.1.call-start = ((), (), s32[]{:S(2)}) async-start(), calls=%async_computation.2 | async-start | bytes 3276800 | tf_op jit(solution)/shard_map/reduce_scatter | solution.py:165
  41.2 12.9 %collective-permute-start.1 = (bf16[3,256]{1,0:T(4,128)(2,1)}, bf16[3,256]{1,0:T(4,128)(2,1)}, u32[]{:S(2)}, u32[]{:S(2)}) collective-permute-start(bf16[3,256]{1,0:T(4,128)(2,1)} %slice.133), channel_id=1, source_target_pairs={{0,4},{4,8},{8,12},{12,16},{16,20},{20,24},{24,28},{28,32},{32,36}... | collective-permute-start | bytes 4616 | tf_op jit(solution)/shard_map/ppermute | solution.py:19
  74.2 11.9 %collective-permute-start = (f32[20,128,64]{1,2,0:T(8,128)S(1)}, f32[20,128,64]{1,2,0:T(8,128)S(1)}, u32[]{:S(2)}, u32[]{:S(2)}) collective-permute-start(f32[20,128,64]{1,2,0:T(8,128)S(1)} %multiply_add_fusion.2), channel_id=1, source_target_pairs={{0,4},{4,8},{8,12},{12,16},{16,20},{20,24},{24,28},{28,32},{32,36}... | collective-permute-start | bytes 1966088 | tf_op jit(solution)/shard_map/while/body/eval_jaxpr/ppermute | solution.py:19
  86.2 11.9 %collective-permute-start = (f32[20,128,64]{1,2,0:T(8,128)S(1)}, f32[20,128,64]{1,2,0:T(8,128)S(1)}, u32[]{:S(2)}, u32[]{:S(2)}) collective-permute-start(f32[20,128,64]{1,2,0:T(8,128)S(1)} %multiply_add_fusion.2), channel_id=1, source_target_pairs={{0,4},{4,8},{8,12},{12,16},{16,20},{20,24},{24,28},{28,32},{32,36}... | collective-permute-start | bytes 1966088 | tf_op jit(solution)/shard_map/while/body/eval_jaxpr/ppermute | solution.py:19
  98.3 11.9 %collective-permute-start = (f32[20,128,64]{1,2,0:T(8,128)S(1)}, f32[20,128,64]{1,2,0:T(8,128)S(1)}, u32[]{:S(2)}, u32[]{:S(2)}) collective-permute-start(f32[20,128,64]{1,2,0:T(8,128)S(1)} %multiply_add_fusion.2), channel_id=1, source_target_pairs={{0,4},{4,8},{8,12},{12,16},{16,20},{20,24},{24,28},{28,32},{32,36}... | collective-permute-start | bytes 1966088 | tf_op jit(solution)/shard_map/while/body/eval_jaxpr/ppermute | solution.py:19
  110.3 11.9 %collective-permute-start = (f32[20,128,64]{1,2,0:T(8,128)S(1)}, f32[20,128,64]{1,2,0:T(8,128)S(1)}, u32[]{:S(2)}, u32[]{:S(2)}) collective-permute-start(f32[20,128,64]{1,2,0:T(8,128)S(1)} %multiply_add_fusion.2), channel_id=1, source_target_pairs={{0,4},{4,8},{8,12},{12,16},{16,20},{20,24},{24,28},{28,32},{32,36}... | collective-permute-start | bytes 1966088 | tf_op jit(solution)/shard_map/while/body/eval_jaxpr/ppermute | solution.py:19
  122.4 11.9 %collective-permute-start = (f32[20,128,64]{1,2,0:T(8,128)S(1)}, f32[20,128,64]{1,2,0:T(8,128)S(1)}, u32[]{:S(2)}, u32[]{:S(2)}) collective-permute-start(f32[20,128,64]{1,2,0:T(8,128)S(1)} %multiply_add_fusion.2), channel_id=1, source_target_pairs={{0,4},{4,8},{8,12},{12,16},{16,20},{20,24},{24,28},{28,32},{32,36}... | collective-permute-start | bytes 1966088 | tf_op jit(solution)/shard_map/while/body/eval_jaxpr/ppermute | solution.py:19
  134.4 11.9 %collective-permute-start = (f32[20,128,64]{1,2,0:T(8,128)S(1)}, f32[20,128,64]{1,2,0:T(8,128)S(1)}, u32[]{:S(2)}, u32[]{:S(2)}) collective-permute-start(f32[20,128,64]{1,2,0:T(8,128)S(1)} %multiply_add_fusion.2), channel_id=1, source_target_pairs={{0,4},{4,8},{8,12},{12,16},{16,20},{20,24},{24,28},{28,32},{32,36}... | collective-permute-start | bytes 1966088 | tf_op jit(solution)/shard_map/while/body/eval_jaxpr/ppermute | solution.py:19
  146.4 11.9 %collective-permute-start = (f32[20,128,64]{1,2,0:T(8,128)S(1)}, f32[20,128,64]{1,2,0:T(8,128)S(1)}, u32[]{:S(2)}, u32[]{:S(2)}) collective-permute-start(f32[20,128,64]{1,2,0:T(8,128)S(1)} %multiply_add_fusion.2), channel_id=1, source_target_pairs={{0,4},{4,8},{8,12},{12,16},{16,20},{20,24},{24,28},{28,32},{32,36}... | collective-permute-start | bytes 1966088 | tf_op jit(solution)/shard_map/while/body/eval_jaxpr/ppermute | solution.py:19
  158.5 11.9 %collective-permute-start = (f32[20,128,64]{1,2,0:T(8,128)S(1)}, f32[20,128,64]{1,2,0:T(8,128)S(1)}, u32[]{:S(2)}, u32[]{:S(2)}) collective-permute-start(f32[20,128,64]{1,2,0:T(8,128)S(1)} %multiply_add_fusion.2), channel_id=1, source_target_pairs={{0,4},{4,8},{8,12},{12,16},{16,20},{20,24},{24,28},{28,32},{32,36}... | collective-permute-start | bytes 1966088 | tf_op jit(solution)/shard_map/while/body/eval_jaxpr/ppermute | solution.py:19
  170.5 11.9 %collective-permute-start = (f32[20,128,64]{1,2,0:T(8,128)S(1)}, f32[20,128,64]{1,2,0:T(8,128)S(1)}, u32[]{:S(2)}, u32[]{:S(2)}) collective-permute-start(f32[20,128,64]{1,2,0:T(8,128)S(1)} %multiply_add_fusion.2), channel_id=1, source_target_pairs={{0,4},{4,8},{8,12},{12,16},{16,20},{20,24},{24,28},{28,32},{32,36}... | collective-permute-start | bytes 1966088 | tf_op jit(solution)/shard_map/while/body/eval_jaxpr/ppermute | solution.py:19
  182.6 11.9 %collective-permute-start = (f32[20,128,64]{1,2,0:T(8,128)S(1)}, f32[20,128,64]{1,2,0:T(8,128)S(1)}, u32[]{:S(2)}, u32[]{:S(2)}) collective-permute-start(f32[20,128,64]{1,2,0:T(8,128)S(1)} %multiply_add_fusion.2), channel_id=1, source_target_pairs={{0,4},{4,8},{8,12},{12,16},{16,20},{20,24},{24,28},{28,32},{32,36}... | collective-permute-start | bytes 1966088 | tf_op jit(solution)/shard_map/while/body/eval_jaxpr/ppermute | solution.py:19
  302.9 13.6 %collective-permute-start = (f32[20,128,64]{1,2,0:T(8,128)S(1)}, f32[20,128,64]{1,2,0:T(8,128)S(1)}, u32[]{:S(2)}, u32[]{:S(2)}) collective-permute-start(f32[20,128,64]{1,2,0:T(8,128)S(1)} %multiply_add_fusion.2), channel_id=1, source_target_pairs={{0,4},{4,8},{8,12},{12,16},{16,20},{20,24},{24,28},{28,32},{32,36}... | collective-permute-start | bytes 1966088 | tf_op jit(solution)/shard_map/while/body/eval_jaxpr/ppermute | solution.py:19
  316.6 14.0 %collective-permute-start = (f32[20,128,64]{1,2,0:T(8,128)S(1)}, f32[20,128,64]{1,2,0:T(8,128)S(1)}, u32[]{:S(2)}, u32[]{:S(2)}) collective-permute-start(f32[20,128,64]{1,2,0:T(8,128)S(1)} %multiply_add_fusion.2), channel_id=1, source_target_pairs={{0,4},{4,8},{8,12},{12,16},{16,20},{20,24},{24,28},{28,32},{32,36}... | collective-permute-start | bytes 1966088 | tf_op jit(solution)/shard_map/while/body/eval_jaxpr/ppermute | solution.py:19
  330.8 14.0 %collective-permute-start = (f32[20,128,64]{1,2,0:T(8,128)S(1)}, f32[20,128,64]{1,2,0:T(8,128)S(1)}, u32[]{:S(2)}, u32[]{:S(2)}) collective-permute-start(f32[20,128,64]{1,2,0:T(8,128)S(1)} %multiply_add_fusion.2), channel_id=1, source_target_pairs={{0,4},{4,8},{8,12},{12,16},{16,20},{20,24},{24,28},{28,32},{32,36}... | collective-permute-start | bytes 1966088 | tf_op jit(solution)/shard_map/while/body/eval_jaxpr/ppermute | solution.py:19
  344.9 14.0 %collective-permute-start = (f32[20,128,64]{1,2,0:T(8,128)S(1)}, f32[20,128,64]{1,2,0:T(8,128)S(1)}, u32[]{:S(2)}, u32[]{:S(2)}) collective-permute-start(f32[20,128,64]{1,2,0:T(8,128)S(1)} %multiply_add_fusion.2), channel_id=1, source_target_pairs={{0,4},{4,8},{8,12},{12,16},{16,20},{20,24},{24,28},{28,32},{32,36}... | collective-permute-start | bytes 1966088 | tf_op jit(solution)/shard_map/while/body/eval_jaxpr/ppermute | solution.py:19
  359.1 14.0 %collective-permute-start = (f32[20,128,64]{1,2,0:T(8,128)S(1)}, f32[20,128,64]{1,2,0:T(8,128)S(1)}, u32[]{:S(2)}, u32[]{:S(2)}) collective-permute-start(f32[20,128,64]{1,2,0:T(8,128)S(1)} %multiply_add_fusion.2), channel_id=1, source_target_pairs={{0,4},{4,8},{8,12},{12,16},{16,20},{20,24},{24,28},{28,32},{32,36}... | collective-permute-start | bytes 1966088 | tf_op jit(solution)/shard_map/while/body/eval_jaxpr/ppermute | solution.py:19
  373.2 14.0 %collective-permute-start = (f32[20,128,64]{1,2,0:T(8,128)S(1)}, f32[20,128,64]{1,2,0:T(8,128)S(1)}, u32[]{:S(2)}, u32[]{:S(2)}) collective-permute-start(f32[20,128,64]{1,2,0:T(8,128)S(1)} %multiply_add_fusion.2), channel_id=1, source_target_pairs={{0,4},{4,8},{8,12},{12,16},{16,20},{20,24},{24,28},{28,32},{32,36}... | collective-permute-start | bytes 1966088 | tf_op jit(solution)/shard_map/while/body/eval_jaxpr/ppermute | solution.py:19
  387.4 14.0 %collective-permute-start = (f32[20,128,64]{1,2,0:T(8,128)S(1)}, f32[20,128,64]{1,2,0:T(8,128)S(1)}, u32[]{:S(2)}, u32[]{:S(2)}) collective-permute-start(f32[20,128,64]{1,2,0:T(8,128)S(1)} %multiply_add_fusion.2), channel_id=1, source_target_pairs={{0,4},{4,8},{8,12},{12,16},{16,20},{20,24},{24,28},{28,32},{32,36}... | collective-permute-start | bytes 1966088 | tf_op jit(solution)/shard_map/while/body/eval_jaxpr/ppermute | solution.py:19
  401.5 14.0 %collective-permute-start = (f32[20,128,64]{1,2,0:T(8,128)S(1)}, f32[20,128,64]{1,2,0:T(8,128)S(1)}, u32[]{:S(2)}, u32[]{:S(2)}) collective-permute-start(f32[20,128,64]{1,2,0:T(8,128)S(1)} %multiply_add_fusion.2), channel_id=1, source_target_pairs={{0,4},{4,8},{8,12},{12,16},{16,20},{20,24},{24,28},{28,32},{32,36}... | collective-permute-start | bytes 1966088 | tf_op jit(solution)/shard_map/while/body/eval_jaxpr/ppermute | solution.py:19
  415.7 14.0 %collective-permute-start = (f32[20,128,64]{1,2,0:T(8,128)S(1)}, f32[20,128,64]{1,2,0:T(8,128)S(1)}, u32[]{:S(2)}, u32[]{:S(2)}) collective-permute-start(f32[20,128,64]{1,2,0:T(8,128)S(1)} %multiply_add_fusion.2), channel_id=1, source_target_pairs={{0,4},{4,8},{8,12},{12,16},{16,20},{20,24},{24,28},{28,32},{32,36}... | collective-permute-start | bytes 1966088 | tf_op jit(solution)/shard_map/while/body/eval_jaxpr/ppermute | solution.py:19
  429.8 14.0 %collective-permute-start = (f32[20,128,64]{1,2,0:T(8,128)S(1)}, f32[20,128,64]{1,2,0:T(8,128)S(1)}, u32[]{:S(2)}, u32[]{:S(2)}) collective-permute-start(f32[20,128,64]{1,2,0:T(8,128)S(1)} %multiply_add_fusion.2), channel_id=1, source_target_pairs={{0,4},{4,8},{8,12},{12,16},{16,20},{20,24},{24,28},{28,32},{32,36}... | collective-permute-start | bytes 1966088 | tf_op jit(solution)/shard_map/while/body/eval_jaxpr/ppermute | solution.py:19
  444.0 14.0 %collective-permute-start = (f32[20,128,64]{1,2,0:T(8,128)S(1)}, f32[20,128,64]{1,2,0:T(8,128)S(1)}, u32[]{:S(2)}, u32[]{:S(2)}) collective-permute-start(f32[20,128,64]{1,2,0:T(8,128)S(1)} %multiply_add_fusion.2), channel_id=1, source_target_pairs={{0,4},{4,8},{8,12},{12,16},{16,20},{20,24},{24,28},{28,32},{32,36}... | collective-permute-start | bytes 1966088 | tf_op jit(solution)/shard_map/while/body/eval_jaxpr/ppermute | solution.py:19
  (34 other events, 283.2 us)
Sparse Core Ops, SparseCore 0:
  9.9 27.1 all-gather.1
  486.5 76.1 reduce-scatter.1
where the time goes:
time: 573 us; the launch traced here: 571 us
  waiting for transfers between devices  330 us (58%)
  starting transfers between devices  165 us (29%)
  matrix products  28.8 us (5%)
  other arithmetic  15.4 us (3%)
  between operations  15.1 us (3%)
  local copies, waits for them, and re-layouts  8.96 us (2%)
  blocking collectives  7.39 us (1%)
    ppermute x33, waiting for transfers between devices, from_behind(): return lax.ppermute(block, axis, route)  233 us
    ppermute x33, starting transfers between devices, from_behind(): return lax.ppermute(block, axis, route)  165 us
    reduce_scatter x1, waiting for transfers between devices, on_device(): lax.psum_scatter(jnp.dot(normed_out, out_weight, preferred_element_type=j...  76.3 us
    all_gather x1, waiting for transfers between devices, on_device(): gathered = lax.all_gather(normed, 'head', axis=0, tiled=True)  21.3 us
  transfers between devices with their start and end apart: 35, of which 33 were waited for; matrix products, arithmetic and copies ran while one was open for 3% of the time, Pallas kernels for 0%

commit v1 on v0

v1 whole, which is shorter than its diff:
```python
import jax
import jax.numpy as jnp
from jax import lax
from jax.sharding import PartitionSpec as P

H = 80
P_SIZE = 64
N = 128
K = 4
RIM = 8
LANES = 128


def from_behind(block, axis, distance):
    devices = range(lax.axis_size(axis))
    route = [(i - distance, i) for i in devices if i - distance in devices]
    return lax.ppermute(block, axis, route)


def around(block, axis, distance):
    size = lax.axis_size(axis)
    return lax.ppermute(block, axis, [(i, (i + distance) % size) for i in range(size)])


def gather_tokens(tokens):
    size = lax.axis_size("head")
    here = lax.axis_index("head")
    rows = tokens.shape[0]
    whole = jnp.zeros((size * rows, tokens.shape[1]), tokens.dtype)
    whole = lax.dynamic_update_slice(whole, tokens, (here * rows, 0))
    for distance in range(1, size):
        piece = around(tokens, "head", distance)
        owner = (here - distance) % size
        whole = lax.dynamic_update_slice(whole, piece, (owner * rows, 0))
    return whole


def gather_rim(tokens):
    heads = lax.axis_size("head")
    blocks = lax.axis_size("seq")
    tail = tokens[tokens.shape[0] - RIM :]
    total = None
    for target in range(heads):
        route = [
            (s * heads + heads - 1, (s + 1) * heads + target) for s in range(blocks - 1)
        ]
        piece = lax.ppermute(tail, ("seq", "head"), route)
        total = piece if total is None else total + piece
    return total


def split3(x):
    first = x.astype(jnp.bfloat16)
    rest = x - first.astype(jnp.float32)
    second = rest.astype(jnp.bfloat16)
    third = (rest - second.astype(jnp.float32)).astype(jnp.bfloat16)
    return first, second, third


def passage_ids(lengths, positions):
    starts = jnp.cumsum(lengths) - lengths
    return jnp.sum((positions[:, None] >= starts[None, :]).astype(jnp.int32), axis=1) - 1


def causal_conv(padded, weights, ids, padded_ids):
    length = ids.shape[0]
    total = jnp.zeros((length, padded.shape[1]), jnp.float32)
    for offset in range(K):
        first = RIM - offset
        shifted = padded[first : first + length]
        agrees = (padded_ids[first : first + length] == ids).astype(jnp.float32)
        total = total + weights[offset][None, :] * shifted * agrees[:, None]
    return jax.nn.silu(total)


def spread(x):
    return jnp.repeat(x, P_SIZE, axis=1)


def carried_states(local, total_decay):
    blocks = lax.axis_size("seq")
    heads_here = total_decay.shape[0]
    parts = jnp.concatenate(split3(total_decay))
    parts = jnp.pad(parts, (0, LANES - parts.shape[0]))
    sent = jnp.concatenate(
        [local.astype(jnp.bfloat16), jnp.broadcast_to(parts[None], (N, LANES))], axis=1
    )
    got = lax.all_to_all(sent, "seq", 0, 0, tiled=True)
    width = local.shape[1]
    pieces = got[:, :width].astype(jnp.float32).reshape(blocks, N // blocks, width)
    decays = got[:, width:].astype(jnp.float32).reshape(blocks, N // blocks, LANES)[:, 0]
    decays = sum(decays[:, i * heads_here : (i + 1) * heads_here] for i in range(3))
    decays = spread(decays)
    state = jnp.zeros((N // blocks, width), jnp.float32)
    outs = []
    for b in range(blocks):
        outs.append(state)
        state = decays[b][None] * state + pieces[b]
    back = jnp.stack(outs).astype(jnp.bfloat16).reshape(N, width)
    return lax.all_to_all(back, "seq", 0, 0, tiled=True)


def on_device(
    tokens,
    input_gain,
    gate_weight,
    inner_weight,
    state_weight,
    step_weight,
    step_bias,
    decay_exponent,
    conv_inner,
    conv_state,
    skip_gain,
    norm_gain,
    out_weight,
    passage_lengths,
):
    rows = tokens.shape[0]
    whole = jnp.concatenate([gather_rim(tokens), gather_tokens(tokens)])
    length = whole.shape[0] - RIM
    tok_float = whole.astype(jnp.float32)
    normed = (
        tok_float
        * lax.rsqrt(jnp.mean(tok_float * tok_float, axis=-1, keepdims=True) + 1e-05)
        * input_gain
    ).astype(jnp.bfloat16)
    gate_vals = jnp.dot(normed[RIM:], gate_weight, preferred_element_type=jnp.float32).astype(
        jnp.bfloat16
    )
    inner_pad = jnp.dot(normed, inner_weight, preferred_element_type=jnp.float32).astype(
        jnp.bfloat16
    )
    state_pad = jnp.dot(normed, state_weight, preferred_element_type=jnp.float32).astype(
        jnp.bfloat16
    )
    step_raw = jnp.dot(normed[RIM:], step_weight, preferred_element_type=jnp.float32)
    heads_here = step_weight.shape[1]
    first_pos = lax.axis_index("seq") * length
    padded_pos = first_pos + jnp.arange(-RIM, length, dtype=jnp.int32)
    padded_ids = passage_ids(passage_lengths, padded_pos)
    ids = padded_ids[RIM:]
    prior_id = padded_ids[RIM - 1]
    inner_conv = causal_conv(
        inner_pad.astype(jnp.float32), conv_inner, ids, padded_ids
    ).astype(jnp.bfloat16)
    state_conv = causal_conv(
        state_pad.astype(jnp.float32), conv_state, ids, padded_ids
    ).astype(jnp.bfloat16)
    state_in = state_conv[:, :N]
    state_out = state_conv[:, N:]
    step_size = jax.nn.softplus(step_raw + step_bias)
    log_decay = -step_size * (decay_exponent.astype(jnp.float32) * 2.0 ** (-21))
    cum = jnp.cumsum(log_decay, axis=0)
    tail = jnp.exp(cum[-1][None] - cum) * (ids == ids[-1]).astype(jnp.float32)[:, None]
    head_decay = jnp.exp(cum) * (ids == prior_id).astype(jnp.float32)[:, None]
    conv_float = inner_conv.astype(jnp.float32)
    scaled_in = (conv_float * spread(step_size)).astype(jnp.bfloat16)
    tail_in = (spread(tail) * scaled_in.astype(jnp.float32)).astype(jnp.bfloat16)
    local = jnp.dot(state_in.T, tail_in, preferred_element_type=jnp.float32)
    incoming = carried_states(local, head_decay[-1])

    order = jnp.arange(length)
    mask = (ids[:, None] == ids[None, :]) & (order[:, None] >= order[None, :])
    scores = jnp.dot(state_out, state_in.T, preferred_element_type=jnp.float32)
    cum_heads = cum.T
    gaps = cum_heads[:, :, None] - cum_heads[:, None, :]
    decay_mat = jnp.exp(jnp.where(mask[None], gaps, -1e30))
    weighted = (decay_mat * scores[None]).astype(jnp.bfloat16)
    intra = jnp.einsum(
        "hts,shp->thp",
        weighted,
        scaled_in.reshape(length, heads_here, P_SIZE),
        preferred_element_type=jnp.float32,
    ).reshape(length, heads_here * P_SIZE)
    inter = jnp.dot(state_out, incoming, preferred_element_type=jnp.float32) * spread(head_decay)
    ssd_out = intra + inter + spread(skip_gain[None]) * conv_float
    gated = ssd_out * jax.nn.silu(gate_vals.astype(jnp.float32))
    squares = jnp.sum(gated * gated, axis=1, keepdims=True)
    partial = jnp.dot(
        (gated * norm_gain).astype(jnp.bfloat16), out_weight, preferred_element_type=jnp.float32
    )
    sent = jnp.concatenate(
        [partial.astype(jnp.bfloat16), jnp.pad(jnp.concatenate(split3(squares), 1), ((0, 0), (0, LANES - 3)))],
        axis=1,
    )
    here = lax.axis_index("head")
    size = lax.axis_size("head")
    pieces = [lax.dynamic_slice_in_dim(sent, here * rows, rows)]
    for distance in range(1, size):
        target = (here + distance) % size
        pieces.append(
            around(lax.dynamic_slice_in_dim(sent, target * rows, rows), "head", distance)
        )
    total = sum(p.astype(jnp.float32) for p in pieces)
    width = partial.shape[1]
    mean = jnp.sum(total[:, width : width + 3], axis=1, keepdims=True) / (H * P_SIZE)
    return (total[:, :width] * lax.rsqrt(mean + 1e-05)).astype(jnp.bfloat16)


def solution(mesh):
    in_specs = (
        P(("seq", "head"), None),
        P(),
        P(None, "head"),
        P(None, "head"),
        P(),
        P(None, "head"),
        P("head"),
        P("head"),
        P(None, "head"),
        P(),
        P("head"),
        P("head"),
        P("head", None),
        P(),
    )
    out_specs = P(("seq", "head"), None)
    return jax.shard_map(
        on_device, mesh=mesh, in_specs=in_specs, out_specs=out_specs, check_vma=False
    )
```

time: 573 us -> 156 us (0.27)
  waiting for transfers between devices: 330 us -> 35.6 us
  starting transfers between devices: 165 us -> 31.1 us
  local copies, waits for them, and re-layouts: 8.96 us -> 32.6 us
  other arithmetic: 15.4 us -> 32 us
  between operations: 15.1 us -> 0.68 us
  blocking collectives: 7.39 us -> 0 us
    ppermute x33 -> x10, waiting for transfers between devices: 233 us -> 29 us  [the longest x6 29 us: around(): lax.ppermute(block, axis, [(i, (i + distance) % size) for i in range(size)])]
    ppermute x33 -> x10, starting transfers between devices: 165 us -> 17.7 us  [the longest x6 13.8 us: around(): lax.ppermute(block, axis, [(i, (i + distance) % size) for i in range(size)])]
    reduce_scatter x1 -> x0, waiting for transfers between devices: 76.3 us -> none  [on_device(): lax.psum_scatter(jnp.dot(normed_out, out_weight, preferred_element_type=j...]
    all_gather x1 -> x0, waiting for transfers between devices: 21.3 us -> none  [on_device(): gathered = lax.all_gather(normed, 'head', axis=0, tiled=True)]
    unnamed x0 -> x30, other arithmetic: none -> 21.2 us
    broadcast_in_dim x0 -> x67, local copies, waits for them, and re-layouts: none -> 14.3 us  [the longest x66 14.2 us: spread(): return jnp.repeat(x, P_SIZE, axis=1)]
    all_to_all x0 -> x2, starting transfers between devices: none -> 13.5 us  [the longest x1 8.82 us: carried_states(): got = lax.all_to_all(sent, 'seq', 0, 0, tiled=True)]
    psum x1 -> x0, blocking collectives: 7.39 us -> none  [on_device(): squares = lax.psum(jnp.sum(gated * gated, axis=1), 'head')]
  transfers between devices with their start and end apart: 35 -> 12, of which waited for: 33 -> 6; matrix products, arithmetic and copies ran while one was open for 3% -> 16% of each run, Pallas kernels for 0% -> 0%
where the time goes in v1:
time: 156 us; the launch traced here: 155 us
  waiting for transfers between devices  35.6 us (23%)
  local copies, waits for them, and re-layouts  32.6 us (21%)
  other arithmetic  32 us (21%)
  starting transfers between devices  31.1 us (20%)
  matrix products  23.3 us (15%)
    ppermute x6, waiting for transfers between devices, around(): lax.ppermute(block, axis, [(i, (i + distance) % size) for i in range(size)])  29 us
    unnamed x30, other arithmetic  21.2 us
    broadcast_in_dim x66, local copies, waits for them, and re-layouts, spread(): return jnp.repeat(x, P_SIZE, axis=1)  14.2 us
    ppermute x6, starting transfers between devices, around(): lax.ppermute(block, axis, [(i, (i + distance) % size) for i in range(size)])  13.8 us
    all_to_all x1, starting transfers between devices, carried_states(): got = lax.all_to_all(sent, 'seq', 0, 0, tiled=True)  8.82 us
    reshape x3, local copies, waits for them, and re-layouts, spread(): return jnp.repeat(x, P_SIZE, axis=1)  5.96 us
    dot_general x1, matrix products, on_device(): jnp.dot(normed[RIM:], gate_weight, preferred_element_type=jnp.float32)  5.8 us
    dot_general x1, matrix products, on_device(): jnp.dot(normed, inner_weight, preferred_element_type=jnp.float32)  5.28 us
  transfers between devices with their start and end apart: 12, of which 6 were waited for; matrix products, arithmetic and copies ran while one was open for 16% of the time, Pallas kernels for 0%

profile of v1, /device:TPU:1, one launch (start us, length us, event | category | flops | bytes accessed | tf_op | source)
XLA Modules:
  0.0 155.3 jit_solution(9122758522462059749)
XLA Ops:
  0.0 2.5 %collective-permute-start.4 = (bf16[64,2560]{1,0:T(8,128)(2,1)}, bf16[64,2560]{1,0:T(8,128)(2,1)S(1)}, u32[]{:S(2)}, u32[]{:S(2)}) collective-permute-start(bf16[64,2560]{1,0:T(8,128)(2,1)} %param.14), channel_id=1, source_target_pairs={{0,1},{1,2},{2,3},{3,0},{4,5},{5,6},{6,7},{7,4},{8,9},{9,10},{10,1... | collective-permute-start | bytes 983048 | tf_op jit(solution)/shard_map/ppermute | solution.py:22
  11.6 1.4 fusion.58
  13.2 1.9 %compare_convert_fusion.1 = (f32[256]{0:T(256)}, f32[256]{0:T(256)}, f32[256]{0:T(256)}, f32[256]{0:T(256)}, f32[256]{0:T(256)}) fusion(s32[]{:T(128)} %bitcast.11, s32[264]{0:T(512)S(1)} %broadcast_add_fusion.1, s32[]{:T(128)} %bitcast.13), kind=kLoop, calls=%fused_computation.177 | loop fusion | flops 2560 | bytes 9224 | tf_op jit(solution)/shard_map/convert_element_type | solution.py:155
  17.2 3.3 %collective-permute-start.5 = (bf16[64,2560]{1,0:T(8,128)(2,1)S(1)}, bf16[64,2560]{1,0:T(8,128)(2,1)S(1)}, u32[]{:S(2)}, u32[]{:S(2)}) collective-permute-start(bf16[64,2560]{1,0:T(8,128)(2,1)S(1)} %copy-done.6), channel_id=1, source_target_pairs={{0,2},{1,3},{2,0},{3,1},{4,6},{5,7},{6,4},{7,5},{8,10},{9,11},{10,... | collective-permute-start | bytes 983048 | tf_op jit(solution)/shard_map/ppermute | solution.py:22
  20.5 4.6 %collective-permute-start.6 = (bf16[64,2560]{1,0:T(8,128)(2,1)S(1)}, bf16[64,2560]{1,0:T(8,128)(2,1)S(1)}, u32[]{:S(2)}, u32[]{:S(2)}) collective-permute-start(bf16[64,2560]{1,0:T(8,128)(2,1)S(1)} %copy-done.6), channel_id=1, source_target_pairs={{0,3},{1,0},{2,1},{3,2},{4,7},{5,4},{6,5},{7,6},{8,11},{9,8},{10,9... | collective-permute-start | bytes 983048 | tf_op jit(solution)/shard_map/ppermute | solution.py:22
  25.9 2.4 %collective-permute-done.5 = bf16[64,2560]{1,0:T(8,128)(2,1)S(1)} collective-permute-done((bf16[64,2560]{1,0:T(8,128)(2,1)S(1)}, bf16[64,2560]{1,0:T(8,128)(2,1)S(1)}, u32[]{:S(2)}, u32[]{:S(2)}) %collective-permute-start.5) | collective-permute-done | bytes 327712 | tf_op jit(solution)/shard_map/ppermute | solution.py:22
  28.4 11.0 %collective-permute-done.6 = bf16[64,2560]{1,0:T(8,128)(2,1)S(1)} collective-permute-done((bf16[64,2560]{1,0:T(8,128)(2,1)S(1)}, bf16[64,2560]{1,0:T(8,128)(2,1)S(1)}, u32[]{:S(2)}, u32[]{:S(2)}) %collective-permute-start.6) | collective-permute-done | bytes 327712 | tf_op jit(solution)/shard_map/ppermute | solution.py:22
  44.6 1.7 %copy.56 = f32[256,1280]{1,0:T(8,128)S(1)} copy(f32[256,1280]{0,1:T(8,128)} %bitcast.177) | data formatting | bytes 2621440 | tf_op jit(solution)/shard_map/reshape | solution.py:77
  47.5 2.8 %copy.52 = f32[256,1280]{1,0:T(8,128)} copy(f32[256,1280]{0,1:T(8,128)} %bitcast.178) | data formatting | bytes 2621440 | tf_op jit(solution)/shard_map/reshape | solution.py:77
  50.3 5.3 %fusion.13 = f32[264,1280]{1,0:T(8,128)S(1)} fusion(bf16[264,2560]{1,0:T(8,128)(2,1)} %copy-done.2, bf16[2560,1280]{1,0:T(8,128)(2,1)} %param.17), kind=kOutput, calls=%fused_computation.20 | convolution fusion | flops 1730826240 | bytes 9256960 | tf_op jit(solution)/shard_map/dot_general | solution.py:131
  57.0 1.9 %fusion.16 = (bf16[256,1280]{1,0:T(8,128)(2,1)S(1)}, bf16[256,1280]{1,0:T(8,128)(2,1)}) fusion(f32[256,1280]{1,0:T(8,128)S(1)} %copy-done.1, f32[256]{0:T(256)S(1)} %copy-done.17, f32[264,1280]{1,0:T(8,128)S(1)} %fusion.13, f32[1280]{0:T(1024)S(1)} %copy-done.7, f32[256]{0:T(256)S(1)} %copy-done.18, f32[1280]{0:T(1024)S(1)} %copy-done.8, ...), kind=kLoop, calls=%fused_computation.28 | loop fusion | flops 5898240 | bytes 7887872 | tf_op jit(solution)/shard_map/convert_element_type | solution.py:158
  60.1 8.8 %all-to-all-start = ((bf16[32,4,1408]{2,1,0:T(4,128)(2,1)}), bf16[32,4,1408]{2,1,0:T(4,128)(2,1)}, u32[]{:S(2)}, u32[]{:S(2)}) async-start(bf16[32,4,1408]{2,1,0:T(4,128)(2,1)} %all_to_all.14), calls=%async_computation | async-start | bytes 720896 | tf_op jit(solution)/shard_map/all_to_all | solution.py:88
  71.0 1.5 copy.57
  72.5 2.2 %fusion.7 = f32[20,64,256]{2,1,0:T(8,128)S(1)} fusion(bf16[256,20,64]{0,2,1:T(8,128)(2,1)S(1)} %bitcast.181, f32[256,256]{1,0:T(8,128)} %fusion.40, f32[20,256]{1,0:T(8,128)S(1)} %bitcast.185, pred[256,256]{1,0:T(8,128)(4,1)S(1)} %fusion.38), kind=kOutput, calls=%fused_computation.13 | convolution fusion | flops 173015040 | bytes 2314240 | tf_op jit(solution)/shard_map/hts,shp->thp/dot_general | solution.py:170
  74.7 1.5 copy.58
  76.2 2.8 %all-to-all-done = bf16[32,4,1408]{2,1,0:T(4,128)(2,1)} async-done(((bf16[32,4,1408]{2,1,0:T(4,128)(2,1)}), bf16[32,4,1408]{2,1,0:T(4,128)(2,1)}, u32[]{:S(2)}, u32[]{:S(2)}) %all-to-all-start) | async-done | bytes 360480 | tf_op jit(solution)/shard_map/all_to_all | solution.py:88
  112.5 4.6 %all-to-all-start.1 = ((bf16[32,4,1280]{2,1,0:T(4,128)(2,1)}), bf16[32,4,1280]{2,1,0:T(4,128)(2,1)S(1)}, u32[]{:S(2)}, u32[]{:S(2)}) async-start(bf16[32,4,1280]{2,1,0:T(4,128)(2,1)} %constant_dynamic-update-slice_fusion), calls=%async_computation.1 | async-start | bytes 655360 | tf_op jit(solution)/shard_map/all_to_all | solution.py:100
  117.2 5.8 %fusion.14 = f32[256,1280]{1,0:T(8,128)} fusion(bf16[2560,1280]{1,0:T(8,128)(2,1)} %param.16, bf16[264,2560]{1,0:T(8,128)(2,1)S(1)} %copy-done.4), kind=kOutput, calls=%fused_computation.22 | convolution fusion | flops 1678376960 | bytes 9175040 | tf_op jit(solution)/shard_map/dot_general | solution.py:128
  123.0 3.8 %all-to-all-done.1 = bf16[32,4,1280]{2,1,0:T(4,128)(2,1)S(1)} async-done(((bf16[32,4,1280]{2,1,0:T(4,128)(2,1)}), bf16[32,4,1280]{2,1,0:T(4,128)(2,1)S(1)}, u32[]{:S(2)}, u32[]{:S(2)}) %all-to-all-start.1) | async-done | bytes 327712 | tf_op jit(solution)/shard_map/all_to_all | solution.py:100
  126.9 3.1 %multiply_reduce_fusion = (f32[256]{0:T(256)S(1)}, f32[256,1280]{1,0:T(8,128)S(1)}) fusion(f32[256,1280]{1,0:T(8,128)} %fusion.14, bf16[256,1280]{1,0:T(8,128)(2,1)} %get-tuple-element.40, f32[1280]{0:T(1024)S(1)} %copy-done.20, f32[256,1280]{1,0:T(8,128)} %copy.58, f32[256,1280]{1,0:T(8,128)} %copy.57, bf16[128,1280]{1,0:T(8,128)(2,1)S(1)} %all_to_all.18, ...), kind=kOutput, calls=%fused_computation.39 | convolution fusion | flops 87817984 | bytes 6300672 | tf_op jit(solution)/shard_map/dot_general | solution.py:176
  130.2 4.7 %convolution_convert_fusion = bf16[256,2560]{1,0:T(8,128)(2,1)S(1)} fusion(bf16[1280,2560]{1,0:T(8,128)(2,1)} %param.26, f32[256,1280]{1,0:T(8,128)S(1)} %get-tuple-element.96, f32[1280]{0:T(1024)S(1)} %copy-done.29), kind=kOutput, calls=%fused_computation.1 | convolution fusion | flops 1679032320 | bytes 9180160 | tf_op jit(solution)/shard_map/dot_general | solution.py:180
  135.2 3.3 %collective-permute-start.8 = (bf16[64,2688]{1,0:T(8,128)(2,1)S(1)}, bf16[64,2688]{1,0:T(8,128)(2,1)S(1)}, u32[]{:S(2)}, u32[]{:S(2)}) collective-permute-start(bf16[64,2688]{1,0:T(8,128)(2,1)S(1)} %get-tuple-element.43), channel_id=1, source_target_pairs={{0,2},{1,3},{2,0},{3,1},{4,6},{5,7},{6,4},{7,5},{8,10},{9,11},{10,... | collective-permute-start | bytes 1032200 | tf_op jit(solution)/shard_map/ppermute | solution.py:22
  138.5 7.6 %collective-permute-done.7 = bf16[64,2688]{1,0:T(8,128)(2,1)S(1)} collective-permute-done((bf16[64,2688]{1,0:T(8,128)(2,1)S(1)}, bf16[64,2688]{1,0:T(8,128)(2,1)S(1)}, u32[]{:S(2)}, u32[]{:S(2)}) %collective-permute-start.7) | collective-permute-done | bytes 344096 | tf_op jit(solution)/shard_map/ppermute | solution.py:22
  146.1 8.0 %collective-permute-done.8 = bf16[64,2688]{1,0:T(8,128)(2,1)S(1)} collective-permute-done((bf16[64,2688]{1,0:T(8,128)(2,1)S(1)}, bf16[64,2688]{1,0:T(8,128)(2,1)S(1)}, u32[]{:S(2)}, u32[]{:S(2)}) %collective-permute-start.8) | collective-permute-done | bytes 344096 | tf_op jit(solution)/shard_map/ppermute | solution.py:22
  (238 shorter events, 58.0 us)
Async XLA Ops:
  0.0 55.6 %copy-start = (bf16[2560,256]{1,0:T(8,128)(2,1)S(1)}, bf16[2560,256]{1,0:T(8,128)(2,1)}, u32[]{:S(2)}) copy-start(bf16[2560,256]{1,0:T(8,128)(2,1)} %param.18) | copy-start | bytes 3932164
  0.0 13.2 %copy-start.6 = (bf16[64,2560]{1,0:T(8,128)(2,1)S(1)}, bf16[64,2560]{1,0:T(8,128)(2,1)}, u32[]{:S(2)}) copy-start(bf16[64,2560]{1,0:T(8,128)(2,1)} %param.14) | copy-start | bytes 983044
  0.0 15.2 %copy-start.15 = (f32[4,1280]{1,0:T(4,128)S(1)}, f32[4,1280]{1,0:T(4,128)}, u32[]{:S(2)}) copy-start(f32[4,1280]{1,0:T(4,128)} %param.22) | copy-start | bytes 61444
  0.0 25.9 %collective-permute-start.4 = (bf16[64,2560]{1,0:T(8,128)(2,1)}, bf16[64,2560]{1,0:T(8,128)(2,1)S(1)}, u32[]{:S(2)}, u32[]{:S(2)}) collective-permute-start(bf16[64,2560]{1,0:T(8,128)(2,1)} %param.14), channel_id=1, source_target_pairs={{0,1},{1,2},{2,3},{3,0},{4,5},{5,6},{6,7},{7,4},{8,9},{9,10},{10,1... | collective-permute-start | bytes 983048 | tf_op jit(solution)/shard_map/ppermute | solution.py:22
  3.4 13.9 %collective-permute-start = (bf16[8,2560]{1,0:T(8,128)(2,1)S(1)}, bf16[8,2560]{1,0:T(8,128)(2,1)S(1)}, u32[]{:S(2)}, u32[]{:S(2)}) collective-permute-start(bf16[8,2560]{1,0:T(8,128)(2,1)S(1)} %slice.462), channel_id=1, source_target_pairs={{3,4},{7,8},{11,12},{15,16},{19,20},{23,24},{27,28},{31,32},{35,36... | collective-permute-start | bytes 122888 | tf_op jit(solution)/shard_map/ppermute | solution.py:47
  4.6 15.9 %collective-permute-start.1 = (bf16[8,2560]{1,0:T(8,128)(2,1)S(1)}, bf16[8,2560]{1,0:T(8,128)(2,1)S(1)}, u32[]{:S(2)}, u32[]{:S(2)}) collective-permute-start(bf16[8,2560]{1,0:T(8,128)(2,1)S(1)} %slice.462), channel_id=1, source_target_pairs={{3,5},{7,9},{11,13},{15,17},{19,21},{23,25},{27,29},{31,33},{35,37... | collective-permute-start | bytes 122888 | tf_op jit(solution)/shard_map/ppermute | solution.py:47
  5.3 19.8 %collective-permute-start.2 = (bf16[8,2560]{1,0:T(8,128)(2,1)S(1)}, bf16[8,2560]{1,0:T(8,128)(2,1)S(1)}, u32[]{:S(2)}, u32[]{:S(2)}) collective-permute-start(bf16[8,2560]{1,0:T(8,128)(2,1)S(1)} %slice.462), channel_id=1, source_target_pairs={{3,6},{7,10},{11,14},{15,18},{19,22},{23,26},{27,30},{31,34},{35,3... | collective-permute-start | bytes 122888 | tf_op jit(solution)/shard_map/ppermute | solution.py:47
  6.0 19.1 %collective-permute-start.3 = (bf16[8,2560]{1,0:T(8,128)(2,1)S(1)}, bf16[8,2560]{1,0:T(8,128)(2,1)}, u32[]{:S(2)}, u32[]{:S(2)}) collective-permute-start(bf16[8,2560]{1,0:T(8,128)(2,1)S(1)} %slice.462), channel_id=1, source_target_pairs={{3,7},{7,11},{11,15},{15,19},{19,23},{23,27},{27,31},{31,35},{35,3... | collective-permute-start | bytes 122888 | tf_op jit(solution)/shard_map/ppermute | solution.py:47
  17.2 11.1 %collective-permute-start.5 = (bf16[64,2560]{1,0:T(8,128)(2,1)S(1)}, bf16[64,2560]{1,0:T(8,128)(2,1)S(1)}, u32[]{:S(2)}, u32[]{:S(2)}) collective-permute-start(bf16[64,2560]{1,0:T(8,128)(2,1)S(1)} %copy-done.6), channel_id=1, source_target_pairs={{0,2},{1,3},{2,0},{3,1},{4,6},{5,7},{6,4},{7,5},{8,10},{9,11},{10,... | collective-permute-start | bytes 983048 | tf_op jit(solution)/shard_map/ppermute | solution.py:22
  20.5 18.8 %collective-permute-start.6 = (bf16[64,2560]{1,0:T(8,128)(2,1)S(1)}, bf16[64,2560]{1,0:T(8,128)(2,1)S(1)}, u32[]{:S(2)}, u32[]{:S(2)}) collective-permute-start(bf16[64,2560]{1,0:T(8,128)(2,1)S(1)} %copy-done.6), channel_id=1, source_target_pairs={{0,3},{1,0},{2,1},{3,2},{4,7},{5,4},{6,5},{7,6},{8,11},{9,8},{10,9... | collective-permute-start | bytes 983048 | tf_op jit(solution)/shard_map/ppermute | solution.py:22
  25.9 13.8 %copy-start.16 = (f32[2560]{0:T(1024)S(1)}, f32[2560]{0:T(1024)}, u32[]{:S(2)}) copy-start(f32[2560]{0:T(1024)} %param.15) | copy-start | bytes 30724
  60.1 18.9 %all-to-all-start = ((bf16[32,4,1408]{2,1,0:T(4,128)(2,1)}), bf16[32,4,1408]{2,1,0:T(4,128)(2,1)}, u32[]{:S(2)}, u32[]{:S(2)}) async-start(bf16[32,4,1408]{2,1,0:T(4,128)(2,1)} %all_to_all.14), calls=%async_computation | async-start | bytes 720896 | tf_op jit(solution)/shard_map/all_to_all | solution.py:88
  90.7 13.2 %copy-start.14 = (f32[1280]{0:T(1024)S(1)}, f32[1280]{0:T(1024)}, u32[]{:S(2)}) copy-start(f32[1280]{0:T(1024)} %broadcast_in_dim.230) | copy-start | bytes 15364
  90.7 14.5 %copy-start.13 = (f32[1280]{0:T(1024)S(1)}, f32[1280]{0:T(1024)}, u32[]{:S(2)}) copy-start(f32[1280]{0:T(1024)} %broadcast_in_dim.234) | copy-start | bytes 15364
  90.7 15.7 %copy-start.12 = (f32[1280]{0:T(1024)S(1)}, f32[1280]{0:T(1024)}, u32[]{:S(2)}) copy-start(f32[1280]{0:T(1024)} %broadcast_in_dim.238) | copy-start | bytes 15364
  90.7 16.9 %copy-start.11 = (f32[1280]{0:T(1024)S(1)}, f32[1280]{0:T(1024)}, u32[]{:S(2)}) copy-start(f32[1280]{0:T(1024)} %broadcast_in_dim.242) | copy-start | bytes 15364
  90.7 18.1 %copy-start.10 = (f32[1280]{0:T(1024)S(1)}, f32[1280]{0:T(1024)}, u32[]{:S(2)}) copy-start(f32[1280]{0:T(1024)} %broadcast_in_dim.246) | copy-start | bytes 15364
  90.7 19.4 %copy-start.9 = (f32[1280]{0:T(1024)S(1)}, f32[1280]{0:T(1024)}, u32[]{:S(2)}) copy-start(f32[1280]{0:T(1024)} %broadcast_in_dim.250) | copy-start | bytes 15364
  95.7 21.5 %copy-start.4 = (bf16[264,2560]{1,0:T(8,128)(2,1)S(1)}, bf16[264,2560]{1,0:T(8,128)(2,1)}, u32[]{:S(2)}) copy-start(bf16[264,2560]{1,0:T(8,128)(2,1)} %copy-done.2) | copy-start | bytes 4055044
  112.5 14.3 %all-to-all-start.1 = ((bf16[32,4,1280]{2,1,0:T(4,128)(2,1)}), bf16[32,4,1280]{2,1,0:T(4,128)(2,1)S(1)}, u32[]{:S(2)}, u32[]{:S(2)}) async-start(bf16[32,4,1280]{2,1,0:T(4,128)(2,1)} %constant_dynamic-update-slice_fusion), calls=%async_computation.1 | async-start | bytes 655360 | tf_op jit(solution)/shard_map/all_to_all | solution.py:100
  117.2 9.7 %copy-start.20 = (f32[1280]{0:T(1024)S(1)}, f32[1280]{0:T(1024)}, u32[]{:S(2)}) copy-start(f32[1280]{0:T(1024)} %broadcast_in_dim.259) | copy-start | bytes 15364
  135.1 11.0 %collective-permute-start.7 = (bf16[64,2688]{1,0:T(8,128)(2,1)S(1)}, bf16[64,2688]{1,0:T(8,128)(2,1)S(1)}, u32[]{:S(2)}, u32[]{:S(2)}) collective-permute-start(bf16[64,2688]{1,0:T(8,128)(2,1)S(1)} %get-tuple-element.41), channel_id=1, source_target_pairs={{0,1},{1,2},{2,3},{3,0},{4,5},{5,6},{6,7},{7,4},{8,9},{9,10},{10,1... | collective-permute-start | bytes 1032200 | tf_op jit(solution)/shard_map/ppermute | solution.py:22
  135.2 18.9 %collective-permute-start.8 = (bf16[64,2688]{1,0:T(8,128)(2,1)S(1)}, bf16[64,2688]{1,0:T(8,128)(2,1)S(1)}, u32[]{:S(2)}, u32[]{:S(2)}) collective-permute-start(bf16[64,2688]{1,0:T(8,128)(2,1)S(1)} %get-tuple-element.43), channel_id=1, source_target_pairs={{0,2},{1,3},{2,0},{3,1},{4,6},{5,7},{6,4},{7,5},{8,10},{9,11},{10,... | collective-permute-start | bytes 1032200 | tf_op jit(solution)/shard_map/ppermute | solution.py:22
  138.5 15.6 %collective-permute-start.9 = (bf16[64,2688]{1,0:T(8,128)(2,1)S(1)}, bf16[64,2688]{1,0:T(8,128)(2,1)S(1)}, u32[]{:S(2)}, u32[]{:S(2)}) collective-permute-start(bf16[64,2688]{1,0:T(8,128)(2,1)S(1)} %get-tuple-element.42), channel_id=1, source_target_pairs={{0,3},{1,0},{2,1},{3,2},{4,7},{5,4},{6,5},{7,6},{8,11},{9,8},{10,9... | collective-permute-start | bytes 1032200 | tf_op jit(solution)/shard_map/ppermute | solution.py:22
  (19 other events, 27.6 us)

commit v2 on v1

v2 whole, which is shorter than its diff:
```python
import jax
import jax.numpy as jnp
from jax import lax
from jax.experimental import pallas as pl
from jax.experimental.pallas import tpu as pltpu
from jax.sharding import PartitionSpec as P

H = 80
P_SIZE = 64
N = 128
K = 4
RIM = 16
LANES = 128
CHUNK = 256
WIDE = 512
VMEM_LIMIT = 40 << 20
F32 = jnp.float32
BF16 = jnp.bfloat16


def around(block, axis, distance):
    size = lax.axis_size(axis)
    return lax.ppermute(block, axis, [(i, (i + distance) % size) for i in range(size)])


def gather_tokens(tokens):
    heads = lax.axis_size("head")
    blocks = lax.axis_size("seq")
    half = tokens.shape[0] // 2
    tail = tokens[tokens.shape[0] - RIM :]
    below = around(tokens, "head", 1)
    above = around(tokens, "head", heads - 1)
    rim = None
    for target in range(0, heads, 2):
        route = [
            (s * heads + heads - 1, (s + 1) * heads + target) for s in range(blocks - 1)
        ]
        piece = lax.ppermute(tail, ("seq", "head"), route)
        rim = piece if rim is None else rim + piece
    top = around(jnp.concatenate([below[:half], rim]), "head", 1)
    bottom = around(above[half:], "head", heads - 1)
    return below, above, top, bottom, rim


def split3(x):
    first = x.astype(BF16).astype(F32)
    rest = x - first
    second = rest.astype(BF16).astype(F32)
    return first, second, rest - second


def by_lane(x, count):
    lane = lax.broadcasted_iota(jnp.int32, x.shape, 1)
    first, second, third = split3(x)
    picked = jnp.where(lane < count, first, jnp.where(lane < 2 * count, second, third))
    return jnp.where(lane < 3 * count, picked, 0.0).astype(BF16)


def head_slot(shape, count):
    slot = lax.broadcasted_iota(jnp.int32, shape, 0)
    live = slot < 3 * count
    slot = slot - jnp.where(slot >= 2 * count, 2 * count, jnp.where(slot >= count, count, 0))
    return jnp.where(live, slot, -1)


def spread_matrix(first_head, width, count):
    shape = (LANES, width)
    head = first_head + lax.broadcasted_iota(jnp.int32, shape, 1) // P_SIZE
    return jnp.where(head_slot(shape, count) == head, 1.0, 0.0).astype(BF16)


def dot(a, b):
    return jnp.dot(a, b, preferred_element_type=F32)


def block_kernel(
    place,
    lens_row,
    lens_col,
    own,
    below,
    above,
    top,
    bottom,
    rim,
    gain,
    state_w,
    step_w,
    step_bias,
    rate,
    taps_state,
    inner_w,
    taps_inner,
    normed_out,
    sent,
    conv_out,
    scaled_out,
    cum_out,
    cum_rows,
    scores_out,
    maps_out,
    head_decay_out,
    normed,
    agree,
    step3,
    tail3,
    maps_in_t,
    local,
    total3,
    *,
    heads_here,
):
    j = pl.program_id(0)
    rows = own.shape[0]
    length = normed.shape[0] - RIM

    def conv(raw, taps):
        acc = taps[0:1, :] * raw[RIM:]
        for lag in range(1, K):
            moved = pltpu.roll(raw, lag, 0)[RIM:]
            same = agree[lag - 1]
            same = jnp.concatenate([same] * (raw.shape[1] // LANES), axis=1)
            acc = acc + taps[lag : lag + 1, :] * moved * same
        return (acc * jax.nn.sigmoid(acc)).astype(BF16)

    @pl.when(j == 0)
    def _():
        here = place[0]
        first = place[1]

        def norm(x):
            x = x.astype(F32)
            mean = jnp.mean(x * x, axis=-1, keepdims=True)
            return (x * lax.rsqrt(mean + 1e-05) * gain[...]).astype(BF16)

        def put(owner, offset, x):
            start = pl.multiple_of(RIM + owner * rows + offset, RIM)
            normed[pl.ds(start, x.shape[0]), :] = norm(x)

        half = rows // 2
        put(here, 0, own[...])
        put((here + 3) % 4, 0, below[...])
        put((here + 1) % 4, 0, above[...])
        far = (here + 2) % 4
        put(far, 0, top[0:half, :])
        put(far, half, bottom[...])
        rim_tokens = (rim[...].astype(F32) + top[half:, :].astype(F32)).astype(BF16)
        normed[0:RIM, :] = norm(rim_tokens)
        normed_out[...] = normed[RIM:, :]

        passages = lens_row.shape[1]
        up = lax.broadcasted_iota(jnp.int32, (passages, passages), 0)
        across = lax.broadcasted_iota(jnp.int32, (passages, passages), 1)
        starts_row = jnp.sum(
            jnp.where(up < across, lens_col[...].astype(F32), 0.0), axis=0, keepdims=True
        )
        starts_col = jnp.sum(
            jnp.where(across < up, lens_row[...].astype(F32), 0.0), axis=1, keepdims=True
        )
        base = first.astype(F32)
        pos = lax.broadcasted_iota(jnp.int32, (length + RIM, passages), 0).astype(F32)
        ids_pad = jnp.sum(
            jnp.where(pos + (base - RIM) >= starts_row, 1.0, 0.0), axis=1, keepdims=True
        )
        pos = lax.broadcasted_iota(jnp.int32, (passages, length), 1).astype(F32)
        ids_row = jnp.sum(jnp.where(pos + base >= starts_col, 1.0, 0.0), axis=0, keepdims=True)
        ids_wide = jnp.broadcast_to(ids_pad, (length + RIM, LANES))
        ids = ids_wide[RIM:]
        for lag in range(1, K):
            agree[lag - 1] = jnp.where(pltpu.roll(ids_wide, lag, 0)[RIM:] == ids, 1.0, 0.0)

        raw = dot(normed[...], state_w[...]).astype(BF16).astype(F32)
        maps = conv(raw, taps_state)
        maps_in = maps[:, :N]
        maps_out[...] = maps[:, N:]
        maps_in_t[...] = maps_in.astype(F32).T.astype(BF16)
        t = lax.broadcasted_iota(jnp.int32, (length, length), 0)
        s = lax.broadcasted_iota(jnp.int32, (length, length), 1)
        ids_two = jnp.concatenate([ids] * (length // LANES), axis=1)
        mask = (ids_two == ids_row) & (t >= s)
        scores_out[...] = jnp.where(mask, dot(maps[:, N:], maps_in_t[...]), 0.0)

        x = dot(normed[RIM:, :], step_w[...]) + step_bias[...]
        step = jnp.maximum(x, 0.0) + jnp.log1p(jnp.exp(-jnp.abs(x)))
        log_decay = -step * rate[...]
        ones = jnp.where(t >= s, 1.0, 0.0).astype(BF16)
        cum = sum(dot(ones, part.astype(BF16)) for part in split3(log_decay))
        last = cum[length - 1 :, :]
        ids_last = ids[length - 1 :, :]
        prior = ids_wide[RIM - 1 : RIM, :]
        step3[...] = by_lane(step, heads_here)
        tail = jnp.exp(jnp.minimum(last - cum, 0.0)) * jnp.where(ids == ids_last, 1.0, 0.0)
        tail3[...] = by_lane(tail, heads_here)
        keep = jnp.exp(cum) * jnp.where(ids == prior, 1.0, 0.0)
        head_decay_out[...] = by_lane(keep, heads_here)
        total3[...] = by_lane(keep, heads_here)[length - RIM :].astype(F32)
        cum_out[...] = by_lane(cum, heads_here)
        cum_rows[...] = cum.T

    raw = dot(normed[...], inner_w[...]).astype(BF16).astype(F32)
    mixed = conv(raw, taps_inner)
    conv_out[...] = mixed
    spread = spread_matrix(j * (CHUNK // P_SIZE), CHUNK, heads_here)
    scaled = (mixed.astype(F32) * dot(step3[...], spread)).astype(BF16)
    scaled_out[...] = scaled
    tail_in = (dot(tail3[...], spread) * scaled.astype(F32)).astype(BF16)
    local[:, pl.ds(pl.multiple_of(j * CHUNK, CHUNK), CHUNK)] = dot(maps_in_t[...], tail_in)

    @pl.when(j == pl.num_programs(0) - 1)
    def _():
        span = local.shape[1] // 2
        decay = jnp.broadcast_to(total3[RIM - 1 : RIM, :], (8, LANES)).astype(BF16)
        for piece in range(sent.shape[0]):
            group, side = piece // 2, piece % 2
            block = local[8 * group : 8 * group + 8, side * span : (side + 1) * span]
            sent[piece, :, 0:span] = block.astype(BF16)
            sent[piece, :, span:] = decay


def inside_kernel(
    normed, gate_w, scaled, conv, cum, cum_rows, scores, skip, inside, gate, *, heads_here
):
    j = pl.program_id(0)
    length = scaled.shape[0]
    half = length // 2
    per = CHUNK // P_SIZE
    lane = lax.broadcasted_iota(jnp.int32, scaled.shape, 1) // P_SIZE
    slots = head_slot((LANES, length), heads_here)
    x = scaled[...]
    tops, bottoms, top_x, all_x = [], [], [], []
    for i in range(per):
        head = j * per + i
        pick = jnp.where(slots == head, 1.0, 0.0).astype(BF16)
        cum_t = dot(cum[...], pick)
        cum_s = cum_rows[pl.ds(head, 1), :]
        own = jnp.where(lane == i, x, jnp.zeros_like(x))
        upper = jnp.exp(jnp.minimum(cum_t[:half, :half] - cum_s[:, :half], 0.0))
        lower = jnp.exp(jnp.minimum(cum_t[half:] - cum_s, 0.0))
        tops.append((upper * scores[0:half, 0:half]).astype(BF16))
        bottoms.append((lower * scores[half:, :]).astype(BF16))
        top_x.append(own[:half])
        all_x.append(own)
    upper = dot(jnp.concatenate(tops, axis=1), jnp.concatenate(top_x, axis=0))
    lower = dot(jnp.concatenate(bottoms, axis=1), jnp.concatenate(all_x, axis=0))
    inside[...] = jnp.concatenate([upper, lower], axis=0) + skip[...] * conv[...].astype(F32)
    vals = dot(normed[...], gate_w[...]).astype(BF16).astype(F32)
    gate[...] = vals * jax.nn.sigmoid(vals)


def scan_kernel(place, got, back, *, heads_here):
    blocks, depth, width = got.shape
    span = width - LANES
    side = place[0] % 2
    spread = spread_matrix(side * (span // P_SIZE), span, heads_here)
    parts = got[:, :, span:].astype(F32).reshape(blocks * depth, LANES).astype(BF16)
    decay = dot(parts, spread)
    state = jnp.zeros((depth, span), F32)
    for b in range(blocks):
        back[b] = state.astype(BF16)
        if b < blocks - 1:
            state = decay[b * depth : (b + 1) * depth] * state + got[b, :, 0:span].astype(F32)


def out_kernel(
    place,
    got,
    maps,
    head_decay,
    inside,
    gate,
    norm_gain,
    out_w,
    out0,
    out1,
    out2,
    out3,
    states,
    x,
    sums,
    *,
    heads_here,
):
    j = pl.program_id(0)
    outs = (out0, out1, out2, out3)
    length = inside.shape[0]
    rows = length // 4
    width = out_w.shape[1] * pl.num_programs(0)

    @pl.when(j == 0)
    def _():
        here = place[0]
        span = got.shape[2]
        for piece in range(got.shape[0]):
            group, side = piece // 2, piece % 2
            states[8 * group : 8 * group + 8, side * span : (side + 1) * span] = got[
                piece
            ].astype(F32)
        total = jnp.zeros((length, 1), F32)
        for c in range(inside.shape[1] // CHUNK):
            cols = slice(c * CHUNK, (c + 1) * CHUNK)
            spread = spread_matrix(c * (CHUNK // P_SIZE), CHUNK, heads_here)
            carried = dot(maps[...], states[:, cols].astype(BF16)) * dot(head_decay[...], spread)
            gated = (inside[:, cols] + carried) * gate[:, cols]
            total = total + jnp.sum(gated * gated, axis=1, keepdims=True)
            ready = (gated * norm_gain[:, cols]).astype(BF16)
            for b in range(4):
                start = pl.multiple_of(((b + 4 - here) % 4) * rows, rows)
                x[pl.ds(start, rows), cols] = ready[b * rows : (b + 1) * rows]
        packed = by_lane(jnp.broadcast_to(total, (length, LANES)), 1)
        for b in range(4):
            start = pl.multiple_of(((b + 4 - here) % 4) * rows, rows)
            sums[pl.ds(start, rows), :] = packed[b * rows : (b + 1) * rows]
        for d in range(4):
            outs[d][:, 5 * WIDE :] = sums[d * rows : (d + 1) * rows, :]

    part = dot(x[...], out_w[...]).astype(BF16)
    for d in range(4):
        start = pl.multiple_of(j * WIDE, WIDE)
        outs[d][:, pl.ds(start, WIDE)] = part[d * rows : (d + 1) * rows]


def whole(shape):
    return pl.BlockSpec(shape, lambda j: (0,) * len(shape))


def columns(shape):
    return pl.BlockSpec(shape, lambda j: (0, j))


def smem():
    return pl.BlockSpec(memory_space=pltpu.SMEM)


def params():
    return pltpu.CompilerParams(
        dimension_semantics=("arbitrary",), vmem_limit_bytes=VMEM_LIMIT
    )


def on_device(
    tokens,
    input_gain,
    gate_weight,
    inner_weight,
    state_weight,
    step_weight,
    step_bias,
    decay_exponent,
    conv_inner,
    conv_state,
    skip_gain,
    norm_gain,
    out_weight,
    passage_lengths,
):
    rows, width = tokens.shape
    heads = lax.axis_size("head")
    blocks = lax.axis_size("seq")
    heads_here = step_weight.shape[1]
    channels = heads_here * P_SIZE
    length = heads * rows
    passages = passage_lengths.shape[0]
    span = channels // 2
    steps = channels // CHUNK
    here = lax.axis_index("head")
    block = lax.axis_index("seq")
    place = jnp.stack([here, block * length]).astype(jnp.int32)

    def lanes3(a):
        a = jnp.concatenate([a] * 3, axis=-1)
        return jnp.pad(a, ((0, 0), (0, LANES - a.shape[1])))

    step_w = lanes3(step_weight)
    bias = lanes3(step_bias[None])
    rate = lanes3(decay_exponent.astype(F32)[None] * 2.0 ** (-21))
    skip = jnp.repeat(skip_gain, P_SIZE)[None]
    below, above, top, bottom, rim = gather_tokens(tokens)

    def shape(dims, kind):
        return jax.ShapeDtypeStruct(dims, kind)

    half = rows // 2
    normed, sent, conv, scaled, cum, cum_rows, scores, maps, head_decay = pl.pallas_call(
        lambda *refs: block_kernel(*refs, heads_here=heads_here),
        grid=(steps,),
        in_specs=[
            smem(),
            whole((1, passages)),
            whole((passages, 1)),
            whole((rows, width)),
            whole((rows, width)),
            whole((rows, width)),
            whole((half + RIM, width)),
            whole((half, width)),
            whole((RIM, width)),
            whole((1, width)),
            whole((width, 2 * N)),
            whole((width, LANES)),
            whole((1, LANES)),
            whole((1, LANES)),
            whole((K, 2 * N)),
            columns((width, CHUNK)),
            columns((K, CHUNK)),
        ],
        out_specs=[
            whole((length, width)),
            whole((blocks, 8, span + LANES)),
            columns((length, CHUNK)),
            columns((length, CHUNK)),
            whole((length, LANES)),
            whole((LANES, length)),
            whole((length, length)),
            whole((length, N)),
            whole((length, LANES)),
        ],
        out_shape=[
            shape((length, width), BF16),
            shape((blocks, 8, span + LANES), BF16),
            shape((length, channels), BF16),
            shape((length, channels), BF16),
            shape((length, LANES), BF16),
            shape((LANES, length), F32),
            shape((length, length), F32),
            shape((length, N), BF16),
            shape((length, LANES), BF16),
        ],
        scratch_shapes=[
            pltpu.VMEM((length + RIM, width), BF16),
            pltpu.VMEM((K - 1, length, LANES), F32),
            pltpu.VMEM((length, LANES), BF16),
            pltpu.VMEM((length, LANES), BF16),
            pltpu.VMEM((N, length), BF16),
            pltpu.VMEM((N, channels), F32),
            pltpu.VMEM((RIM, LANES), F32),
        ],
        compiler_params=params(),
        name="block",
    )(
        place,
        passage_lengths[None],
        passage_lengths[:, None],
        tokens,
        below,
        above,
        top,
        bottom,
        rim,
        input_gain[None],
        state_weight,
        step_w,
        bias,
        rate,
        conv_state,
        inner_weight,
        conv_inner,
    )

    got = lax.all_to_all(sent, "seq", 0, 0, tiled=True)
    inside, gate = pl.pallas_call(
        lambda *refs: inside_kernel(*refs, heads_here=heads_here),
        grid=(steps,),
        in_specs=[
            whole((length, width)),
            columns((width, CHUNK)),
            columns((length, CHUNK)),
            columns((length, CHUNK)),
            whole((length, LANES)),
            whole((LANES, length)),
            whole((length, length)),
            columns((1, CHUNK)),
        ],
        out_specs=[columns((length, CHUNK)), columns((length, CHUNK))],
        out_shape=[shape((length, channels), F32), shape((length, channels), F32)],
        compiler_params=params(),
        name="inside",
    )(normed, gate_weight, scaled, conv, cum, cum_rows, scores, skip)

    back = pl.pallas_call(
        lambda *refs: scan_kernel(*refs, heads_here=heads_here),
        in_specs=[smem(), pl.BlockSpec(memory_space=pltpu.VMEM)],
        out_specs=pl.BlockSpec(memory_space=pltpu.VMEM),
        out_shape=shape((blocks, 8, span), BF16),
        compiler_params=pltpu.CompilerParams(vmem_limit_bytes=VMEM_LIMIT),
        name="scan",
    )(block.astype(jnp.int32)[None], got)
    states = lax.all_to_all(back, "seq", 0, 0, tiled=True)

    out_width = out_weight.shape[1]
    parts = pl.pallas_call(
        lambda *refs: out_kernel(*refs, heads_here=heads_here),
        grid=(out_width // WIDE,),
        in_specs=[
            smem(),
            whole((blocks, 8, span)),
            whole((length, N)),
            whole((length, LANES)),
            whole((length, channels)),
            whole((length, channels)),
            whole((1, channels)),
            columns((channels, WIDE)),
        ],
        out_specs=[whole((rows, out_width + LANES))] * 4,
        out_shape=[shape((rows, out_width + LANES), BF16)] * 4,
        scratch_shapes=[
            pltpu.VMEM((N, channels), F32),
            pltpu.VMEM((length, channels), BF16),
            pltpu.VMEM((length, LANES), BF16),
        ],
        compiler_params=params(),
        name="out",
    )(place, states, maps, head_decay, inside, gate, norm_gain[None], out_weight)
    total = parts[0].astype(F32)
    for distance in range(1, heads):
        total = total + around(parts[distance], "head", distance).astype(F32)
    mean = jnp.sum(total[:, out_width : out_width + 3], axis=1, keepdims=True) / (H * P_SIZE)
    return (total[:, :out_width] * lax.rsqrt(mean + 1e-05)).astype(BF16)


def solution(mesh):
    in_specs = (
        P(("seq", "head"), None),
        P(),
        P(None, "head"),
        P(None, "head"),
        P(),
        P(None, "head"),
        P("head"),
        P("head"),
        P(None, "head"),
        P(),
        P("head"),
        P("head"),
        P("head", None),
        P(),
    )
    out_specs = P(("seq", "head"), None)
    return jax.shard_map(
        on_device, mesh=mesh, in_specs=in_specs, out_specs=out_specs, check_vma=False
    )
```

time: 156 us -> 112 us (0.72)
  other arithmetic: 32 us -> 2.53 us
  matrix products: 23.3 us -> 0 us
  Pallas kernels: 0 us -> 20 us
  blocking collectives: 0 us -> 18.8 us
  starting transfers between devices: 31.1 us -> 15.5 us
  waiting for transfers between devices: 35.6 us -> 27 us
  local copies, waits for them, and re-layouts: 32.6 us -> 27.2 us
    dot_general x9 -> x0, matrix products: 23.3 us -> none  [the longest x1 5.8 us: on_device(): jnp.dot(normed[RIM:], gate_weight, preferred_element_type=jnp.float32)]
    unnamed x65 -> x77, local copies, waits for them, and re-layouts: 2.37 us -> 25.2 us
    unnamed x30 -> x0, other arithmetic: 21.2 us -> none
    pallas_call x0 -> x4, Pallas kernels: none -> 20 us  [the longest x1 9.25 us: on_device(): pl.pallas_call(lambda *refs: block_kernel(*refs, heads_here=heads_here),...]
    all_to_all x0 -> x1, blocking collectives: none -> 18.8 us  [on_device(): got = lax.all_to_all(sent, 'seq', 0, 0, tiled=True)]
    broadcast_in_dim x67 -> x4, local copies, waits for them, and re-layouts: 14.3 us -> 0.18 us  [the longest x1 0.1 us: on_device(): passage_lengths[:, None]]
    all_to_all x2 -> x1, starting transfers between devices: 13.5 us -> 3.66 us  [on_device(): states = lax.all_to_all(back, 'seq', 0, 0, tiled=True)]
    reshape x4 -> x0, local copies, waits for them, and re-layouts: 7.45 us -> none  [the longest x3 5.96 us: spread(): return jnp.repeat(x, P_SIZE, axis=1)]
  transfers between devices with their start and end apart: 12 -> 10, of which waited for: 6 -> 6; matrix products, arithmetic and copies ran while one was open for 16% -> 4% of each run, Pallas kernels for 0% -> 5%
where the time goes in v2:
time: 112 us; the launch traced here: 111 us
  local copies, waits for them, and re-layouts  27.2 us (24%)
  waiting for transfers between devices  27 us (24%)
  Pallas kernels  20 us (18%)
  blocking collectives  18.8 us (17%)
  starting transfers between devices  15.5 us (14%)
  other arithmetic  2.53 us (2%)
    unnamed x77, local copies, waits for them, and re-layouts  25.2 us
    ppermute x7, waiting for transfers between devices, around(): lax.ppermute(block, axis, [(i, (i + distance) % size) for i in range(size)])  22.8 us
    all_to_all x1, blocking collectives, on_device(): got = lax.all_to_all(sent, 'seq', 0, 0, tiled=True)  18.8 us
    ppermute x7, starting transfers between devices, around(): lax.ppermute(block, axis, [(i, (i + distance) % size) for i in range(size)])  9.92 us
    pallas_call x1, Pallas kernels, on_device(): pl.pallas_call(lambda *refs: block_kernel(*refs, heads_here=heads_here),...  9.25 us
    pallas_call x1, Pallas kernels, on_device(): pl.pallas_call(lambda *refs: inside_kernel(*refs, heads_here=heads_here),...  5.58 us
    ppermute x2, waiting for transfers between devices, gather_tokens(): piece = lax.ppermute(tail, ('seq', 'head'), route)  4.21 us
    pallas_call x1, Pallas kernels, on_device(): pl.pallas_call(lambda *refs: out_kernel(*refs, heads_here=heads_here), gr...  4.16 us
  transfers between devices with their start and end apart: 10, of which 6 were waited for; matrix products, arithmetic and copies ran while one was open for 4% of the time, Pallas kernels for 5%

profile of v2, /device:TPU:1, one launch (start us, length us, event | category | flops | bytes accessed | tf_op | source)
XLA Modules:
  0.0 111.3 jit_solution(11814185258305342289)
XLA Ops:
  0.0 2.5 %collective-permute-start = (bf16[64,2560]{1,0:T(8,128)(2,1)}, bf16[64,2560]{1,0:T(8,128)(2,1)S(1)}, u32[]{:S(2)}, u32[]{:S(2)}) collective-permute-start(bf16[64,2560]{1,0:T(8,128)(2,1)} %refs_3_.1), channel_id=1, source_target_pairs={{0,1},{1,2},{2,3},{3,0},{4,5},{5,6},{6,7},{7,4},{8,9},{9,10},{10,1... | collective-permute-start | bytes 983048 | tf_op jit(solution)/shard_map/ppermute | solution.py:23
  2.5 2.1 %collective-permute-start.1 = (bf16[64,2560]{1,0:T(8,128)(2,1)}, bf16[64,2560]{1,0:T(8,128)(2,1)S(1)}, u32[]{:S(2)}, u32[]{:S(2)}) collective-permute-start(bf16[64,2560]{1,0:T(8,128)(2,1)} %refs_3_.1), channel_id=1, source_target_pairs={{0,3},{1,0},{2,1},{3,2},{4,7},{5,4},{6,5},{7,6},{8,11},{9,8},{10,9... | collective-permute-start | bytes 983048 | tf_op jit(solution)/shard_map/ppermute | solution.py:23
  5.5 1.3 %collective-permute-start.2 = (bf16[16,2560]{1,0:T(8,128)(2,1)S(1)}, bf16[16,2560]{1,0:T(8,128)(2,1)S(1)}, u32[]{:S(2)}, u32[]{:S(2)}) collective-permute-start(bf16[16,2560]{1,0:T(8,128)(2,1)S(1)} %slice.16), channel_id=1, source_target_pairs={{3,4},{7,8},{11,12},{15,16},{19,20},{23,24},{27,28},{31,32},{35,36... | collective-permute-start | bytes 245768 | tf_op jit(solution)/shard_map/ppermute | solution.py:38
  7.5 1.3 %copy.15 = bf16[2560,20]{1,0:T(8,128)(2,1)S(1)} copy(bf16[2560,20]{0,1:T(8,128)(2,1)} %param.19) | data formatting | bytes 204800 | tf_op args[5]
  9.4 4.2 %collective-permute-done.2 = bf16[16,2560]{1,0:T(8,128)(2,1)S(1)} collective-permute-done((bf16[16,2560]{1,0:T(8,128)(2,1)S(1)}, bf16[16,2560]{1,0:T(8,128)(2,1)S(1)}, u32[]{:S(2)}, u32[]{:S(2)}) %collective-permute-start.2) | collective-permute-done | bytes 81952 | tf_op jit(solution)/shard_map/ppermute | solution.py:38
  14.6 2.6 %collective-permute-start.5 = (bf16[32,2560]{1,0:T(8,128)(2,1)}, bf16[32,2560]{1,0:T(8,128)(2,1)S(1)}, u32[]{:S(2)}, u32[]{:S(2)}) collective-permute-start(bf16[32,2560]{1,0:T(8,128)(2,1)} %slice.21), channel_id=1, source_target_pairs={{0,3},{1,0},{2,1},{3,2},{4,7},{5,4},{6,5},{7,6},{8,11},{9,8},{10,9... | collective-permute-start | bytes 491528 | tf_op jit(solution)/shard_map/ppermute | solution.py:23
  18.1 3.1 %collective-permute-done.5.refs_7_ = bf16[32,2560]{1,0:T(8,128)(2,1)S(1)} collective-permute-done((bf16[32,2560]{1,0:T(8,128)(2,1)}, bf16[32,2560]{1,0:T(8,128)(2,1)S(1)}, u32[]{:S(2)}, u32[]{:S(2)}) %collective-permute-start.5) | collective-permute-done | bytes 163872 | tf_op jit(solution)/shard_map/ppermute | solution.py:23
  21.2 1.5 %collective-permute-done.4.refs_6_ = bf16[48,2560]{1,0:T(8,128)(2,1)S(1)} collective-permute-done((bf16[48,2560]{1,0:T(8,128)(2,1)S(1)}, bf16[48,2560]{1,0:T(8,128)(2,1)S(1)}, u32[]{:S(2)}, u32[]{:S(2)}) %collective-permute-start.4) | collective-permute-done | bytes 245792 | tf_op jit(solution)/shard_map/ppermute | solution.py:23
  23.5 2.9 %copy-done = bf16[2560,1280]{1,0:T(8,128)(2,1)S(1)} copy-done((bf16[2560,1280]{1,0:T(8,128)(2,1)S(1)}, bf16[2560,1280]{1,0:T(8,128)(2,1)}, u32[]{:S(2)}) %copy-start) | copy-done | bytes 6553624
  33.0 9.2 %block.1 = (bf16[256,2560]{1,0:T(8,128)(2,1)S(1)}, bf16[32,8,768]{2,1,0:T(8,128)(2,1)S(1)}, bf16[256,1280]{1,0:T(8,128)(2,1)S(1)}, bf16[256,1280]{1,0:T(8,128)(2...) custom-call(s32[2]{0:T(128)S(1)} %copy-done.31, ...), custom_call_target="tpu_custom_call" | custom-call | tf_op jit(solution)/shard_map/block/pallas_call | solution.py:383
  44.0 18.8 %all_to_all.10.refs_1_ = bf16[32,8,768]{2,1,0:T(8,128)(2,1)S(1)} all-to-all(bf16[32,8,768]{2,1,0:T(8,128)(2,1)S(1)} %get-tuple-element.20), channel_id=1, replica_groups=mesh['seq'=32,'head'=4] {'seq'}, dimensions={0} | all-to-all | bytes 786432 | tf_op jit(solution)/shard_map/all_to_all | solution.py:458
  63.8 3.7 %all-to-all-start.1 = ((bf16[32,8,640]{2,1,0:T(8,128)(2,1)}), bf16[32,8,640]{2,1,0:T(8,128)(2,1)S(1)}, u32[]{:S(2)}, u32[]{:S(2)}) async-start(bf16[32,8,640]{2,1,0:T(8,128)(2,1)} %scan.1), calls=%async_computation.1 | async-start | bytes 655360 | tf_op jit(solution)/shard_map/all_to_all | solution.py:486
  67.7 2.9 %copy-done.1 = bf16[2560,1280]{1,0:T(8,128)(2,1)S(1)} copy-done((bf16[2560,1280]{1,0:T(8,128)(2,1)S(1)}, bf16[2560,1280]{1,0:T(8,128)(2,1)}, u32[]{:S(2)}) %copy-start.1) | copy-done | bytes 6553624
  70.5 1.1 copy-done.11
  71.6 1.1 copy-done.13
  74.5 5.6 %inside.1 = (f32[256,1280]{1,0:T(8,128)S(1)}, f32[256,1280]{1,0:T(8,128)S(1)}) custom-call(bf16[256,2560]{1,0:T(8,128)(2,1)S(1)} %get-tuple-element.23.refs_0_, bf16[2560,1280]{1,0:T(8,128)(2,1)S(1)} %copy-done.1, bf16[256,1280]{1,0:T(8,128)(2,1)S(1)} %copy-done.13, bf16[256,1280]{1,0:T(8,128)(2,1)S(1)} %copy-done.11, bf16[256,128]{1,0:T(8,128)(2,1)S(1)} %copy-done.26, ...), custom_call_target="tpu_custom_call" | custom-call | tf_op jit(solution)/shard_map/inside/pallas_call | solution.py:459
  80.1 1.1 copy-done.4
  81.2 2.9 %copy-done.2 = bf16[1280,2560]{1,0:T(8,128)(2,1)S(1)} copy-done((bf16[1280,2560]{1,0:T(8,128)(2,1)S(1)}, bf16[1280,2560]{1,0:T(8,128)(2,1)}, u32[]{:S(2)}) %copy-start.2) | copy-done | bytes 6553624
  84.0 1.3 %copy-done.5 = f32[256,1280]{1,0:T(8,128)S(1)} copy-done((f32[256,1280]{1,0:T(8,128)S(1)}, f32[256,1280]{1,0:T(8,128)}, u32[]{:S(2)}) %copy-start.5) | copy-done | bytes 1310744
  85.4 4.2 %out.1 = (bf16[64,2688]{1,0:T(8,128)(2,1)S(1)}, bf16[64,2688]{1,0:T(8,128)(2,1)S(1)}, bf16[64,2688]{1,0:T(8,128)(2,1)S(1)}, bf16[64,2688]{1,0:T(8,128)(2,1)S(1)}) custom-call(s32[2]{0:T(128)S(1)} %copy-done.32, bf16[32,8,640]{2,1,0:T(8,128)(2,1)S(1)} %all-to-all-done.1.refs_1_, bf16[256,128]{1,0:T(8,128)(2,1)S(1)} %copy-done.22, ...), custom_call_target="tpu_custom_call" | custom-call | tf_op jit(solution)/shard_map/out/pallas_call | solution.py:489
  89.5 2.0 %collective-permute-start.8 = (bf16[64,2688]{1,0:T(8,128)(2,1)S(1)}, bf16[64,2688]{1,0:T(8,128)(2,1)S(1)}, u32[]{:S(2)}, u32[]{:S(2)}) collective-permute-start(bf16[64,2688]{1,0:T(8,128)(2,1)S(1)} %get-tuple-element.34), channel_id=1, source_target_pairs={{0,3},{1,0},{2,1},{3,2},{4,7},{5,4},{6,5},{7,6},{8,11},{9,8},{10,9... | collective-permute-start | bytes 1032200 | tf_op jit(solution)/shard_map/ppermute | solution.py:23
  92.2 7.1 %collective-permute-done.8 = bf16[64,2688]{1,0:T(8,128)(2,1)S(1)} collective-permute-done((bf16[64,2688]{1,0:T(8,128)(2,1)S(1)}, bf16[64,2688]{1,0:T(8,128)(2,1)S(1)}, u32[]{:S(2)}, u32[]{:S(2)}) %collective-permute-start.8) | collective-permute-done | bytes 344096 | tf_op jit(solution)/shard_map/ppermute | solution.py:23
  99.2 3.1 %collective-permute-done.7 = bf16[64,2688]{1,0:T(8,128)(2,1)S(1)} collective-permute-done((bf16[64,2688]{1,0:T(8,128)(2,1)S(1)}, bf16[64,2688]{1,0:T(8,128)(2,1)S(1)}, u32[]{:S(2)}, u32[]{:S(2)}) %collective-permute-start.7) | collective-permute-done | bytes 344096 | tf_op jit(solution)/shard_map/ppermute | solution.py:23
  102.3 7.9 %collective-permute-done.6 = bf16[64,2688]{1,0:T(8,128)(2,1)S(1)} collective-permute-done((bf16[64,2688]{1,0:T(8,128)(2,1)S(1)}, bf16[64,2688]{1,0:T(8,128)(2,1)S(1)}, u32[]{:S(2)}, u32[]{:S(2)}) %collective-permute-start.6) | collective-permute-done | bytes 344096 | tf_op jit(solution)/shard_map/ppermute | solution.py:23
  (96 shorter events, 17.7 us)
Async XLA Ops:
  0.0 13.7 %collective-permute-start = (bf16[64,2560]{1,0:T(8,128)(2,1)}, bf16[64,2560]{1,0:T(8,128)(2,1)S(1)}, u32[]{:S(2)}, u32[]{:S(2)}) collective-permute-start(bf16[64,2560]{1,0:T(8,128)(2,1)} %refs_3_.1), channel_id=1, source_target_pairs={{0,1},{1,2},{2,3},{3,0},{4,5},{5,6},{6,7},{7,4},{8,9},{9,10},{10,1... | collective-permute-start | bytes 983048 | tf_op jit(solution)/shard_map/ppermute | solution.py:23
  2.5 11.4 %collective-permute-start.1 = (bf16[64,2560]{1,0:T(8,128)(2,1)}, bf16[64,2560]{1,0:T(8,128)(2,1)S(1)}, u32[]{:S(2)}, u32[]{:S(2)}) collective-permute-start(bf16[64,2560]{1,0:T(8,128)(2,1)} %refs_3_.1), channel_id=1, source_target_pairs={{0,3},{1,0},{2,1},{3,2},{4,7},{5,4},{6,5},{7,6},{8,11},{9,8},{10,9... | collective-permute-start | bytes 983048 | tf_op jit(solution)/shard_map/ppermute | solution.py:23
  5.5 8.1 %collective-permute-start.2 = (bf16[16,2560]{1,0:T(8,128)(2,1)S(1)}, bf16[16,2560]{1,0:T(8,128)(2,1)S(1)}, u32[]{:S(2)}, u32[]{:S(2)}) collective-permute-start(bf16[16,2560]{1,0:T(8,128)(2,1)S(1)} %slice.16), channel_id=1, source_target_pairs={{3,4},{7,8},{11,12},{15,16},{19,20},{23,24},{27,28},{31,32},{35,36... | collective-permute-start | bytes 245768 | tf_op jit(solution)/shard_map/ppermute | solution.py:38
  6.8 6.8 %collective-permute-start.3 = (bf16[16,2560]{1,0:T(8,128)(2,1)S(1)}, bf16[16,2560]{1,0:T(8,128)(2,1)S(1)}, u32[]{:S(2)}, u32[]{:S(2)}) collective-permute-start(bf16[16,2560]{1,0:T(8,128)(2,1)S(1)} %slice.16), channel_id=1, source_target_pairs={{3,6},{7,10},{11,14},{15,18},{19,22},{23,26},{27,30},{31,34},{35,3... | collective-permute-start | bytes 245768 | tf_op jit(solution)/shard_map/ppermute | solution.py:38
  8.7 9.2 %copy-start.29 = (s32[64]{0:T(128)S(1)}, s32[64]{0:T(128)}, u32[]{:S(2)}) copy-start(s32[64]{0:T(128)} %param.27) | copy-start | bytes 772
  8.8 14.7 %copy-start.3 = (bf16[2560,256]{1,0:T(8,128)(2,1)S(1)}, bf16[2560,256]{1,0:T(8,128)(2,1)}, u32[]{:S(2)}) copy-start(bf16[2560,256]{1,0:T(8,128)(2,1)} %refs_10_.1) | copy-start | bytes 3932164
  9.4 8.6 %copy-start.33 = (f32[2560]{0:T(1024)S(1)}, f32[2560]{0:T(1024)}, u32[]{:S(2)}) copy-start(f32[2560]{0:T(1024)} %param.15) | copy-start | bytes 30724
  9.4 8.6 %copy-start.36 = (f32[20]{0:T(128)S(1)}, f32[20]{0:T(128)}, u32[]{:S(2)}) copy-start(f32[20]{0:T(128)} %param.20) | copy-start | bytes 244
  13.7 9.8 %copy-start.6 = (bf16[64,2560]{1,0:T(8,128)(2,1)}, bf16[64,2560]{1,0:T(8,128)(2,1)S(1)}, u32[]{:S(2)}) copy-start(bf16[64,2560]{1,0:T(8,128)(2,1)S(1)} %collective-permute-done.refs_4_) | copy-start | bytes 983044
  13.7 9.0 %collective-permute-start.4 = (bf16[48,2560]{1,0:T(8,128)(2,1)S(1)}, bf16[48,2560]{1,0:T(8,128)(2,1)S(1)}, u32[]{:S(2)}, u32[]{:S(2)}) collective-permute-start(bf16[48,2560]{1,0:T(8,128)(2,1)S(1)} %pad_maximum_fusion), channel_id=1, source_target_pairs={{0,1},{1,2},{2,3},{3,0},{4,5},{5,6},{6,7},{7,4},{8,9},{9,10},{10,1... | collective-permute-start | bytes 737288 | tf_op jit(solution)/shard_map/ppermute | solution.py:23
  13.9 9.6 %copy-start.8 = (bf16[64,2560]{1,0:T(8,128)(2,1)}, bf16[64,2560]{1,0:T(8,128)(2,1)S(1)}, u32[]{:S(2)}) copy-start(bf16[64,2560]{1,0:T(8,128)(2,1)S(1)} %collective-permute-done.1.refs_5_) | copy-start | bytes 983044
  14.6 6.6 %collective-permute-start.5 = (bf16[32,2560]{1,0:T(8,128)(2,1)}, bf16[32,2560]{1,0:T(8,128)(2,1)S(1)}, u32[]{:S(2)}, u32[]{:S(2)}) collective-permute-start(bf16[32,2560]{1,0:T(8,128)(2,1)} %slice.21), channel_id=1, source_target_pairs={{0,3},{1,0},{2,1},{3,2},{4,7},{5,4},{6,5},{7,6},{8,11},{9,8},{10,9... | collective-permute-start | bytes 491528 | tf_op jit(solution)/shard_map/ppermute | solution.py:23
  43.9 18.9 %copy-start.15 = (f32[256,256]{1,0:T(8,128)}, f32[256,256]{1,0:T(8,128)S(1)}, u32[]{:S(2)}) copy-start(f32[256,256]{1,0:T(8,128)S(1)} %get-tuple-element.28.refs_6_) | copy-start | bytes 786436
  43.9 18.9 %copy-start.19 = (f32[128,256]{1,0:T(8,128)}, f32[128,256]{1,0:T(8,128)S(1)}, u32[]{:S(2)}) copy-start(f32[128,256]{1,0:T(8,128)S(1)} %get-tuple-element.27.refs_5_) | copy-start | bytes 393220
  43.9 18.9 %copy-start.21 = (bf16[256,128]{1,0:T(8,128)(2,1)}, bf16[256,128]{1,0:T(8,128)(2,1)S(1)}, u32[]{:S(2)}) copy-start(bf16[256,128]{1,0:T(8,128)(2,1)S(1)} %get-tuple-element.21.refs_2_) | copy-start | bytes 196612
  43.9 18.9 %copy-start.23 = (bf16[256,128]{1,0:T(8,128)(2,1)}, bf16[256,128]{1,0:T(8,128)(2,1)S(1)}, u32[]{:S(2)}) copy-start(bf16[256,128]{1,0:T(8,128)(2,1)S(1)} %get-tuple-element.22.refs_3_) | copy-start | bytes 196612
  43.9 18.9 %copy-start.25 = (bf16[256,128]{1,0:T(8,128)(2,1)}, bf16[256,128]{1,0:T(8,128)(2,1)S(1)}, u32[]{:S(2)}) copy-start(bf16[256,128]{1,0:T(8,128)(2,1)S(1)} %get-tuple-element.26.refs_4_) | copy-start | bytes 196612
  44.0 23.5 %copy-start.35 = (f32[20]{0:T(128)S(1)}, f32[20]{0:T(128)}, u32[]{:S(2)}) copy-start(f32[20]{0:T(128)} %param.24) | copy-start | bytes 244
  44.0 23.7 %copy-start.34 = (f32[1280]{0:T(1024)S(1)}, f32[1280]{0:T(1024)}, u32[]{:S(2)}) copy-start(f32[1280]{0:T(1024)} %param.25) | copy-start | bytes 15364
  63.8 17.3 %all-to-all-start.1 = ((bf16[32,8,640]{2,1,0:T(8,128)(2,1)}), bf16[32,8,640]{2,1,0:T(8,128)(2,1)S(1)}, u32[]{:S(2)}, u32[]{:S(2)}) async-start(bf16[32,8,640]{2,1,0:T(8,128)(2,1)} %scan.1), calls=%async_computation.1 | async-start | bytes 655360 | tf_op jit(solution)/shard_map/all_to_all | solution.py:486
  74.5 6.7 %copy-start.32 = (s32[2]{0:T(128)S(1)}, s32[2]{0:T(128)}, u32[]{:S(2)}) copy-start(s32[2]{0:T(128)} %pad_add_fusion.refs_0_) | copy-start | bytes 28
  89.5 9.7 %collective-permute-start.8 = (bf16[64,2688]{1,0:T(8,128)(2,1)S(1)}, bf16[64,2688]{1,0:T(8,128)(2,1)S(1)}, u32[]{:S(2)}, u32[]{:S(2)}) collective-permute-start(bf16[64,2688]{1,0:T(8,128)(2,1)S(1)} %get-tuple-element.34), channel_id=1, source_target_pairs={{0,3},{1,0},{2,1},{3,2},{4,7},{5,4},{6,5},{7,6},{8,11},{9,8},{10,9... | collective-permute-start | bytes 1032200 | tf_op jit(solution)/shard_map/ppermute | solution.py:23
  91.5 10.8 %collective-permute-start.7 = (bf16[64,2688]{1,0:T(8,128)(2,1)S(1)}, bf16[64,2688]{1,0:T(8,128)(2,1)S(1)}, u32[]{:S(2)}, u32[]{:S(2)}) collective-permute-start(bf16[64,2688]{1,0:T(8,128)(2,1)S(1)} %get-tuple-element.33), channel_id=1, source_target_pairs={{0,2},{1,3},{2,0},{3,1},{4,6},{5,7},{6,4},{7,5},{8,10},{9,11},{10,... | collective-permute-start | bytes 1032200 | tf_op jit(solution)/shard_map/ppermute | solution.py:23
  91.7 18.5 %collective-permute-start.6 = (bf16[64,2688]{1,0:T(8,128)(2,1)S(1)}, bf16[64,2688]{1,0:T(8,128)(2,1)S(1)}, u32[]{:S(2)}, u32[]{:S(2)}) collective-permute-start(bf16[64,2688]{1,0:T(8,128)(2,1)S(1)} %get-tuple-element.32), channel_id=1, source_target_pairs={{0,1},{1,2},{2,3},{3,0},{4,5},{5,6},{6,7},{7,4},{8,9},{9,10},{10,1... | collective-permute-start | bytes 1032200 | tf_op jit(solution)/shard_map/ppermute | solution.py:23
  (24 other events, 47.3 us)

commit v3 on v2

--- a/solution.py
+++ b/solution.py
@@ -13,7 +13,7 @@
 LANES = 128
 CHUNK = 256
 WIDE = 512
-VMEM_LIMIT = 40 << 20
+VMEM_LIMIT = 60 << 20
 F32 = jnp.float32
 BF16 = jnp.bfloat16
 
@@ -31,15 +31,19 @@
     below = around(tokens, "head", 1)
     above = around(tokens, "head", heads - 1)
     rim = None
-    for target in range(0, heads, 2):
+    for target in range(2):
         route = [
             (s * heads + heads - 1, (s + 1) * heads + target) for s in range(blocks - 1)
         ]
         piece = lax.ppermute(tail, ("seq", "head"), route)
         rim = piece if rim is None else rim + piece
-    top = around(jnp.concatenate([below[:half], rim]), "head", 1)
-    bottom = around(above[half:], "head", heads - 1)
+    top = around(tokens[:half], "head", 2)
+    bottom = around(jnp.concatenate([tokens[half:], rim]), "head", 2)
     return below, above, top, bottom, rim
+
+
+def far_memory(x):
+    return pltpu.with_memory_space_constraint(x, pltpu.HBM)
 
 
 def split3(x):
@@ -142,9 +146,9 @@
         put((here + 3) % 4, 0, below[...])
         put((here + 1) % 4, 0, above[...])
         far = (here + 2) % 4
-        put(far, 0, top[0:half, :])
-        put(far, half, bottom[...])
-        rim_tokens = (rim[...].astype(F32) + top[half:, :].astype(F32)).astype(BF16)
+        put(far, 0, top[...])
+        put(far, half, bottom[0:half, :])
+        rim_tokens = (rim[...].astype(F32) + bottom[half:, :].astype(F32)).astype(BF16)
         normed[0:RIM, :] = norm(rim_tokens)
         normed_out[...] = normed[RIM:, :]
 
@@ -374,7 +378,7 @@
     bias = lanes3(step_bias[None])
     rate = lanes3(decay_exponent.astype(F32)[None] * 2.0 ** (-21))
     skip = jnp.repeat(skip_gain, P_SIZE)[None]
-    below, above, top, bottom, rim = gather_tokens(tokens)
+    below, above, top, bottom, rim = map(far_memory, gather_tokens(tokens))
 
     def shape(dims, kind):
         return jax.ShapeDtypeStruct(dims, kind)
@@ -390,8 +394,8 @@
             whole((rows, width)),
             whole((rows, width)),
             whole((rows, width)),
+            whole((half, width)),
             whole((half + RIM, width)),
-            whole((half, width)),
             whole((RIM, width)),
             whole((1, width)),
             whole((width, 2 * N)),
@@ -483,7 +487,7 @@
         compiler_params=pltpu.CompilerParams(vmem_limit_bytes=VMEM_LIMIT),
         name="scan",
     )(block.astype(jnp.int32)[None], got)
-    states = lax.all_to_all(back, "seq", 0, 0, tiled=True)
+    states = far_memory(lax.all_to_all(back, "seq", 0, 0, tiled=True))
 
     out_width = out_weight.shape[1]
     parts = pl.pallas_call(

time: 112 us -> 105 us (0.938)
  local copies, waits for them, and re-layouts: 27.2 us -> 7.31 us
  Pallas kernels: 20 us -> 31.6 us
  other arithmetic: 2.53 us -> 4.89 us
    unnamed x77 -> x25, local copies, waits for them, and re-layouts: 25.2 us -> 2.73 us
    pallas_call x1, Pallas kernels: 4.16 us -> 8.14 us  [on_device(): pl.pallas_call(lambda *refs: out_kernel(*refs, heads_here=heads_here), gr...]
    pallas_call x1, Pallas kernels: 9.25 us -> 12.9 us  [on_device(): pl.pallas_call(lambda *refs: block_kernel(*refs, heads_here=heads_here),...]
    pallas_call x1, Pallas kernels: 5.58 us -> 8.63 us  [on_device(): pl.pallas_call(lambda *refs: inside_kernel(*refs, heads_here=heads_here),...]
    ppermute x2, waiting for transfers between devices: 4.21 us -> 2.43 us  [gather_tokens(): piece = lax.ppermute(tail, ('seq', 'head'), route)]
    concatenate x2, other arithmetic: 0.72 us -> 2.16 us  [lanes3(): a = jnp.concatenate([a] * 3, axis=-1)]
    ppermute x7, waiting for transfers between devices: 22.8 us -> 24 us  [around(): lax.ppermute(block, axis, [(i, (i + distance) % size) for i in range(size)])]
  transfers between devices with their start and end apart: 10 -> 10, of which waited for: 6 -> 4; matrix products, arithmetic and copies ran while one was open for 4% -> 8% of each run, Pallas kernels for 5% -> 8%
where the time goes in v3:
time: 105 us; the launch traced here: 104 us
  Pallas kernels  31.6 us (30%)
  waiting for transfers between devices  26.4 us (25%)
  blocking collectives  19 us (18%)
  starting transfers between devices  14.7 us (14%)
  local copies, waits for them, and re-layouts  7.31 us (7%)
  other arithmetic  4.89 us (5%)
    ppermute x7, waiting for transfers between devices, around(): lax.ppermute(block, axis, [(i, (i + distance) % size) for i in range(size)])  24 us
    all_to_all x1, blocking collectives, on_device(): got = lax.all_to_all(sent, 'seq', 0, 0, tiled=True)  19 us
    pallas_call x1, Pallas kernels, on_device(): pl.pallas_call(lambda *refs: block_kernel(*refs, heads_here=heads_here),...  12.9 us
    ppermute x7, starting transfers between devices, around(): lax.ppermute(block, axis, [(i, (i + distance) % size) for i in range(size)])  9.1 us
    pallas_call x1, Pallas kernels, on_device(): pl.pallas_call(lambda *refs: inside_kernel(*refs, heads_here=heads_here),...  8.63 us
    pallas_call x1, Pallas kernels, on_device(): pl.pallas_call(lambda *refs: out_kernel(*refs, heads_here=heads_here), gr...  8.14 us
    all_to_all x1, starting transfers between devices, on_device(): states = far_memory(lax.all_to_all(back, 'seq', 0, 0, tiled=True))  3.66 us
    unnamed x25, local copies, waits for them, and re-layouts  2.73 us
  transfers between devices with their start and end apart: 10, of which 4 were waited for; matrix products, arithmetic and copies ran while one was open for 8% of the time, Pallas kernels for 8%

profile of v3, /device:TPU:1, one launch (start us, length us, event | category | flops | bytes accessed | tf_op | source)
XLA Modules:
  0.0 104.2 jit_solution(15645454507310418147)
XLA Ops:
  0.0 2.5 %collective-permute-start = (bf16[64,2560]{1,0:T(8,128)(2,1)}, bf16[64,2560]{1,0:T(8,128)(2,1)S(1)}, u32[]{:S(2)}, u32[]{:S(2)}) collective-permute-start(bf16[64,2560]{1,0:T(8,128)(2,1)} %refs_3_.1), channel_id=1, source_target_pairs={{0,1},{1,2},{2,3},{3,0},{4,5},{5,6},{6,7},{7,4},{8,9},{9,10},{10,1... | collective-permute-start | bytes 983048 | tf_op jit(solution)/shard_map/ppermute | solution.py:23
  2.5 2.1 %collective-permute-start.1 = (bf16[64,2560]{1,0:T(8,128)(2,1)}, bf16[64,2560]{1,0:T(8,128)(2,1)S(1)}, u32[]{:S(2)}, u32[]{:S(2)}) collective-permute-start(bf16[64,2560]{1,0:T(8,128)(2,1)} %refs_3_.1), channel_id=1, source_target_pairs={{0,3},{1,0},{2,1},{3,2},{4,7},{5,4},{6,5},{7,6},{8,11},{9,8},{10,9... | collective-permute-start | bytes 983048 | tf_op jit(solution)/shard_map/ppermute | solution.py:23
  4.6 0.9 slice.17
  5.5 1.3 %collective-permute-start.3 = (bf16[16,2560]{1,0:T(8,128)(2,1)S(1)}, bf16[16,2560]{1,0:T(8,128)(2,1)S(1)}, u32[]{:S(2)}, u32[]{:S(2)}) collective-permute-start(bf16[16,2560]{1,0:T(8,128)(2,1)S(1)} %slice.17), channel_id=1, source_target_pairs={{3,4},{7,8},{11,12},{15,16},{19,20},{23,24},{27,28},{31,32},{35,36... | collective-permute-start | bytes 245768 | tf_op jit(solution)/shard_map/ppermute | solution.py:38
  7.5 1.0 fusion.6
  8.6 0.8 collective-permute-start.2
  9.3 1.3 %copy.15 = bf16[2560,20]{1,0:T(8,128)(2,1)S(1)} copy(bf16[2560,20]{0,1:T(8,128)(2,1)} %param.19) | data formatting | bytes 204800 | tf_op args[5]
  10.6 1.5 %fusion.4.refs_11_ = bf16[2560,128]{1,0:T(8,128)(2,1)} fusion(bf16[2560,20]{1,0:T(8,128)(2,1)S(1)} %copy.15), kind=kLoop, calls=%fused_computation.6 | loop fusion | flops 3276800 | bytes 757760 | tf_op jit(solution)/shard_map/concatenate | solution.py:374
  12.1 2.4 %collective-permute-done.3 = bf16[16,2560]{1,0:T(8,128)(2,1)S(1)} collective-permute-done((bf16[16,2560]{1,0:T(8,128)(2,1)S(1)}, bf16[16,2560]{1,0:T(8,128)(2,1)S(1)}, u32[]{:S(2)}, u32[]{:S(2)}) %collective-permute-start.3) | collective-permute-done | bytes 81952 | tf_op jit(solution)/shard_map/ppermute | solution.py:38
  17.3 6.1 %collective-permute-done.5.refs_7_ = bf16[48,2560]{1,0:T(8,128)(2,1)S(1)} collective-permute-done((bf16[48,2560]{1,0:T(8,128)(2,1)S(1)}, bf16[48,2560]{1,0:T(8,128)(2,1)S(1)}, u32[]{:S(2)}, u32[]{:S(2)}) %collective-permute-start.5) | collective-permute-done | bytes 245792 | tf_op jit(solution)/shard_map/ppermute | solution.py:23
  23.4 0.7 copy-done.4
  24.1 12.9 %block.1 = (bf16[256,2560]{1,0:T(8,128)(2,1)}, bf16[32,8,768]{2,1,0:T(8,128)(2,1)}, bf16[256,1280]{1,0:T(8,128)(2,1)}, bf16[256,1280]{1,0:T(8,128)(2,1)}, bf16[2...) custom-call(s32[2]{0:T(128)} %pad_add_fusion.refs_0_, ...), custom_call_target="tpu_custom_call" | custom-call | tf_op jit(solution)/shard_map/block/pallas_call | solution.py:387
  37.0 19.0 %all_to_all.10.refs_1_ = bf16[32,8,768]{2,1,0:T(8,128)(2,1)} all-to-all(bf16[32,8,768]{2,1,0:T(8,128)(2,1)} %get-tuple-element.20), channel_id=1, replica_groups=mesh['seq'=32,'head'=4] {'seq'}, dimensions={0} | all-to-all | bytes 786432 | tf_op jit(solution)/shard_map/all_to_all | solution.py:462
  56.0 2.0 %scan.1 = bf16[32,8,640]{2,1,0:T(8,128)(2,1)} custom-call(s32[1]{0:T(128)} %bitcast.2.refs_0_, bf16[32,8,768]{2,1,0:T(8,128)(2,1)} %all_to_all.10.refs_1_), custom_call_target="tpu_custom_call" | custom-call | tf_op jit(solution)/shard_map/scan/pallas_call | solution.py:482
  58.0 3.7 %all-to-all-start.1 = ((bf16[32,8,640]{2,1,0:T(8,128)(2,1)}), bf16[32,8,640]{2,1,0:T(8,128)(2,1)S(1)}, u32[]{:S(2)}, u32[]{:S(2)}) async-start(bf16[32,8,640]{2,1,0:T(8,128)(2,1)} %scan.1), calls=%async_computation.1 | async-start | bytes 655360 | tf_op jit(solution)/shard_map/all_to_all | solution.py:490
  63.0 8.6 %inside.1 = (f32[256,1280]{1,0:T(8,128)}, f32[256,1280]{1,0:T(8,128)}) custom-call(bf16[256,2560]{1,0:T(8,128)(2,1)} %get-tuple-element.23.refs_0_, bf16[2560,1280]{1,0:T(8,128)(2,1)} %refs_1_.1, bf16[256,1280]{1,0:T(8,128)(2,1)} %get-tuple-element.24.refs_2_, bf16[256,1280]{1,0:T(8,128)(2,1)} %get-tuple-element.25.refs_3_, ...), custom_call_target="tpu_custom_call" | custom-call | tf_op jit(solution)/shard_map/inside/pallas_call | solution.py:463
  71.7 0.7 copy-done
  72.4 8.1 %out.1 = (bf16[64,2688]{1,0:T(8,128)(2,1)}, bf16[64,2688]{1,0:T(8,128)(2,1)}, bf16[64,2688]{1,0:T(8,128)(2,1)}, bf16[64,2688]{1,0:T(8,128)(2,1)}) custom-call(s32[2]{0:T(128)} %pad_add_fusion.refs_0_, bf16[32,8,640]{2,1,0:T(8,128)(2,1)} %copy-done, bf16[256,128]{1,0:T(8,128)(2,1)} %get-tuple-element.21.refs_2_, bf16[256,128]{1,0:T(8,128)(2,1)} %get-tuple-element.22.refs_3_, ...), custom_call_target="tpu_custom_call" | custom-call | tf_op jit(solution)/shard_map/out/pallas_call | solution.py:493
  80.5 2.5 %collective-permute-start.8 = (bf16[64,2688]{1,0:T(8,128)(2,1)}, bf16[64,2688]{1,0:T(8,128)(2,1)S(1)}, u32[]{:S(2)}, u32[]{:S(2)}) collective-permute-start(bf16[64,2688]{1,0:T(8,128)(2,1)} %get-tuple-element.34), channel_id=1, source_target_pairs={{0,3},{1,0},{2,1},{3,2},{4,7},{5,4},{6,5},{7,6},{8,11},{9,8},{10,9... | collective-permute-start | bytes 1032200 | tf_op jit(solution)/shard_map/ppermute | solution.py:23
  83.0 1.2 %collective-permute-start.7 = (bf16[64,2688]{1,0:T(8,128)(2,1)}, bf16[64,2688]{1,0:T(8,128)(2,1)S(1)}, u32[]{:S(2)}, u32[]{:S(2)}) collective-permute-start(bf16[64,2688]{1,0:T(8,128)(2,1)} %get-tuple-element.33), channel_id=1, source_target_pairs={{0,2},{1,3},{2,0},{3,1},{4,6},{5,7},{6,4},{7,5},{8,10},{9,11},{10,... | collective-permute-start | bytes 1032200 | tf_op jit(solution)/shard_map/ppermute | solution.py:23
  84.2 13.8 %collective-permute-done.8 = bf16[64,2688]{1,0:T(8,128)(2,1)S(1)} collective-permute-done((bf16[64,2688]{1,0:T(8,128)(2,1)}, bf16[64,2688]{1,0:T(8,128)(2,1)S(1)}, u32[]{:S(2)}, u32[]{:S(2)}) %collective-permute-start.8) | collective-permute-done | bytes 344096 | tf_op jit(solution)/shard_map/ppermute | solution.py:23
  98.0 4.1 %collective-permute-done.6 = bf16[64,2688]{1,0:T(8,128)(2,1)S(1)} collective-permute-done((bf16[64,2688]{1,0:T(8,128)(2,1)}, bf16[64,2688]{1,0:T(8,128)(2,1)S(1)}, u32[]{:S(2)}, u32[]{:S(2)}) %collective-permute-start.6) | collective-permute-done | bytes 344096 | tf_op jit(solution)/shard_map/ppermute | solution.py:23
  102.1 1.1 %convert_add_fusion = f32[64,2688]{1,0:T(8,128)S(1)} fusion(bf16[64,2688]{1,0:T(8,128)(2,1)S(1)} %collective-permute-done.8, bf16[64,2688]{1,0:T(8,128)(2,1)S(1)} %collective-permute-done.7, bf16[64,2688]{1,0:T(8,128)(2,1)S(1)} %collective-permute-done.6, bf16[64,2688]{1,0:T(8,128)(2,1)} %get-tuple-element.31), kind=kLoop, calls=%fused_computation.4 | loop fusion | flops 1204224 | bytes 2064384 | tf_op jit(solution)/shard_map/add | solution.py:518
  103.4 0.8 fusion.5
  (43 shorter events, 4.9 us)
Async XLA Ops:
  0.0 17.2 %collective-permute-start = (bf16[64,2560]{1,0:T(8,128)(2,1)}, bf16[64,2560]{1,0:T(8,128)(2,1)S(1)}, u32[]{:S(2)}, u32[]{:S(2)}) collective-permute-start(bf16[64,2560]{1,0:T(8,128)(2,1)} %refs_3_.1), channel_id=1, source_target_pairs={{0,1},{1,2},{2,3},{3,0},{4,5},{5,6},{6,7},{7,4},{8,9},{9,10},{10,1... | collective-permute-start | bytes 983048 | tf_op jit(solution)/shard_map/ppermute | solution.py:23
  2.5 14.8 %collective-permute-start.1 = (bf16[64,2560]{1,0:T(8,128)(2,1)}, bf16[64,2560]{1,0:T(8,128)(2,1)S(1)}, u32[]{:S(2)}, u32[]{:S(2)}) collective-permute-start(bf16[64,2560]{1,0:T(8,128)(2,1)} %refs_3_.1), channel_id=1, source_target_pairs={{0,3},{1,0},{2,1},{3,2},{4,7},{5,4},{6,5},{7,6},{8,11},{9,8},{10,9... | collective-permute-start | bytes 983048 | tf_op jit(solution)/shard_map/ppermute | solution.py:23
  5.5 9.0 %collective-permute-start.3 = (bf16[16,2560]{1,0:T(8,128)(2,1)S(1)}, bf16[16,2560]{1,0:T(8,128)(2,1)S(1)}, u32[]{:S(2)}, u32[]{:S(2)}) collective-permute-start(bf16[16,2560]{1,0:T(8,128)(2,1)S(1)} %slice.17), channel_id=1, source_target_pairs={{3,4},{7,8},{11,12},{15,16},{19,20},{23,24},{27,28},{31,32},{35,36... | collective-permute-start | bytes 245768 | tf_op jit(solution)/shard_map/ppermute | solution.py:38
  6.8 7.7 %collective-permute-start.4 = (bf16[16,2560]{1,0:T(8,128)(2,1)S(1)}, bf16[16,2560]{1,0:T(8,128)(2,1)S(1)}, u32[]{:S(2)}, u32[]{:S(2)}) collective-permute-start(bf16[16,2560]{1,0:T(8,128)(2,1)S(1)} %slice.17), channel_id=1, source_target_pairs={{3,5},{7,9},{11,13},{15,17},{19,21},{23,25},{27,29},{31,33},{35,37... | collective-permute-start | bytes 245768 | tf_op jit(solution)/shard_map/ppermute | solution.py:38
  8.5 6.1 %copy-start.11 = (s32[20]{0:T(128)S(1)}, s32[20]{0:T(128)}, u32[]{:S(2)}) copy-start(s32[20]{0:T(128)} %param.21) | copy-start | bytes 244
  8.5 6.8 %copy-start.8 = (s32[64]{0:T(128)S(1)}, s32[64]{0:T(128)}, u32[]{:S(2)}) copy-start(s32[64]{0:T(128)} %param.27) | copy-start | bytes 772
  8.5 7.4 %copy-start.6 = (f32[2560]{0:T(1024)S(1)}, f32[2560]{0:T(1024)}, u32[]{:S(2)}) copy-start(f32[2560]{0:T(1024)} %param.15) | copy-start | bytes 30724
  8.5 8.0 %copy-start.10 = (f32[20]{0:T(128)S(1)}, f32[20]{0:T(128)}, u32[]{:S(2)}) copy-start(f32[20]{0:T(128)} %param.20) | copy-start | bytes 244
  8.6 8.7 %collective-permute-start.2 = (bf16[32,2560]{1,0:T(8,128)(2,1)S(1)}, bf16[32,2560]{1,0:T(8,128)(2,1)S(1)}, u32[]{:S(2)}, u32[]{:S(2)}) collective-permute-start(bf16[32,2560]{1,0:T(8,128)(2,1)S(1)} %get-tuple-element.36), channel_id=1, source_target_pairs={{0,2},{1,3},{2,0},{3,1},{4,6},{5,7},{6,4},{7,5},{8,10},{9,11},{10,... | collective-permute-start | bytes 491528 | tf_op jit(solution)/shard_map/ppermute | solution.py:23
  14.5 8.9 %copy-start.1 = (bf16[16,2560]{1,0:T(8,128)(2,1)}, bf16[16,2560]{1,0:T(8,128)(2,1)S(1)}, u32[]{:S(2)}) copy-start(bf16[16,2560]{1,0:T(8,128)(2,1)S(1)} %add.29.refs_8_) | copy-start | bytes 245764
  14.6 8.8 %collective-permute-start.5 = (bf16[48,2560]{1,0:T(8,128)(2,1)S(1)}, bf16[48,2560]{1,0:T(8,128)(2,1)S(1)}, u32[]{:S(2)}, u32[]{:S(2)}) collective-permute-start(bf16[48,2560]{1,0:T(8,128)(2,1)S(1)} %pad_maximum_fusion), channel_id=1, source_target_pairs={{0,2},{1,3},{2,0},{3,1},{4,6},{5,7},{6,4},{7,5},{8,10},{9,11},{10,... | collective-permute-start | bytes 737288 | tf_op jit(solution)/shard_map/ppermute | solution.py:23
  17.2 6.1 %copy-start.5 = (bf16[32,2560]{1,0:T(8,128)(2,1)}, bf16[32,2560]{1,0:T(8,128)(2,1)S(1)}, u32[]{:S(2)}) copy-start(bf16[32,2560]{1,0:T(8,128)(2,1)S(1)} %collective-permute-done.2.refs_6_) | copy-start | bytes 491524
  17.3 6.1 %copy-start.2 = (bf16[64,2560]{1,0:T(8,128)(2,1)}, bf16[64,2560]{1,0:T(8,128)(2,1)S(1)}, u32[]{:S(2)}) copy-start(bf16[64,2560]{1,0:T(8,128)(2,1)S(1)} %collective-permute-done.refs_4_) | copy-start | bytes 983044
  17.3 6.1 %copy-start.3 = (bf16[64,2560]{1,0:T(8,128)(2,1)}, bf16[64,2560]{1,0:T(8,128)(2,1)S(1)}, u32[]{:S(2)}) copy-start(bf16[64,2560]{1,0:T(8,128)(2,1)S(1)} %collective-permute-done.1.refs_5_) | copy-start | bytes 983044
  23.4 0.7 copy-start.4
  37.0 24.7 %copy-start.9 = (f32[20]{0:T(128)S(1)}, f32[20]{0:T(128)}, u32[]{:S(2)}) copy-start(f32[20]{0:T(128)} %param.24) | copy-start | bytes 244
  37.0 25.4 %copy-start.7 = (f32[1280]{0:T(1024)S(1)}, f32[1280]{0:T(1024)}, u32[]{:S(2)}) copy-start(f32[1280]{0:T(1024)} %param.25) | copy-start | bytes 15364
  58.0 13.7 %all-to-all-start.1 = ((bf16[32,8,640]{2,1,0:T(8,128)(2,1)}), bf16[32,8,640]{2,1,0:T(8,128)(2,1)S(1)}, u32[]{:S(2)}, u32[]{:S(2)}) async-start(bf16[32,8,640]{2,1,0:T(8,128)(2,1)} %scan.1), calls=%async_computation.1 | async-start | bytes 655360 | tf_op jit(solution)/shard_map/all_to_all | solution.py:490
  71.6 0.7 copy-start
  80.5 17.5 %collective-permute-start.8 = (bf16[64,2688]{1,0:T(8,128)(2,1)}, bf16[64,2688]{1,0:T(8,128)(2,1)S(1)}, u32[]{:S(2)}, u32[]{:S(2)}) collective-permute-start(bf16[64,2688]{1,0:T(8,128)(2,1)} %get-tuple-element.34), channel_id=1, source_target_pairs={{0,3},{1,0},{2,1},{3,2},{4,7},{5,4},{6,5},{7,6},{8,11},{9,8},{10,9... | collective-permute-start | bytes 1032200 | tf_op jit(solution)/shard_map/ppermute | solution.py:23
  83.0 15.0 %collective-permute-start.7 = (bf16[64,2688]{1,0:T(8,128)(2,1)}, bf16[64,2688]{1,0:T(8,128)(2,1)S(1)}, u32[]{:S(2)}, u32[]{:S(2)}) collective-permute-start(bf16[64,2688]{1,0:T(8,128)(2,1)} %get-tuple-element.33), channel_id=1, source_target_pairs={{0,2},{1,3},{2,0},{3,1},{4,6},{5,7},{6,4},{7,5},{8,10},{9,11},{10,... | collective-permute-start | bytes 1032200 | tf_op jit(solution)/shard_map/ppermute | solution.py:23
  84.2 17.9 %collective-permute-start.6 = (bf16[64,2688]{1,0:T(8,128)(2,1)}, bf16[64,2688]{1,0:T(8,128)(2,1)S(1)}, u32[]{:S(2)}, u32[]{:S(2)}) collective-permute-start(bf16[64,2688]{1,0:T(8,128)(2,1)} %get-tuple-element.32), channel_id=1, source_target_pairs={{0,1},{1,2},{2,3},{3,0},{4,5},{5,6},{6,7},{7,4},{8,9},{9,10},{10,1... | collective-permute-start | bytes 1032200 | tf_op jit(solution)/shard_map/ppermute | solution.py:23

commit v4 on v0

v4 whole, which is shorter than its diff:
```python
import jax
import jax.numpy as jnp
from jax import lax
from jax.experimental import pallas as pl
from jax.experimental.pallas import tpu as pltpu
from jax.sharding import PartitionSpec as P

H = 80
P_SIZE = 64
N = 128
K = 4
RIM = 16
LANES = 128
CHUNK = 256
WIDE = 512
BLOCK_LIMIT = 16
INSIDE_LIMIT = 16
OUT_LIMIT = 16
SMALL_LIMIT = 8
F32 = jnp.float32
BF16 = jnp.bfloat16


def around(block, axis, distance):
    size = lax.axis_size(axis)
    return lax.ppermute(block, axis, [(i, (i + distance) % size) for i in range(size)])


def gather_tokens(tokens, inner_weight, state_weight):
    heads = lax.axis_size("head")
    blocks = lax.axis_size("seq")
    half = tokens.shape[0] // 2
    bottom = around(tokens[half:], "head", 2)
    below = around(tokens, "head", 1)
    above = around(tokens, "head", heads - 1)
    top = around(tokens[:half], "head", 2)
    (near,) = call(
        near_kernel,
        "near",
        [vmem()] * 2,
        [jax.ShapeDtypeStruct((16, LANES), tokens.dtype)],
        [],
        BLOCK_LIMIT,
    )(inner_weight, state_weight)
    (tail,) = call(
        tail_kernel,
        "tail",
        [vmem()] * 5,
        [jax.ShapeDtypeStruct((RIM, tokens.shape[1]), tokens.dtype)],
        [],
        SMALL_LIMIT,
    )(below, bottom, above, tokens, near)
    rim = lax.ppermute(tail, "seq", [(s, s + 1) for s in range(blocks - 1)])
    return below, above, top, bottom, rim


def split3(x):
    first = x.astype(BF16).astype(F32)
    rest = x - first
    second = rest.astype(BF16).astype(F32)
    return first, second, rest - second


def by_lane(x, count):
    lane = lax.broadcasted_iota(jnp.int32, x.shape, 1)
    first, second, third = split3(x)
    picked = jnp.where(lane < count, first, jnp.where(lane < 2 * count, second, third))
    return jnp.where(lane < 3 * count, picked, 0.0).astype(BF16)


def head_slot(shape, count):
    slot = lax.broadcasted_iota(jnp.int32, shape, 0)
    live = slot < 3 * count
    slot = slot - jnp.where(slot >= 2 * count, 2 * count, jnp.where(slot >= count, count, 0))
    return jnp.where(live, slot, -1)


def spread_matrix(first_head, width, count):
    shape = (LANES, width)
    head = first_head + lax.broadcasted_iota(jnp.int32, shape, 1) // P_SIZE
    return jnp.where(head_slot(shape, count) == head, 1.0, 0.0).astype(BF16)


def dot(a, b):
    return jnp.dot(a, b, preferred_element_type=F32)


def near_kernel(inner_w, state_w, near):
    near[...] = inner_w[0:16, 0:LANES] + state_w[0:16, 0:LANES]


def tail_kernel(below, bottom, above, own, near, tail):
    here = lax.axis_index("head")
    last = [x[x.shape[0] - RIM :, :] for x in (below, bottom, above, own)]
    low = jnp.where(here == 0, last[0], last[1])
    high = jnp.where(here == 2, last[2], last[3])
    tail[...] = jnp.where(here < 2, low, high)


def repeat_lanes(x):
    count = x.shape[1]
    lane = lax.broadcasted_iota(jnp.int32, (count, LANES), 1)
    slot = lax.broadcasted_iota(jnp.int32, (count, LANES), 0)
    hits = (lane == slot) | (lane == slot + count) | (lane == slot + 2 * count)
    copies = jnp.where(hits, 1.0, 0.0).astype(BF16)
    return sum(dot(part.astype(BF16), copies) for part in split3(x))


def block_kernel(
    lens_row,
    own,
    below,
    above,
    top,
    bottom,
    rim,
    gain,
    step_w,
    step_bias,
    rate,
    taps_state,
    taps_inner,
    state_w,
    inner_w,
    normed_out,
    sent,
    conv_out,
    scaled_out,
    cum_out,
    cum_rows,
    scores_out,
    maps_out,
    head_decay_out,
    normed,
    local,
    *,
    heads_here,
):
    rows = own.shape[0]
    length = normed.shape[0] - RIM
    here = lax.axis_index("head")
    first = lax.axis_index("seq") * length

    def norm(x):
        x = x.astype(F32)
        mean = jnp.mean(x * x, axis=-1, keepdims=True)
        return (x * lax.rsqrt(mean + 1e-05) * gain[...]).astype(BF16)

    def put(owner, offset, x):
        start = pl.multiple_of(RIM + owner * rows + offset, RIM)
        normed[pl.ds(start, x.shape[0]), :] = norm(x)

    half = rows // 2
    put(here, 0, own[...])
    put((here + 3) % 4, 0, below[...])
    put((here + 1) % 4, 0, above[...])
    far = (here + 2) % 4
    put(far, 0, top[...])
    put(far, half, bottom[...])
    normed[0:RIM, :] = norm(rim[...])
    normed_out[...] = normed[RIM:, :]

    passages = lens_row.shape[1]
    up = lax.broadcasted_iota(jnp.int32, (passages, passages), 0)
    across = lax.broadcasted_iota(jnp.int32, (passages, passages), 1)
    lens = jnp.broadcast_to(lens_row[...].astype(F32), (8, passages))
    whole = jnp.floor(lens * (1.0 / 128.0))
    before = jnp.where(up < across, 1.0, 0.0).astype(BF16)
    starts_row = 128.0 * dot(whole.astype(BF16), before)
    starts_row = (starts_row + dot((lens - 128.0 * whole).astype(BF16), before))[0:1]
    starts_col = jnp.sum(
        jnp.where(across < up, lens_row[...].astype(F32), 0.0), axis=1, keepdims=True
    )
    base = first.astype(F32)
    pos = lax.broadcasted_iota(jnp.int32, (length + RIM, passages), 0).astype(F32)
    ids_pad = jnp.sum(
        jnp.where(pos + (base - RIM) >= starts_row, 1.0, 0.0), axis=1, keepdims=True
    )
    pos = lax.broadcasted_iota(jnp.int32, (passages, length), 1).astype(F32)
    ids_row = jnp.sum(jnp.where(pos + base >= starts_col, 1.0, 0.0), axis=0, keepdims=True)
    ids_wide = jnp.broadcast_to(ids_pad, (length + RIM, LANES))
    ids = ids_wide[RIM:]
    agree = [
        jnp.where(pltpu.roll(ids_wide, lag, 0)[RIM:] == ids, 1.0, 0.0) for lag in range(1, K)
    ]

    def conv(raw, taps):
        acc = taps[0:1] * raw[RIM:]
        for lag in range(1, K):
            moved = pltpu.roll(raw, lag, 0)[RIM:]
            same = jnp.concatenate([agree[lag - 1]] * (raw.shape[1] // LANES), axis=1)
            acc = acc + taps[lag : lag + 1] * moved * same
        return (acc * jax.nn.sigmoid(acc)).astype(BF16)

    x = lax.dot_general(
        normed[RIM:, :], step_w[...], (((1,), (1,)), ((), ())), preferred_element_type=F32
    )
    x = repeat_lanes(x + step_bias[...])
    rates = jnp.broadcast_to(rate[...].astype(F32) * 2.0 ** (-21), (8, rate.shape[1]))
    raw = dot(normed[...], state_w[...]).astype(BF16).astype(F32)
    maps = conv(raw, taps_state[...])
    maps_in = maps[:, :N]
    maps_out[...] = maps[:, N:]
    maps_in_t = maps_in.astype(F32).T.astype(BF16)
    t = lax.broadcasted_iota(jnp.int32, (length, length), 0)
    s = lax.broadcasted_iota(jnp.int32, (length, length), 1)
    ids_two = jnp.concatenate([ids] * (length // LANES), axis=1)
    mask = (ids_two == ids_row) & (t >= s)
    scores_out[...] = jnp.where(mask, dot(maps[:, N:], maps_in_t), 0.0)

    step = jnp.maximum(x, 0.0) + jnp.log1p(jnp.exp(-jnp.abs(x)))
    log_decay = -step * repeat_lanes(rates)[0:1]
    ones = jnp.where(t >= s, 1.0, 0.0).astype(BF16)
    cum = sum(dot(ones, part.astype(BF16)) for part in split3(log_decay))
    last = cum[length - 1 :, :]
    ids_last = ids[length - 1 :, :]
    prior = ids_wide[RIM - 1 : RIM, :]
    step3 = by_lane(step, heads_here)
    tail = jnp.exp(jnp.minimum(last - cum, 0.0)) * jnp.where(ids == ids_last, 1.0, 0.0)
    tail3 = by_lane(tail, heads_here)
    keep = jnp.exp(cum) * jnp.where(ids == prior, 1.0, 0.0)
    keep3 = by_lane(keep, heads_here)
    head_decay_out[...] = keep3
    cum_out[...] = by_lane(cum, heads_here)
    cum_rows[...] = cum.T

    for c in range(local.shape[1] // CHUNK):
        cols = slice(c * CHUNK, (c + 1) * CHUNK)
        raw = dot(normed[...], inner_w[:, cols]).astype(BF16).astype(F32)
        mixed = conv(raw, taps_inner[:, cols])
        conv_out[:, cols] = mixed
        spread = spread_matrix(c * (CHUNK // P_SIZE), CHUNK, heads_here)
        scaled = (mixed.astype(F32) * dot(step3, spread)).astype(BF16)
        scaled_out[:, cols] = scaled
        tail_in = (dot(tail3, spread) * scaled.astype(F32)).astype(BF16)
        local[:, cols] = dot(maps_in_t, tail_in)

    span = local.shape[1] // 2
    decay = jnp.broadcast_to(keep3[length - RIM :].astype(F32)[RIM - 1 :], (8, LANES))
    for piece in range(sent.shape[0]):
        group, side = piece // 2, piece % 2
        part = local[8 * group : 8 * group + 8, side * span : (side + 1) * span]
        sent[piece, :, 0:span] = part.astype(BF16)
        sent[piece, :, span:] = decay.astype(BF16)


def inside_kernel(
    normed,
    scaled,
    conv,
    cum,
    cum_rows,
    scores,
    skip,
    gate_w,
    inside,
    gate,
    *,
    heads_here,
):
    length = scaled.shape[0]
    half = length // 2
    per = CHUNK // P_SIZE
    lane = lax.broadcasted_iota(jnp.int32, (length, CHUNK), 1) // P_SIZE
    slots = head_slot((LANES, length), heads_here)
    skip3 = by_lane(repeat_lanes(jnp.broadcast_to(skip[...], (8, heads_here))), heads_here)
    for c in range(scaled.shape[1] // CHUNK):
        cols = slice(c * CHUNK, (c + 1) * CHUNK)
        x = scaled[:, cols]
        tops, bottoms, top_x, all_x = [], [], [], []
        for i in range(per):
            head = c * per + i
            pick = jnp.where(slots == head, 1.0, 0.0).astype(BF16)
            cum_t = dot(cum[...], pick)
            cum_s = cum_rows[head : head + 1, :]
            own = jnp.where(lane == i, x, jnp.zeros_like(x))
            upper = jnp.exp(jnp.minimum(cum_t[:half, :half] - cum_s[:, :half], 0.0))
            lower = jnp.exp(jnp.minimum(cum_t[half:] - cum_s, 0.0))
            tops.append((upper * scores[0:half, 0:half]).astype(BF16))
            bottoms.append((lower * scores[half:, :]).astype(BF16))
            top_x.append(own[:half])
            all_x.append(own)
        spread = spread_matrix(c * per, CHUNK, heads_here)
        skips = dot(skip3, spread)[0:1]
        upper = dot(jnp.concatenate(tops, axis=1), jnp.concatenate(top_x, axis=0))
        lower = dot(jnp.concatenate(bottoms, axis=1), jnp.concatenate(all_x, axis=0))
        inside[:, cols] = jnp.concatenate([upper, lower], axis=0) + (
            skips * conv[:, cols].astype(F32)
        )
        vals = dot(normed[...], gate_w[:, cols]).astype(BF16).astype(F32)
        gate[:, cols] = vals * jax.nn.sigmoid(vals)


def scan_kernel(got, back, *, heads_here):
    blocks, depth, width = got.shape
    span = width - LANES
    side = lax.axis_index("seq") % 2
    spread = spread_matrix(side * (span // P_SIZE), span, heads_here)
    parts = got[:, :, span:].astype(F32).reshape(blocks * depth, LANES).astype(BF16)
    decay = dot(parts, spread)
    state = jnp.zeros((depth, span), F32)
    for b in range(blocks):
        back[b] = state.astype(BF16)
        if b < blocks - 1:
            state = decay[b * depth : (b + 1) * depth] * state + got[b, :, 0:span].astype(F32)


def out_kernel(
    got,
    maps,
    head_decay,
    inside,
    gate,
    norm_gain,
    out_w,
    out0,
    out1,
    out2,
    out2b,
    out3,
    states,
    x,
    sums,
    *,
    heads_here,
):
    length = inside.shape[0]
    rows = length // 4
    half = rows // 2
    here = lax.axis_index("head")
    span = got.shape[2]
    for piece in range(got.shape[0]):
        group, side = piece // 2, piece % 2
        states[8 * group : 8 * group + 8, side * span : (side + 1) * span] = got[piece].astype(
            F32
        )
    total = jnp.zeros((length, 1), F32)
    for c in range(inside.shape[1] // CHUNK):
        cols = slice(c * CHUNK, (c + 1) * CHUNK)
        spread = spread_matrix(c * (CHUNK // P_SIZE), CHUNK, heads_here)
        carried = dot(maps[...], states[:, cols].astype(BF16)) * dot(head_decay[...], spread)
        gated = (inside[:, cols] + carried) * gate[:, cols]
        total = total + jnp.sum(gated * gated, axis=1, keepdims=True)
        ready = (gated * norm_gain[:, cols]).astype(BF16)
        for b in range(4):
            start = pl.multiple_of(((b + 4 - here) % 4) * rows, rows)
            x[pl.ds(start, rows), cols] = ready[b * rows : (b + 1) * rows]
    packed = by_lane(jnp.broadcast_to(total, (length, LANES)), 1)
    for b in range(4):
        start = pl.multiple_of(((b + 4 - here) % 4) * rows, rows)
        sums[pl.ds(start, rows), :] = packed[b * rows : (b + 1) * rows]

    def put(cols, part):
        out0[:, cols] = part[0:rows]
        out1[:, cols] = part[rows : 2 * rows]
        out2[:, cols] = part[2 * rows : 2 * rows + half]
        out2b[:, cols] = part[2 * rows + half : 3 * rows]
        out3[:, cols] = part[3 * rows :]

    width = out_w.shape[1]
    for c in range(width // WIDE):
        cols = slice(c * WIDE, (c + 1) * WIDE)
        put(cols, dot(x[...], out_w[:, cols]).astype(BF16))
    put(slice(width, width + LANES), sums[...])


def close_kernel(own, one, two, two_b, three, mixed):
    width = mixed.shape[1]
    half = two.shape[0]
    for i, far in enumerate((two, two_b)):
        rows = slice(i * half, (i + 1) * half)
        total = own[rows, :].astype(F32) + one[rows, :].astype(F32)
        total = total + far[...].astype(F32) + three[rows, :].astype(F32)
        mean = jnp.sum(total[:, width:], axis=1, keepdims=True) / (H * P_SIZE)
        mixed[rows, :] = (total[:, :width] * lax.rsqrt(mean + 1e-05)).astype(BF16)


def vmem():
    return pl.BlockSpec(memory_space=pltpu.VMEM)


def call(kernel, name, in_specs, out_shape, scratch_shapes, limit):
    return pl.pallas_call(
        kernel,
        in_specs=in_specs,
        out_specs=[vmem()] * len(out_shape),
        out_shape=out_shape,
        scratch_shapes=scratch_shapes,
        compiler_params=pltpu.CompilerParams(vmem_limit_bytes=limit << 20),
        name=name,
    )


def on_device(
    tokens,
    input_gain,
    gate_weight,
    inner_weight,
    state_weight,
    step_weight,
    step_bias,
    decay_exponent,
    conv_inner,
    conv_state,
    skip_gain,
    norm_gain,
    out_weight,
    passage_lengths,
):
    rows, width = tokens.shape
    heads = lax.axis_size("head")
    blocks = lax.axis_size("seq")
    heads_here = step_weight.shape[1]
    channels = heads_here * P_SIZE
    length = heads * rows
    passages = passage_lengths.shape[0]
    span = channels // 2
    below, above, top, bottom, rim = gather_tokens(tokens, inner_weight, state_weight)

    def shape(dims, kind):
        return jax.ShapeDtypeStruct(dims, kind)

    normed, sent, conv, scaled, cum, cum_rows, scores, maps, head_decay = call(
        lambda *refs: block_kernel(*refs, heads_here=heads_here),
        "block",
        [vmem()] * 15,
        [
            shape((length, width), BF16),
            shape((blocks, 8, span + LANES), BF16),
            shape((length, channels), BF16),
            shape((length, channels), BF16),
            shape((length, LANES), BF16),
            shape((LANES, length), F32),
            shape((length, length), F32),
            shape((length, N), BF16),
            shape((length, LANES), BF16),
        ],
        [
            pltpu.VMEM((length + RIM, width), BF16),
            pltpu.VMEM((N, channels), F32),
        ],
        BLOCK_LIMIT,
    )(
        passage_lengths[None],
        tokens,
        below,
        above,
        top,
        bottom,
        rim,
        input_gain[None],
        step_weight.T,
        step_bias[None],
        decay_exponent[None],
        conv_state,
        conv_inner,
        state_weight,
        inner_weight,
    )

    inside, gate = call(
        lambda *refs: inside_kernel(*refs, heads_here=heads_here),
        "inside",
        [vmem()] * 8,
        [shape((length, channels), F32), shape((length, channels), F32)],
        [],
        INSIDE_LIMIT,
    )(normed, scaled, conv, cum, cum_rows, scores, skip_gain[None], gate_weight)
    sent, inside, gate, out_gain = lax.optimization_barrier(
        (sent, inside, gate, norm_gain[None])
    )
    got = lax.all_to_all(sent, "seq", 0, 0, tiled=True)

    (back,) = call(
        lambda *refs: scan_kernel(*refs, heads_here=heads_here),
        "scan",
        [vmem()],
        [shape((blocks, 8, span), BF16)],
        [],
        SMALL_LIMIT,
    )(got)
    states = lax.all_to_all(back, "seq", 0, 0, tiled=True)

    out_width = out_weight.shape[1]
    packed = out_width + LANES
    own, one, two, two_b, three = call(
        lambda *refs: out_kernel(*refs, heads_here=heads_here),
        "out",
        [vmem()] * 7,
        [shape((n, packed), BF16) for n in (rows, rows, rows // 2, rows // 2, rows)],
        [
            pltpu.VMEM((N, channels), F32),
            pltpu.VMEM((length, channels), BF16),
            pltpu.VMEM((length, LANES), BF16),
        ],
        OUT_LIMIT,
    )(states, maps, head_decay, inside, gate, out_gain, out_weight)
    (mixed,) = call(
        close_kernel,
        "close",
        [vmem()] * 5,
        [shape((rows, out_width), BF16)],
        [],
        SMALL_LIMIT,
    )(
        own,
        around(one, "head", 1),
        around(two, "head", 2),
        around(two_b, "head", 2),
        around(three, "head", 3),
    )
    return mixed


def solution(mesh):
    in_specs = (
        P(("seq", "head"), None),
        P(),
        P(None, "head"),
        P(None, "head"),
        P(),
        P(None, "head"),
        P("head"),
        P("head"),
        P(None, "head"),
        P(),
        P("head"),
        P("head"),
        P("head", None),
        P(),
    )
    out_specs = P(("seq", "head"), None)
    return jax.shard_map(
        on_device, mesh=mesh, in_specs=in_specs, out_specs=out_specs, check_vma=False
    )
```

time: 573 us -> 91.7 us (0.16)
  waiting for transfers between devices: 330 us -> 18.8 us
  starting transfers between devices: 165 us -> 20.4 us
  matrix products: 28.8 us -> 0 us
  blocking collectives: 7.39 us -> 31.4 us
  other arithmetic: 15.4 us -> 0.01 us
  Pallas kernels: 0 us -> 15.3 us
  between operations: 15.1 us -> 0.24 us
    ppermute x33 -> x9, waiting for transfers between devices: 233 us -> 18.8 us  [the longest x8 17.4 us: around(): lax.ppermute(block, axis, [(i, (i + distance) % size) for i in range(size)])]
    ppermute x33 -> x9, starting transfers between devices: 165 us -> 20.4 us  [the longest x8 14 us: around(): lax.ppermute(block, axis, [(i, (i + distance) % size) for i in range(size)])]
    reduce_scatter x1 -> x0, waiting for transfers between devices: 76.3 us -> none  [on_device(): lax.psum_scatter(jnp.dot(normed_out, out_weight, preferred_element_type=j...]
    all_to_all x0 -> x2, blocking collectives: none -> 31.4 us  [the longest x1 18.4 us: on_device(): got = lax.all_to_all(sent, 'seq', 0, 0, tiled=True)]
    dot_general x8 -> x0, matrix products: 26.4 us -> none  [the longest x1 6.7 us: on_device(): jnp.dot(normed_out, out_weight, preferred_element_type=jnp.float32)]
    all_gather x1 -> x0, waiting for transfers between devices: 21.3 us -> none  [on_device(): gathered = lax.all_gather(normed, 'head', axis=0, tiled=True)]
    pallas_call x0 -> x7, Pallas kernels: none -> 15.3 us  [the longest x1 8.07 us: on_device(): call(lambda *refs: block_kernel(*refs, heads_here=heads_here), 'block', [...]
    convert_element_type x7 -> x0, other arithmetic: 8.51 us -> none  [the longest x1 2.03 us: ssd_group(): (ids_part == ids_part[-1]).astype(jnp.float32)[:, None]]
  transfers between devices with their start and end apart: 35 -> 9, of which waited for: 33 -> 4; matrix products, arithmetic and copies ran while one was open for 3% -> 1% of each run, Pallas kernels for 0% -> 0%
where the time goes in v4:
time: 91.7 us; the launch traced here: 91.4 us
  blocking collectives  31.4 us (34%)
  starting transfers between devices  20.4 us (22%)
  waiting for transfers between devices  18.8 us (21%)
  Pallas kernels  15.3 us (17%)
  local copies, waits for them, and re-layouts  5.28 us (6%)
    all_to_all x1, blocking collectives, on_device(): got = lax.all_to_all(sent, 'seq', 0, 0, tiled=True)  18.4 us
    ppermute x8, waiting for transfers between devices, around(): lax.ppermute(block, axis, [(i, (i + distance) % size) for i in range(size)])  17.4 us
    ppermute x8, starting transfers between devices, around(): lax.ppermute(block, axis, [(i, (i + distance) % size) for i in range(size)])  14 us
    all_to_all x1, blocking collectives, on_device(): states = lax.all_to_all(back, 'seq', 0, 0, tiled=True)  13 us
    pallas_call x1, Pallas kernels, on_device(): call(lambda *refs: block_kernel(*refs, heads_here=heads_here), 'block', [...  8.07 us
    ppermute x1, starting transfers between devices, gather_tokens(): rim = lax.ppermute(tail, 'seq', [(s, s + 1) for s in range(blocks - 1)])  6.36 us
    unnamed x32, local copies, waits for them, and re-layouts  4.25 us
    pallas_call x1, Pallas kernels, on_device(): call(lambda *refs: inside_kernel(*refs, heads_here=heads_here), 'inside',...  3.59 us
  transfers between devices with their start and end apart: 9, of which 4 were waited for; matrix products, arithmetic and copies ran while one was open for 1% of the time, Pallas kernels for 0%

profile of v4, /device:TPU:1, one launch (start us, length us, event | category | flops | bytes accessed | tf_op | source)
XLA Modules:
  0.0 91.4 jit_solution(18415873637173543521)
XLA Ops:
  0.0 2.5 %collective-permute-start = (bf16[64,2560]{1,0:T(8,128)(2,1)}, bf16[64,2560]{1,0:T(8,128)(2,1)S(1)}, u32[]{:S(2)}, u32[]{:S(2)}) collective-permute-start(bf16[64,2560]{1,0:T(8,128)(2,1)} %refs_1_.1), channel_id=1, source_target_pairs={{0,1},{1,2},{2,3},{3,0},{4,5},{5,6},{6,7},{7,4},{8,9},{9,10},{10,1... | collective-permute-start | bytes 983048 | tf_op jit(solution)/shard_map/ppermute | solution.py:26
  2.5 2.1 %collective-permute-start.1 = (bf16[64,2560]{1,0:T(8,128)(2,1)}, bf16[64,2560]{1,0:T(8,128)(2,1)S(1)}, u32[]{:S(2)}, u32[]{:S(2)}) collective-permute-start(bf16[64,2560]{1,0:T(8,128)(2,1)} %refs_1_.1), channel_id=1, source_target_pairs={{0,3},{1,0},{2,1},{3,2},{4,7},{5,4},{6,5},{7,6},{8,11},{9,8},{10,9... | collective-permute-start | bytes 983048 | tf_op jit(solution)/shard_map/ppermute | solution.py:26
  4.6 1.0 %fusion = (bf16[32,2560]{1,0:T(8,128)(2,1)S(1)}, bf16[32,2560]{1,0:T(8,128)(2,1)S(1)}) fusion(bf16[64,2560]{1,0:T(8,128)(2,1)} %refs_1_.1), kind=kLoop, calls=%fused_computation | loop fusion | bytes 655360 | tf_op jit(solution)/shard_map/slice | solution.py:33
  5.6 1.4 %collective-permute-start.3 = (bf16[32,2560]{1,0:T(8,128)(2,1)S(1)}, bf16[32,2560]{1,0:T(8,128)(2,1)S(1)}, u32[]{:S(2)}, u32[]{:S(2)}) collective-permute-start(bf16[32,2560]{1,0:T(8,128)(2,1)S(1)} %get-tuple-element.45), channel_id=1, source_target_pairs={{0,2},{1,3},{2,0},{3,1},{4,6},{5,7},{6,4},{7,5},{8,10},{9,11},{10,... | collective-permute-start | bytes 491528 | tf_op jit(solution)/shard_map/ppermute | solution.py:26
  7.0 1.7 %collective-permute-start.2 = (bf16[32,2560]{1,0:T(8,128)(2,1)S(1)}, bf16[32,2560]{1,0:T(8,128)(2,1)S(1)}, u32[]{:S(2)}, u32[]{:S(2)}) collective-permute-start(bf16[32,2560]{1,0:T(8,128)(2,1)S(1)} %get-tuple-element.46), channel_id=1, source_target_pairs={{0,2},{1,3},{2,0},{3,1},{4,6},{5,7},{6,4},{7,5},{8,10},{9,11},{10,... | collective-permute-start | bytes 491528 | tf_op jit(solution)/shard_map/ppermute | solution.py:26
  8.7 2.9 %copy-done = bf16[2560,1280]{1,0:T(8,128)(2,1)S(1)} copy-done((bf16[2560,1280]{1,0:T(8,128)(2,1)S(1)}, bf16[2560,1280]{1,0:T(8,128)(2,1)}, u32[]{:S(2)}) %copy-start) | copy-done | bytes 6553624
  11.5 1.3 %copy-done.1 = bf16[2560,256]{1,0:T(8,128)(2,1)S(1)} copy-done((bf16[2560,256]{1,0:T(8,128)(2,1)S(1)}, bf16[2560,256]{1,0:T(8,128)(2,1)}, u32[]{:S(2)}) %copy-start.1) | copy-done | bytes 1310744
  12.9 3.7 %collective-permute-done.3.bottom.refs_5_ = bf16[32,2560]{1,0:T(8,128)(2,1)S(1)} collective-permute-done((bf16[32,2560]{1,0:T(8,128)(2,1)S(1)}, bf16[32,2560]{1,0:T(8,128)(2,1)S(1)}, u32[]{:S(2)}, u32[]{:S(2)}) %collective-permute-start.3) | collective-permute-done | bytes 163872 | tf_op jit(solution)/shard_map/ppermute | solution.py:26
  16.6 6.4 %collective-permute-start.4 = (bf16[16,2560]{1,0:T(8,128)(2,1)S(1)}, bf16[16,2560]{1,0:T(8,128)(2,1)S(1)}, u32[]{:S(2)}, u32[]{:S(2)}) collective-permute-start(bf16[16,2560]{1,0:T(8,128)(2,1)S(1)} %tail.1), channel_id=1, source_target_pairs={{0,4},{4,8},{8,12},{12,16},{16,20},{20,24},{24,28},{28,32},{32,36}... | collective-permute-start | bytes 245768 | tf_op jit(solution)/shard_map/ppermute | solution.py:53
  23.1 1.4 %collective-permute-done.4.refs_6_ = bf16[16,2560]{1,0:T(8,128)(2,1)S(1)} collective-permute-done((bf16[16,2560]{1,0:T(8,128)(2,1)S(1)}, bf16[16,2560]{1,0:T(8,128)(2,1)S(1)}, u32[]{:S(2)}, u32[]{:S(2)}) %collective-permute-start.4) | collective-permute-done | bytes 81952 | tf_op jit(solution)/shard_map/ppermute | solution.py:53
  24.5 0.0 slice-start.1
  24.5 8.1 %block.1 = (bf16[256,2560]{1,0:T(8,128)(2,1)S(1)}, bf16[32,8,768]{2,1,0:T(8,128)(2,1)S(1)}, bf16[256,1280]{1,0:T(8,128)(2,1)S(1)}, bf16[256,1280]{1,0:T(8,128)(2...) custom-call(s32[1,64]{1,0:T(1,128)S(1)} %bitcast.10, ...), custom_call_target="tpu_custom_call" | custom-call | tf_op jit(solution)/shard_map/block/pallas_call | solution.py:423
  32.7 3.6 %inside.1 = (f32[256,1280]{1,0:T(8,128)S(1)}, f32[256,1280]{1,0:T(8,128)S(1)}) custom-call(bf16[256,2560]{1,0:T(8,128)(2,1)S(1)} %get-tuple-element.26.refs_0_, bf16[256,1280]{1,0:T(8,128)(2,1)S(1)} %get-tuple-element.27.refs_1_, bf16[256,1280]{1,0:T(8,128)(2,1)S(1)} %get-tuple-element.28.refs_2_, bf16[256,128]{1,0:T(8,128)(2,1)S(1)} %get-tuple-element.29.refs_3_, ...), custom_call_target="tpu_custom_call" | custom-call | tf_op jit(solution)/shard_map/inside/pallas_call | solution.py:461
  36.3 18.4 %all_to_all.10.refs_0_ = bf16[32,8,768]{2,1,0:T(8,128)(2,1)S(1)} all-to-all(bf16[32,8,768]{2,1,0:T(8,128)(2,1)S(1)} %get-tuple-element.34), channel_id=1, replica_groups=mesh['seq'=32,'head'=4] {'seq'}, dimensions={0} | all-to-all | bytes 786432 | tf_op jit(solution)/shard_map/all_to_all | solution.py:472
  54.7 0.3 scan.1
  55.0 13.0 %all_to_all.11.refs_0_ = bf16[32,8,640]{2,1,0:T(8,128)(2,1)S(1)} all-to-all(bf16[32,8,640]{2,1,0:T(8,128)(2,1)S(1)} %scan.1), channel_id=1, replica_groups=mesh['seq'=32,'head'=4] {'seq'}, dimensions={0} | all-to-all | bytes 655360 | tf_op jit(solution)/shard_map/all_to_all | solution.py:482
  67.9 2.4 %out.1 = (bf16[64,2688]{1,0:T(8,128)(2,1)S(1)}, bf16[64,2688]{1,0:T(8,128)(2,1)S(1)}, bf16[32,2688]{1,0:T(8,128)(2,1)S(1)}, bf16[32,2688]{1,0:T(8,128)(2,1)S(1)}, bf16[64,2688]{1,0:T(8,128)(2,1)S(1)}) custom-call(bf16[32,8,640]{2,1,0:T(8,128)(2,1)S(1)} %all_to_all.11.refs_0_, bf16[256,128]{1,0:T(8,128)(2,1)S(1)} %get-tuple-element.35.refs_1_, ...), custom_call_target="tpu_custom_call" | custom-call | tf_op jit(solution)/shard_map/out/pallas_call | solution.py:486
  70.3 0.7 collective-permute-start.5
  71.0 2.8 %collective-permute-start.8 = (bf16[64,2688]{1,0:T(8,128)(2,1)S(1)}, bf16[64,2688]{1,0:T(8,128)(2,1)S(1)}, u32[]{:S(2)}, u32[]{:S(2)}) collective-permute-start(bf16[64,2688]{1,0:T(8,128)(2,1)S(1)} %get-tuple-element.44), channel_id=1, source_target_pairs={{0,3},{1,0},{2,1},{3,2},{4,7},{5,4},{6,5},{7,6},{8,11},{9,8},{10,9... | collective-permute-start | bytes 1032200 | tf_op jit(solution)/shard_map/ppermute | solution.py:26
  73.7 1.1 %collective-permute-start.6 = (bf16[32,2688]{1,0:T(8,128)(2,1)S(1)}, bf16[32,2688]{1,0:T(8,128)(2,1)S(1)}, u32[]{:S(2)}, u32[]{:S(2)}) collective-permute-start(bf16[32,2688]{1,0:T(8,128)(2,1)S(1)} %get-tuple-element.42), channel_id=1, source_target_pairs={{0,2},{1,3},{2,0},{3,1},{4,6},{5,7},{6,4},{7,5},{8,10},{9,11},{10,... | collective-permute-start | bytes 516104 | tf_op jit(solution)/shard_map/ppermute | solution.py:26
  74.8 1.9 %collective-permute-start.7 = (bf16[32,2688]{1,0:T(8,128)(2,1)S(1)}, bf16[32,2688]{1,0:T(8,128)(2,1)S(1)}, u32[]{:S(2)}, u32[]{:S(2)}) collective-permute-start(bf16[32,2688]{1,0:T(8,128)(2,1)S(1)} %get-tuple-element.43), channel_id=1, source_target_pairs={{0,2},{1,3},{2,0},{3,1},{4,6},{5,7},{6,4},{7,5},{8,10},{9,11},{10,... | collective-permute-start | bytes 516104 | tf_op jit(solution)/shard_map/ppermute | solution.py:26
  76.7 10.0 %collective-permute-done.6.two = bf16[32,2688]{1,0:T(8,128)(2,1)S(1)} collective-permute-done((bf16[32,2688]{1,0:T(8,128)(2,1)S(1)}, bf16[32,2688]{1,0:T(8,128)(2,1)S(1)}, u32[]{:S(2)}, u32[]{:S(2)}) %collective-permute-start.6) | collective-permute-done | bytes 172064 | tf_op jit(solution)/shard_map/ppermute | solution.py:26
  86.7 3.7 %collective-permute-done.7.two_b = bf16[32,2688]{1,0:T(8,128)(2,1)S(1)} collective-permute-done((bf16[32,2688]{1,0:T(8,128)(2,1)S(1)}, bf16[32,2688]{1,0:T(8,128)(2,1)S(1)}, u32[]{:S(2)}, u32[]{:S(2)}) %collective-permute-start.7) | collective-permute-done | bytes 172064 | tf_op jit(solution)/shard_map/ppermute | solution.py:26
  90.4 1.0 %close.1 = bf16[64,2560]{1,0:T(8,128)(2,1)} custom-call(bf16[64,2688]{1,0:T(8,128)(2,1)S(1)} %get-tuple-element.40.own, bf16[64,2688]{1,0:T(8,128)(2,1)S(1)} %collective-permute-done.5.one, bf16[32,2688]{1,0:T(8,128)(2,1)S(1)} %collective-permute-done.6.two, bf16[32,2688]{1,0:T(8,128)(2,1)S(1)} %collective-permute-done.7.two_b, ...), custom_call_target="tpu_custom_call" | custom-call | tf_op jit(solution)/shard_map/close/pallas_call | solution.py:498
  (40 shorter events, 0.1 us)
Async XLA Ops:
  0.0 16.6 %collective-permute-start = (bf16[64,2560]{1,0:T(8,128)(2,1)}, bf16[64,2560]{1,0:T(8,128)(2,1)S(1)}, u32[]{:S(2)}, u32[]{:S(2)}) collective-permute-start(bf16[64,2560]{1,0:T(8,128)(2,1)} %refs_1_.1), channel_id=1, source_target_pairs={{0,1},{1,2},{2,3},{3,0},{4,5},{5,6},{6,7},{7,4},{8,9},{9,10},{10,1... | collective-permute-start | bytes 983048 | tf_op jit(solution)/shard_map/ppermute | solution.py:26
  2.5 14.1 %collective-permute-start.1 = (bf16[64,2560]{1,0:T(8,128)(2,1)}, bf16[64,2560]{1,0:T(8,128)(2,1)S(1)}, u32[]{:S(2)}, u32[]{:S(2)}) collective-permute-start(bf16[64,2560]{1,0:T(8,128)(2,1)} %refs_1_.1), channel_id=1, source_target_pairs={{0,3},{1,0},{2,1},{3,2},{4,7},{5,4},{6,5},{7,6},{8,11},{9,8},{10,9... | collective-permute-start | bytes 983048 | tf_op jit(solution)/shard_map/ppermute | solution.py:26
  5.6 11.0 %collective-permute-start.3 = (bf16[32,2560]{1,0:T(8,128)(2,1)S(1)}, bf16[32,2560]{1,0:T(8,128)(2,1)S(1)}, u32[]{:S(2)}, u32[]{:S(2)}) collective-permute-start(bf16[32,2560]{1,0:T(8,128)(2,1)S(1)} %get-tuple-element.45), channel_id=1, source_target_pairs={{0,2},{1,3},{2,0},{3,1},{4,6},{5,7},{6,4},{7,5},{8,10},{9,11},{10,... | collective-permute-start | bytes 491528 | tf_op jit(solution)/shard_map/ppermute | solution.py:26
  7.0 16.1 %collective-permute-start.2 = (bf16[32,2560]{1,0:T(8,128)(2,1)S(1)}, bf16[32,2560]{1,0:T(8,128)(2,1)S(1)}, u32[]{:S(2)}, u32[]{:S(2)}) collective-permute-start(bf16[32,2560]{1,0:T(8,128)(2,1)S(1)} %get-tuple-element.46), channel_id=1, source_target_pairs={{0,2},{1,3},{2,0},{3,1},{4,6},{5,7},{6,4},{7,5},{8,10},{9,11},{10,... | collective-permute-start | bytes 491528 | tf_op jit(solution)/shard_map/ppermute | solution.py:26
  8.7 2.9 %copy-start = (bf16[2560,1280]{1,0:T(8,128)(2,1)S(1)}, bf16[2560,1280]{1,0:T(8,128)(2,1)}, u32[]{:S(2)}) copy-start(bf16[2560,1280]{1,0:T(8,128)(2,1)} %refs_14_.1) | copy-start | bytes 19660804
  12.8 3.8 %copy-start.2 = (bf16[64,2560]{1,0:T(8,128)(2,1)S(1)}, bf16[64,2560]{1,0:T(8,128)(2,1)}, u32[]{:S(2)}) copy-start(bf16[64,2560]{1,0:T(8,128)(2,1)} %refs_1_.1) | copy-start | bytes 983044
  12.8 10.2 %copy-start.10 = (f32[2560]{0:T(1024)S(1)}, f32[2560]{0:T(1024)}, u32[]{:S(2)}) copy-start(f32[2560]{0:T(1024)} %param.15) | copy-start | bytes 30724
  12.8 10.2 %copy-start.11 = (f32[1280]{0:T(1024)S(1)}, f32[1280]{0:T(1024)}, u32[]{:S(2)}) copy-start(f32[1280]{0:T(1024)} %param.25) | copy-start | bytes 15364
  12.8 11.6 %copy-start.4 = (f32[4,1280]{1,0:T(4,128)S(1)}, f32[4,1280]{1,0:T(4,128)}, u32[]{:S(2)}) copy-start(f32[4,1280]{1,0:T(4,128)} %refs_12_.1) | copy-start | bytes 61444
  12.8 11.6 %copy-start.5 = (f32[4,256]{1,0:T(4,128)S(1)}, f32[4,256]{1,0:T(4,128)}, u32[]{:S(2)}) copy-start(f32[4,256]{1,0:T(4,128)} %refs_11_.1) | copy-start | bytes 12292
  12.9 11.6 %copy-start.6 = (s32[64]{0:T(128)S(1)}, s32[64]{0:T(128)}, u32[]{:S(2)}) copy-start(s32[64]{0:T(128)} %param.27) | copy-start | bytes 772
  12.9 11.6 %copy-start.7 = (f32[20]{0:T(128)S(1)}, f32[20]{0:T(128)}, u32[]{:S(2)}) copy-start(f32[20]{0:T(128)} %param.20) | copy-start | bytes 244
  12.9 11.6 %copy-start.8 = (s32[20]{0:T(128)S(1)}, s32[20]{0:T(128)}, u32[]{:S(2)}) copy-start(s32[20]{0:T(128)} %param.21) | copy-start | bytes 244
  12.9 19.7 %slice-start = ((s8[6553600]{0:T(1024)(128)(4,1)}), s8[4194304]{0:T(1024)(128)(4,1)S(1)}, s32[]{:S(2)}) async-start(s8[6553600]{0:T(1024)(128)(4,1)} %bitcast.5), calls=%async_computation.2 | async-start | bytes 8388608
  12.9 11.6 %copy-start.3 = (bf16[2560,20]{0,1:T(8,128)(2,1)S(1)}, bf16[2560,20]{0,1:T(8,128)(2,1)}, u32[]{:S(2)}) copy-start(bf16[2560,20]{0,1:T(8,128)(2,1)} %param.19) | copy-start | bytes 307204
  16.6 7.8 %collective-permute-start.4 = (bf16[16,2560]{1,0:T(8,128)(2,1)S(1)}, bf16[16,2560]{1,0:T(8,128)(2,1)S(1)}, u32[]{:S(2)}, u32[]{:S(2)}) collective-permute-start(bf16[16,2560]{1,0:T(8,128)(2,1)S(1)} %tail.1), channel_id=1, source_target_pairs={{0,4},{4,8},{8,12},{12,16},{16,20},{20,24},{24,28},{28,32},{32,36}... | collective-permute-start | bytes 245768 | tf_op jit(solution)/shard_map/ppermute | solution.py:53
  24.5 8.1 %slice-start.1 = ((s8[6553600]{0:T(1024)(128)(4,1)}), s8[2359296]{0:T(1024)(128)(4,1)S(1)}, s32[]{:S(2)}) async-start(s8[6553600]{0:T(1024)(128)(4,1)} %bitcast.5), calls=%async_computation.3 | async-start | bytes 4718592
  24.5 8.1 %copy-start.9 = (f32[20]{0:T(128)S(1)}, f32[20]{0:T(128)}, u32[]{:S(2)}) copy-start(f32[20]{0:T(128)} %param.24) | copy-start | bytes 244
  32.6 35.3 %slice-start.2 = ((s8[6553600]{0:T(1024)(128)(4,1)}), s8[4194304]{0:T(1024)(128)(4,1)S(1)}, s32[]{:S(2)}) async-start(s8[6553600]{0:T(1024)(128)(4,1)} %bitcast.7), calls=%async_computation.4 | async-start | bytes 8388608
  32.7 35.3 %slice-start.3 = ((s8[6553600]{0:T(1024)(128)(4,1)}), s8[2359296]{0:T(1024)(128)(4,1)S(1)}, s32[]{:S(2)}) async-start(s8[6553600]{0:T(1024)(128)(4,1)} %bitcast.7), calls=%async_computation.5 | async-start | bytes 4718592
  70.3 20.1 %collective-permute-start.5 = (bf16[64,2688]{1,0:T(8,128)(2,1)S(1)}, bf16[64,2688]{1,0:T(8,128)(2,1)S(1)}, u32[]{:S(2)}, u32[]{:S(2)}) collective-permute-start(bf16[64,2688]{1,0:T(8,128)(2,1)S(1)} %get-tuple-element.41), channel_id=1, source_target_pairs={{0,1},{1,2},{2,3},{3,0},{4,5},{5,6},{6,7},{7,4},{8,9},{9,10},{10,1... | collective-permute-start | bytes 1032200 | tf_op jit(solution)/shard_map/ppermute | solution.py:26
  71.0 19.5 %collective-permute-start.8 = (bf16[64,2688]{1,0:T(8,128)(2,1)S(1)}, bf16[64,2688]{1,0:T(8,128)(2,1)S(1)}, u32[]{:S(2)}, u32[]{:S(2)}) collective-permute-start(bf16[64,2688]{1,0:T(8,128)(2,1)S(1)} %get-tuple-element.44), channel_id=1, source_target_pairs={{0,3},{1,0},{2,1},{3,2},{4,7},{5,4},{6,5},{7,6},{8,11},{9,8},{10,9... | collective-permute-start | bytes 1032200 | tf_op jit(solution)/shard_map/ppermute | solution.py:26
  73.7 13.0 %collective-permute-start.6 = (bf16[32,2688]{1,0:T(8,128)(2,1)S(1)}, bf16[32,2688]{1,0:T(8,128)(2,1)S(1)}, u32[]{:S(2)}, u32[]{:S(2)}) collective-permute-start(bf16[32,2688]{1,0:T(8,128)(2,1)S(1)} %get-tuple-element.42), channel_id=1, source_target_pairs={{0,2},{1,3},{2,0},{3,1},{4,6},{5,7},{6,4},{7,5},{8,10},{9,11},{10,... | collective-permute-start | bytes 516104 | tf_op jit(solution)/shard_map/ppermute | solution.py:26
  74.8 15.6 %collective-permute-start.7 = (bf16[32,2688]{1,0:T(8,128)(2,1)S(1)}, bf16[32,2688]{1,0:T(8,128)(2,1)S(1)}, u32[]{:S(2)}, u32[]{:S(2)}) collective-permute-start(bf16[32,2688]{1,0:T(8,128)(2,1)S(1)} %get-tuple-element.43), channel_id=1, source_target_pairs={{0,2},{1,3},{2,0},{3,1},{4,6},{5,7},{6,4},{7,5},{8,10},{9,11},{10,... | collective-permute-start | bytes 516104 | tf_op jit(solution)/shard_map/ppermute | solution.py:26
  (1 other events, 1.3 us)

commit v5 on v4

--- a/solution.py
+++ b/solution.py
@@ -29,29 +29,38 @@
 def gather_tokens(tokens, inner_weight, state_weight):
     heads = lax.axis_size("head")
     blocks = lax.axis_size("seq")
-    half = tokens.shape[0] // 2
-    bottom = around(tokens[half:], "head", 2)
+    rows, width = tokens.shape
+    half = rows // 2
     below = around(tokens, "head", 1)
     above = around(tokens, "head", heads - 1)
+    bottom = around(tokens[half:], "head", 2)
     top = around(tokens[:half], "head", 2)
+    last = heads - 1
+    far = [(s * heads + last, (s + 1) * heads + 1) for s in range(blocks - 1)]
+    rim_far = lax.ppermute(tokens[rows - RIM :], ("seq", "head"), far)
     (near,) = call(
         near_kernel,
         "near",
         [vmem()] * 2,
-        [jax.ShapeDtypeStruct((16, LANES), tokens.dtype)],
+        [jax.ShapeDtypeStruct((RIM, LANES), tokens.dtype)],
         [],
         BLOCK_LIMIT,
     )(inner_weight, state_weight)
     (tail,) = call(
         tail_kernel,
         "tail",
-        [vmem()] * 5,
-        [jax.ShapeDtypeStruct((RIM, tokens.shape[1]), tokens.dtype)],
+        [vmem()] * 4,
+        [jax.ShapeDtypeStruct((RIM, width), tokens.dtype)],
         [],
         SMALL_LIMIT,
-    )(below, bottom, above, tokens, near)
-    rim = lax.ppermute(tail, "seq", [(s, s + 1) for s in range(blocks - 1)])
-    return below, above, top, bottom, rim
+    )(below, above, tokens, near)
+    route = [
+        (s * heads + h, (s + 1) * heads + h)
+        for s in range(blocks - 1)
+        for h in range(heads)
+        if h != 1
+    ]
+    return below, above, top, bottom, lax.ppermute(tail, ("seq", "head"), route), rim_far
 
 
 def split3(x):
@@ -86,15 +95,13 @@
 
 
 def near_kernel(inner_w, state_w, near):
-    near[...] = inner_w[0:16, 0:LANES] + state_w[0:16, 0:LANES]
-
-
-def tail_kernel(below, bottom, above, own, near, tail):
+    near[...] = inner_w[0:RIM, 0:LANES] + state_w[0:RIM, 0:LANES]
+
+
+def tail_kernel(below, above, own, near, tail):
     here = lax.axis_index("head")
-    last = [x[x.shape[0] - RIM :, :] for x in (below, bottom, above, own)]
-    low = jnp.where(here == 0, last[0], last[1])
-    high = jnp.where(here == 2, last[2], last[3])
-    tail[...] = jnp.where(here < 2, low, high)
+    last = [x[x.shape[0] - RIM :, :] for x in (below, above, own)]
+    tail[...] = jnp.where(here == 0, last[0], jnp.where(here == 2, last[1], last[2]))
 
 
 def repeat_lanes(x):
@@ -114,6 +121,7 @@
     top,
     bottom,
     rim,
+    rim_far,
     gain,
     step_w,
     step_bias,
@@ -157,7 +165,7 @@
     far = (here + 2) % 4
     put(far, 0, top[...])
     put(far, half, bottom[...])
-    normed[0:RIM, :] = norm(rim[...])
+    normed[0:RIM, :] = norm(rim[...] + rim_far[...])
     normed_out[...] = normed[RIM:, :]
 
     passages = lens_row.shape[1]
@@ -415,7 +423,7 @@
     length = heads * rows
     passages = passage_lengths.shape[0]
     span = channels // 2
-    below, above, top, bottom, rim = gather_tokens(tokens, inner_weight, state_weight)
+    below, above, top, bottom, rim, rim_far = gather_tokens(tokens, inner_weight, state_weight)
 
     def shape(dims, kind):
         return jax.ShapeDtypeStruct(dims, kind)
@@ -423,7 +431,7 @@
     normed, sent, conv, scaled, cum, cum_rows, scores, maps, head_decay = call(
         lambda *refs: block_kernel(*refs, heads_here=heads_here),
         "block",
-        [vmem()] * 15,
+        [vmem()] * 16,
         [
             shape((length, width), BF16),
             shape((blocks, 8, span + LANES), BF16),
@@ -448,6 +456,7 @@
         top,
         bottom,
         rim,
+        rim_far,
         input_gain[None],
         step_weight.T,
         step_bias[None],

time: 91.7 us -> 91.8 us (level)
  waiting for transfers between devices: 18.8 us -> 15.1 us
  starting transfers between devices: 20.4 us -> 22.3 us
  local copies, waits for them, and re-layouts: 5.28 us -> 7.02 us
    ppermute x8, waiting for transfers between devices: 17.4 us -> 13.7 us  [around(): lax.ppermute(block, axis, [(i, (i + distance) % size) for i in range(size)])]
    ppermute x1 -> x2, starting transfers between devices: 6.36 us -> 8.26 us  [the longest x1 7.61 us: gather_tokens(): lax.ppermute(tail, ('seq', 'head'), route)]
  transfers between devices with their start and end apart: 9 -> 10, of which waited for: 4 -> 3; matrix products, arithmetic and copies ran while one was open for 1% -> 2% of each run, Pallas kernels for 0% -> 0%
where the time goes in v5:
time: 91.8 us; the launch traced here: 91.4 us
  blocking collectives  31.4 us (34%)
  starting transfers between devices  22.3 us (24%)
  Pallas kernels  15.3 us (17%)
  waiting for transfers between devices  15.1 us (16%)
  local copies, waits for them, and re-layouts  7.02 us (8%)
    all_to_all x1, blocking collectives, on_device(): got = lax.all_to_all(sent, 'seq', 0, 0, tiled=True)  18.4 us
    ppermute x8, starting transfers between devices, around(): lax.ppermute(block, axis, [(i, (i + distance) % size) for i in range(size)])  14 us
    ppermute x8, waiting for transfers between devices, around(): lax.ppermute(block, axis, [(i, (i + distance) % size) for i in range(size)])  13.7 us
    all_to_all x1, blocking collectives, on_device(): states = lax.all_to_all(back, 'seq', 0, 0, tiled=True)  13 us
    pallas_call x1, Pallas kernels, on_device(): call(lambda *refs: block_kernel(*refs, heads_here=heads_here), 'block', [...  8.07 us
    ppermute x1, starting transfers between devices, gather_tokens(): lax.ppermute(tail, ('seq', 'head'), route)  7.61 us
    unnamed x32, local copies, waits for them, and re-layouts  5.1 us
    pallas_call x1, Pallas kernels, on_device(): call(lambda *refs: inside_kernel(*refs, heads_here=heads_here), 'inside',...  3.6 us
  transfers between devices with their start and end apart: 10, of which 3 were waited for; matrix products, arithmetic and copies ran while one was open for 2% of the time, Pallas kernels for 0%

profile of v5, /device:TPU:1, one launch (start us, length us, event | category | flops | bytes accessed | tf_op | source)
XLA Modules:
  0.0 91.4 jit_solution(16365338758249480295)
XLA Ops:
  0.0 2.5 %collective-permute-start = (bf16[64,2560]{1,0:T(8,128)(2,1)}, bf16[64,2560]{1,0:T(8,128)(2,1)S(1)}, u32[]{:S(2)}, u32[]{:S(2)}) collective-permute-start(bf16[64,2560]{1,0:T(8,128)(2,1)} %refs_1_.1), channel_id=1, source_target_pairs={{0,1},{1,2},{2,3},{3,0},{4,5},{5,6},{6,7},{7,4},{8,9},{9,10},{10,1... | collective-permute-start | bytes 983048 | tf_op jit(solution)/shard_map/ppermute | solution.py:26
  2.5 2.1 %collective-permute-start.1 = (bf16[64,2560]{1,0:T(8,128)(2,1)}, bf16[64,2560]{1,0:T(8,128)(2,1)S(1)}, u32[]{:S(2)}, u32[]{:S(2)}) collective-permute-start(bf16[64,2560]{1,0:T(8,128)(2,1)} %refs_1_.1), channel_id=1, source_target_pairs={{0,3},{1,0},{2,1},{3,2},{4,7},{5,4},{6,5},{7,6},{8,11},{9,8},{10,9... | collective-permute-start | bytes 983048 | tf_op jit(solution)/shard_map/ppermute | solution.py:26
  4.6 1.0 %fusion = (bf16[32,2560]{1,0:T(8,128)(2,1)S(1)}, bf16[32,2560]{1,0:T(8,128)(2,1)S(1)}) fusion(bf16[64,2560]{1,0:T(8,128)(2,1)} %refs_1_.1), kind=kLoop, calls=%fused_computation | loop fusion | bytes 655360 | tf_op jit(solution)/shard_map/slice | solution.py:36
  5.6 1.4 %collective-permute-start.2 = (bf16[32,2560]{1,0:T(8,128)(2,1)S(1)}, bf16[32,2560]{1,0:T(8,128)(2,1)S(1)}, u32[]{:S(2)}, u32[]{:S(2)}) collective-permute-start(bf16[32,2560]{1,0:T(8,128)(2,1)S(1)} %get-tuple-element.46), channel_id=1, source_target_pairs={{0,2},{1,3},{2,0},{3,1},{4,6},{5,7},{6,4},{7,5},{8,10},{9,11},{10,... | collective-permute-start | bytes 491528 | tf_op jit(solution)/shard_map/ppermute | solution.py:26
  7.0 1.7 %collective-permute-start.3 = (bf16[32,2560]{1,0:T(8,128)(2,1)S(1)}, bf16[32,2560]{1,0:T(8,128)(2,1)S(1)}, u32[]{:S(2)}, u32[]{:S(2)}) collective-permute-start(bf16[32,2560]{1,0:T(8,128)(2,1)S(1)} %get-tuple-element.45), channel_id=1, source_target_pairs={{0,2},{1,3},{2,0},{3,1},{4,6},{5,7},{6,4},{7,5},{8,10},{9,11},{10,... | collective-permute-start | bytes 491528 | tf_op jit(solution)/shard_map/ppermute | solution.py:26
  8.7 0.9 slice.11
  9.6 0.7 collective-permute-start.5
  10.2 2.9 %copy-done = bf16[2560,1280]{1,0:T(8,128)(2,1)S(1)} copy-done((bf16[2560,1280]{1,0:T(8,128)(2,1)S(1)}, bf16[2560,1280]{1,0:T(8,128)(2,1)}, u32[]{:S(2)}) %copy-start) | copy-done | bytes 6553624
  13.1 1.3 %copy-done.1 = bf16[2560,256]{1,0:T(8,128)(2,1)S(1)} copy-done((bf16[2560,256]{1,0:T(8,128)(2,1)S(1)}, bf16[2560,256]{1,0:T(8,128)(2,1)}, u32[]{:S(2)}) %copy-start.1) | copy-done | bytes 1310744
  14.5 0.9 copy-done.2
  15.4 7.6 %collective-permute-start.4 = (bf16[16,2560]{1,0:T(8,128)(2,1)S(1)}, bf16[16,2560]{1,0:T(8,128)(2,1)S(1)}, u32[]{:S(2)}, u32[]{:S(2)}) collective-permute-start(bf16[16,2560]{1,0:T(8,128)(2,1)S(1)} %tail.1), channel_id=1, source_target_pairs={{0,4},{2,6},{3,7},{4,8},{6,10},{7,11},{8,12},{10,14},{11,15},{12,1... | collective-permute-start | bytes 245768 | tf_op jit(solution)/shard_map/ppermute | solution.py:63
  23.1 1.4 %collective-permute-done.4.refs_6_ = bf16[16,2560]{1,0:T(8,128)(2,1)S(1)} collective-permute-done((bf16[16,2560]{1,0:T(8,128)(2,1)S(1)}, bf16[16,2560]{1,0:T(8,128)(2,1)S(1)}, u32[]{:S(2)}, u32[]{:S(2)}) %collective-permute-start.4) | collective-permute-done | bytes 81952 | tf_op jit(solution)/shard_map/ppermute | solution.py:63
  24.5 8.1 %block.1 = (bf16[256,2560]{1,0:T(8,128)(2,1)S(1)}, bf16[32,8,768]{2,1,0:T(8,128)(2,1)S(1)}, bf16[256,1280]{1,0:T(8,128)(2,1)S(1)}, bf16[256,1280]{1,0:T(8,128)(2...) custom-call(s32[1,64]{1,0:T(1,128)S(1)} %bitcast.10, ...), custom_call_target="tpu_custom_call" | custom-call | tf_op jit(solution)/shard_map/block/pallas_call | solution.py:431
  32.7 3.6 %inside.1 = (f32[256,1280]{1,0:T(8,128)S(1)}, f32[256,1280]{1,0:T(8,128)S(1)}) custom-call(bf16[256,2560]{1,0:T(8,128)(2,1)S(1)} %get-tuple-element.26.refs_0_, bf16[256,1280]{1,0:T(8,128)(2,1)S(1)} %get-tuple-element.27.refs_1_, bf16[256,1280]{1,0:T(8,128)(2,1)S(1)} %get-tuple-element.28.refs_2_, bf16[256,128]{1,0:T(8,128)(2,1)S(1)} %get-tuple-element.29.refs_3_, ...), custom_call_target="tpu_custom_call" | custom-call | tf_op jit(solution)/shard_map/inside/pallas_call | solution.py:470
  36.3 18.4 %all_to_all.10.refs_0_ = bf16[32,8,768]{2,1,0:T(8,128)(2,1)S(1)} all-to-all(bf16[32,8,768]{2,1,0:T(8,128)(2,1)S(1)} %get-tuple-element.34), channel_id=1, replica_groups=mesh['seq'=32,'head'=4] {'seq'}, dimensions={0} | all-to-all | bytes 786432 | tf_op jit(solution)/shard_map/all_to_all | solution.py:481
  54.7 0.3 scan.1
  55.0 13.0 %all_to_all.11.refs_0_ = bf16[32,8,640]{2,1,0:T(8,128)(2,1)S(1)} all-to-all(bf16[32,8,640]{2,1,0:T(8,128)(2,1)S(1)} %scan.1), channel_id=1, replica_groups=mesh['seq'=32,'head'=4] {'seq'}, dimensions={0} | all-to-all | bytes 655360 | tf_op jit(solution)/shard_map/all_to_all | solution.py:491
  67.9 2.4 %out.1 = (bf16[64,2688]{1,0:T(8,128)(2,1)S(1)}, bf16[64,2688]{1,0:T(8,128)(2,1)S(1)}, bf16[32,2688]{1,0:T(8,128)(2,1)S(1)}, bf16[32,2688]{1,0:T(8,128)(2,1)S(1)}, bf16[64,2688]{1,0:T(8,128)(2,1)S(1)}) custom-call(bf16[32,8,640]{2,1,0:T(8,128)(2,1)S(1)} %all_to_all.11.refs_0_, bf16[256,128]{1,0:T(8,128)(2,1)S(1)} %get-tuple-element.35.refs_1_, ...), custom_call_target="tpu_custom_call" | custom-call | tf_op jit(solution)/shard_map/out/pallas_call | solution.py:495
  70.4 3.3 %collective-permute-start.9 = (bf16[64,2688]{1,0:T(8,128)(2,1)S(1)}, bf16[64,2688]{1,0:T(8,128)(2,1)S(1)}, u32[]{:S(2)}, u32[]{:S(2)}) collective-permute-start(bf16[64,2688]{1,0:T(8,128)(2,1)S(1)} %get-tuple-element.44), channel_id=1, source_target_pairs={{0,3},{1,0},{2,1},{3,2},{4,7},{5,4},{6,5},{7,6},{8,11},{9,8},{10,9... | collective-permute-start | bytes 1032200 | tf_op jit(solution)/shard_map/ppermute | solution.py:26
  73.7 1.1 %collective-permute-start.7 = (bf16[32,2688]{1,0:T(8,128)(2,1)S(1)}, bf16[32,2688]{1,0:T(8,128)(2,1)S(1)}, u32[]{:S(2)}, u32[]{:S(2)}) collective-permute-start(bf16[32,2688]{1,0:T(8,128)(2,1)S(1)} %get-tuple-element.42), channel_id=1, source_target_pairs={{0,2},{1,3},{2,0},{3,1},{4,6},{5,7},{6,4},{7,5},{8,10},{9,11},{10,... | collective-permute-start | bytes 516104 | tf_op jit(solution)/shard_map/ppermute | solution.py:26
  74.8 1.9 %collective-permute-start.8 = (bf16[32,2688]{1,0:T(8,128)(2,1)S(1)}, bf16[32,2688]{1,0:T(8,128)(2,1)S(1)}, u32[]{:S(2)}, u32[]{:S(2)}) collective-permute-start(bf16[32,2688]{1,0:T(8,128)(2,1)S(1)} %get-tuple-element.43), channel_id=1, source_target_pairs={{0,2},{1,3},{2,0},{3,1},{4,6},{5,7},{6,4},{7,5},{8,10},{9,11},{10,... | collective-permute-start | bytes 516104 | tf_op jit(solution)/shard_map/ppermute | solution.py:26
  76.7 10.0 %collective-permute-done.7.two = bf16[32,2688]{1,0:T(8,128)(2,1)S(1)} collective-permute-done((bf16[32,2688]{1,0:T(8,128)(2,1)S(1)}, bf16[32,2688]{1,0:T(8,128)(2,1)S(1)}, u32[]{:S(2)}, u32[]{:S(2)}) %collective-permute-start.7) | collective-permute-done | bytes 172064 | tf_op jit(solution)/shard_map/ppermute | solution.py:26
  86.7 3.7 %collective-permute-done.8.two_b = bf16[32,2688]{1,0:T(8,128)(2,1)S(1)} collective-permute-done((bf16[32,2688]{1,0:T(8,128)(2,1)S(1)}, bf16[32,2688]{1,0:T(8,128)(2,1)S(1)}, u32[]{:S(2)}, u32[]{:S(2)}) %collective-permute-start.8) | collective-permute-done | bytes 172064 | tf_op jit(solution)/shard_map/ppermute | solution.py:26
  90.4 1.0 %close.1 = bf16[64,2560]{1,0:T(8,128)(2,1)} custom-call(bf16[64,2688]{1,0:T(8,128)(2,1)S(1)} %get-tuple-element.40.own, bf16[64,2688]{1,0:T(8,128)(2,1)S(1)} %collective-permute-done.6.one, bf16[32,2688]{1,0:T(8,128)(2,1)S(1)} %collective-permute-done.7.two, bf16[32,2688]{1,0:T(8,128)(2,1)S(1)} %collective-permute-done.8.two_b, ...), custom_call_target="tpu_custom_call" | custom-call | tf_op jit(solution)/shard_map/close/pallas_call | solution.py:507
  (43 shorter events, 0.2 us)
Async XLA Ops:
  0.0 14.5 %collective-permute-start = (bf16[64,2560]{1,0:T(8,128)(2,1)}, bf16[64,2560]{1,0:T(8,128)(2,1)S(1)}, u32[]{:S(2)}, u32[]{:S(2)}) collective-permute-start(bf16[64,2560]{1,0:T(8,128)(2,1)} %refs_1_.1), channel_id=1, source_target_pairs={{0,1},{1,2},{2,3},{3,0},{4,5},{5,6},{6,7},{7,4},{8,9},{9,10},{10,1... | collective-permute-start | bytes 983048 | tf_op jit(solution)/shard_map/ppermute | solution.py:26
  2.5 12.0 %collective-permute-start.1 = (bf16[64,2560]{1,0:T(8,128)(2,1)}, bf16[64,2560]{1,0:T(8,128)(2,1)S(1)}, u32[]{:S(2)}, u32[]{:S(2)}) collective-permute-start(bf16[64,2560]{1,0:T(8,128)(2,1)} %refs_1_.1), channel_id=1, source_target_pairs={{0,3},{1,0},{2,1},{3,2},{4,7},{5,4},{6,5},{7,6},{8,11},{9,8},{10,9... | collective-permute-start | bytes 983048 | tf_op jit(solution)/shard_map/ppermute | solution.py:26
  5.6 17.5 %collective-permute-start.2 = (bf16[32,2560]{1,0:T(8,128)(2,1)S(1)}, bf16[32,2560]{1,0:T(8,128)(2,1)S(1)}, u32[]{:S(2)}, u32[]{:S(2)}) collective-permute-start(bf16[32,2560]{1,0:T(8,128)(2,1)S(1)} %get-tuple-element.46), channel_id=1, source_target_pairs={{0,2},{1,3},{2,0},{3,1},{4,6},{5,7},{6,4},{7,5},{8,10},{9,11},{10,... | collective-permute-start | bytes 491528 | tf_op jit(solution)/shard_map/ppermute | solution.py:26
  7.0 16.1 %collective-permute-start.3 = (bf16[32,2560]{1,0:T(8,128)(2,1)S(1)}, bf16[32,2560]{1,0:T(8,128)(2,1)S(1)}, u32[]{:S(2)}, u32[]{:S(2)}) collective-permute-start(bf16[32,2560]{1,0:T(8,128)(2,1)S(1)} %get-tuple-element.45), channel_id=1, source_target_pairs={{0,2},{1,3},{2,0},{3,1},{4,6},{5,7},{6,4},{7,5},{8,10},{9,11},{10,... | collective-permute-start | bytes 491528 | tf_op jit(solution)/shard_map/ppermute | solution.py:26
  9.6 13.5 %collective-permute-start.5 = (bf16[16,2560]{1,0:T(8,128)(2,1)S(1)}, bf16[16,2560]{1,0:T(8,128)(2,1)S(1)}, u32[]{:S(2)}, u32[]{:S(2)}) collective-permute-start(bf16[16,2560]{1,0:T(8,128)(2,1)S(1)} %slice.11), channel_id=1, source_target_pairs={{3,5},{7,9},{11,13},{15,17},{19,21},{23,25},{27,29},{31,33},{35,37... | collective-permute-start | bytes 245768 | tf_op jit(solution)/shard_map/ppermute | solution.py:40
  10.2 2.9 %copy-start = (bf16[2560,1280]{1,0:T(8,128)(2,1)S(1)}, bf16[2560,1280]{1,0:T(8,128)(2,1)}, u32[]{:S(2)}) copy-start(bf16[2560,1280]{1,0:T(8,128)(2,1)} %refs_15_.1) | copy-start | bytes 19660804
  14.4 8.6 %copy-start.10 = (f32[2560]{0:T(1024)S(1)}, f32[2560]{0:T(1024)}, u32[]{:S(2)}) copy-start(f32[2560]{0:T(1024)} %param.15) | copy-start | bytes 30724
  14.4 8.6 %copy-start.11 = (f32[1280]{0:T(1024)S(1)}, f32[1280]{0:T(1024)}, u32[]{:S(2)}) copy-start(f32[1280]{0:T(1024)} %param.25) | copy-start | bytes 15364
  14.4 10.1 %copy-start.3 = (bf16[2560,20]{0,1:T(8,128)(2,1)S(1)}, bf16[2560,20]{0,1:T(8,128)(2,1)}, u32[]{:S(2)}) copy-start(bf16[2560,20]{0,1:T(8,128)(2,1)} %param.19) | copy-start | bytes 307204
  14.4 10.1 %copy-start.4 = (f32[4,1280]{1,0:T(4,128)S(1)}, f32[4,1280]{1,0:T(4,128)}, u32[]{:S(2)}) copy-start(f32[4,1280]{1,0:T(4,128)} %refs_13_.1) | copy-start | bytes 61444
  14.4 10.1 %copy-start.5 = (f32[4,256]{1,0:T(4,128)S(1)}, f32[4,256]{1,0:T(4,128)}, u32[]{:S(2)}) copy-start(f32[4,256]{1,0:T(4,128)} %refs_12_.1) | copy-start | bytes 12292
  14.4 10.1 %copy-start.6 = (s32[64]{0:T(128)S(1)}, s32[64]{0:T(128)}, u32[]{:S(2)}) copy-start(s32[64]{0:T(128)} %param.27) | copy-start | bytes 772
  14.4 10.0 %copy-start.7 = (f32[20]{0:T(128)S(1)}, f32[20]{0:T(128)}, u32[]{:S(2)}) copy-start(f32[20]{0:T(128)} %param.20) | copy-start | bytes 244
  14.5 10.0 %copy-start.8 = (s32[20]{0:T(128)S(1)}, s32[20]{0:T(128)}, u32[]{:S(2)}) copy-start(s32[20]{0:T(128)} %param.21) | copy-start | bytes 244
  14.5 18.2 %slice-start = ((s8[6553600]{0:T(1024)(128)(4,1)}), s8[4194304]{0:T(1024)(128)(4,1)S(1)}, s32[]{:S(2)}) async-start(s8[6553600]{0:T(1024)(128)(4,1)} %bitcast.5), calls=%async_computation.2 | async-start | bytes 8388608
  15.4 9.1 %collective-permute-start.4 = (bf16[16,2560]{1,0:T(8,128)(2,1)S(1)}, bf16[16,2560]{1,0:T(8,128)(2,1)S(1)}, u32[]{:S(2)}, u32[]{:S(2)}) collective-permute-start(bf16[16,2560]{1,0:T(8,128)(2,1)S(1)} %tail.1), channel_id=1, source_target_pairs={{0,4},{2,6},{3,7},{4,8},{6,10},{7,11},{8,12},{10,14},{11,15},{12,1... | collective-permute-start | bytes 245768 | tf_op jit(solution)/shard_map/ppermute | solution.py:63
  24.5 8.1 %slice-start.1 = ((s8[6553600]{0:T(1024)(128)(4,1)}), s8[2359296]{0:T(1024)(128)(4,1)S(1)}, s32[]{:S(2)}) async-start(s8[6553600]{0:T(1024)(128)(4,1)} %bitcast.5), calls=%async_computation.3 | async-start | bytes 4718592
  24.5 8.1 %copy-start.9 = (f32[20]{0:T(128)S(1)}, f32[20]{0:T(128)}, u32[]{:S(2)}) copy-start(f32[20]{0:T(128)} %param.24) | copy-start | bytes 244
  32.6 35.3 %slice-start.2 = ((s8[6553600]{0:T(1024)(128)(4,1)}), s8[4194304]{0:T(1024)(128)(4,1)S(1)}, s32[]{:S(2)}) async-start(s8[6553600]{0:T(1024)(128)(4,1)} %bitcast.7), calls=%async_computation.4 | async-start | bytes 8388608
  32.7 35.3 %slice-start.3 = ((s8[6553600]{0:T(1024)(128)(4,1)}), s8[2359296]{0:T(1024)(128)(4,1)S(1)}, s32[]{:S(2)}) async-start(s8[6553600]{0:T(1024)(128)(4,1)} %bitcast.7), calls=%async_computation.5 | async-start | bytes 4718592
  70.3 20.1 %collective-permute-start.6 = (bf16[64,2688]{1,0:T(8,128)(2,1)S(1)}, bf16[64,2688]{1,0:T(8,128)(2,1)S(1)}, u32[]{:S(2)}, u32[]{:S(2)}) collective-permute-start(bf16[64,2688]{1,0:T(8,128)(2,1)S(1)} %get-tuple-element.41), channel_id=1, source_target_pairs={{0,1},{1,2},{2,3},{3,0},{4,5},{5,6},{6,7},{7,4},{8,9},{9,10},{10,1... | collective-permute-start | bytes 1032200 | tf_op jit(solution)/shard_map/ppermute | solution.py:26
  70.4 20.0 %collective-permute-start.9 = (bf16[64,2688]{1,0:T(8,128)(2,1)S(1)}, bf16[64,2688]{1,0:T(8,128)(2,1)S(1)}, u32[]{:S(2)}, u32[]{:S(2)}) collective-permute-start(bf16[64,2688]{1,0:T(8,128)(2,1)S(1)} %get-tuple-element.44), channel_id=1, source_target_pairs={{0,3},{1,0},{2,1},{3,2},{4,7},{5,4},{6,5},{7,6},{8,11},{9,8},{10,9... | collective-permute-start | bytes 1032200 | tf_op jit(solution)/shard_map/ppermute | solution.py:26
  73.7 13.0 %collective-permute-start.7 = (bf16[32,2688]{1,0:T(8,128)(2,1)S(1)}, bf16[32,2688]{1,0:T(8,128)(2,1)S(1)}, u32[]{:S(2)}, u32[]{:S(2)}) collective-permute-start(bf16[32,2688]{1,0:T(8,128)(2,1)S(1)} %get-tuple-element.42), channel_id=1, source_target_pairs={{0,2},{1,3},{2,0},{3,1},{4,6},{5,7},{6,4},{7,5},{8,10},{9,11},{10,... | collective-permute-start | bytes 516104 | tf_op jit(solution)/shard_map/ppermute | solution.py:26
  74.8 15.6 %collective-permute-start.8 = (bf16[32,2688]{1,0:T(8,128)(2,1)S(1)}, bf16[32,2688]{1,0:T(8,128)(2,1)S(1)}, u32[]{:S(2)}, u32[]{:S(2)}) collective-permute-start(bf16[32,2688]{1,0:T(8,128)(2,1)S(1)} %get-tuple-element.43), channel_id=1, source_target_pairs={{0,2},{1,3},{2,0},{3,1},{4,6},{5,7},{6,4},{7,5},{8,10},{9,11},{10,... | collective-permute-start | bytes 516104 | tf_op jit(solution)/shard_map/ppermute | solution.py:26
  (2 other events, 2.3 us)

commit v6 on v5

--- a/solution.py
+++ b/solution.py
@@ -232,16 +232,14 @@
     cum_out[...] = by_lane(cum, heads_here)
     cum_rows[...] = cum.T
 
-    for c in range(local.shape[1] // CHUNK):
-        cols = slice(c * CHUNK, (c + 1) * CHUNK)
-        raw = dot(normed[...], inner_w[:, cols]).astype(BF16).astype(F32)
-        mixed = conv(raw, taps_inner[:, cols])
-        conv_out[:, cols] = mixed
-        spread = spread_matrix(c * (CHUNK // P_SIZE), CHUNK, heads_here)
-        scaled = (mixed.astype(F32) * dot(step3, spread)).astype(BF16)
-        scaled_out[:, cols] = scaled
-        tail_in = (dot(tail3, spread) * scaled.astype(F32)).astype(BF16)
-        local[:, cols] = dot(maps_in_t, tail_in)
+    raw = dot(normed[...], inner_w[...]).astype(BF16).astype(F32)
+    mixed = conv(raw, taps_inner[...])
+    conv_out[...] = mixed
+    spread = spread_matrix(0, local.shape[1], heads_here)
+    scaled = (mixed.astype(F32) * dot(step3, spread)).astype(BF16)
+    scaled_out[...] = scaled
+    tail_in = (dot(tail3, spread) * scaled.astype(F32)).astype(BF16)
+    local[...] = dot(maps_in_t, tail_in)
 
     span = local.shape[1] // 2
     decay = jnp.broadcast_to(keep3[length - RIM :].astype(F32)[RIM - 1 :], (8, LANES))

time: 91.8 us -> 89.4 us (0.974)
  Pallas kernels: 15.3 us -> 13 us
    pallas_call x1, Pallas kernels: 8.07 us -> 5.75 us  [on_device(): call(lambda *refs: block_kernel(*refs, heads_here=heads_here), 'block', [...]
where the time goes in v6:
time: 89.4 us; the launch traced here: 89.1 us
  blocking collectives  31.4 us (35%)
  starting transfers between devices  22.3 us (25%)
  waiting for transfers between devices  15.1 us (17%)
  Pallas kernels  13 us (15%)
  local copies, waits for them, and re-layouts  7.02 us (8%)
    all_to_all x1, blocking collectives, on_device(): got = lax.all_to_all(sent, 'seq', 0, 0, tiled=True)  18.4 us
    ppermute x8, starting transfers between devices, around(): lax.ppermute(block, axis, [(i, (i + distance) % size) for i in range(size)])  14 us
    ppermute x8, waiting for transfers between devices, around(): lax.ppermute(block, axis, [(i, (i + distance) % size) for i in range(size)])  13.7 us
    all_to_all x1, blocking collectives, on_device(): states = lax.all_to_all(back, 'seq', 0, 0, tiled=True)  13 us
    ppermute x1, starting transfers between devices, gather_tokens(): lax.ppermute(tail, ('seq', 'head'), route)  7.61 us
    pallas_call x1, Pallas kernels, on_device(): call(lambda *refs: block_kernel(*refs, heads_here=heads_here), 'block', [...  5.75 us
    unnamed x32, local copies, waits for them, and re-layouts  5.1 us
    pallas_call x1, Pallas kernels, on_device(): call(lambda *refs: inside_kernel(*refs, heads_here=heads_here), 'inside',...  3.61 us
  transfers between devices with their start and end apart: 10, of which 3 were waited for; matrix products, arithmetic and copies ran while one was open for 2% of the time, Pallas kernels for 0%

profile of v6, /device:TPU:1, one launch (start us, length us, event | category | flops | bytes accessed | tf_op | source)
XLA Modules:
  0.0 89.1 jit_solution(17663946982877632915)
XLA Ops:
  0.0 2.5 %collective-permute-start = (bf16[64,2560]{1,0:T(8,128)(2,1)}, bf16[64,2560]{1,0:T(8,128)(2,1)S(1)}, u32[]{:S(2)}, u32[]{:S(2)}) collective-permute-start(bf16[64,2560]{1,0:T(8,128)(2,1)} %refs_1_.1), channel_id=1, source_target_pairs={{0,1},{1,2},{2,3},{3,0},{4,5},{5,6},{6,7},{7,4},{8,9},{9,10},{10,1... | collective-permute-start | bytes 983048 | tf_op jit(solution)/shard_map/ppermute | solution.py:26
  2.5 2.1 %collective-permute-start.1 = (bf16[64,2560]{1,0:T(8,128)(2,1)}, bf16[64,2560]{1,0:T(8,128)(2,1)S(1)}, u32[]{:S(2)}, u32[]{:S(2)}) collective-permute-start(bf16[64,2560]{1,0:T(8,128)(2,1)} %refs_1_.1), channel_id=1, source_target_pairs={{0,3},{1,0},{2,1},{3,2},{4,7},{5,4},{6,5},{7,6},{8,11},{9,8},{10,9... | collective-permute-start | bytes 983048 | tf_op jit(solution)/shard_map/ppermute | solution.py:26
  4.6 1.0 %fusion = (bf16[32,2560]{1,0:T(8,128)(2,1)S(1)}, bf16[32,2560]{1,0:T(8,128)(2,1)S(1)}) fusion(bf16[64,2560]{1,0:T(8,128)(2,1)} %refs_1_.1), kind=kLoop, calls=%fused_computation | loop fusion | bytes 655360 | tf_op jit(solution)/shard_map/slice | solution.py:36
  5.6 1.4 %collective-permute-start.2 = (bf16[32,2560]{1,0:T(8,128)(2,1)S(1)}, bf16[32,2560]{1,0:T(8,128)(2,1)S(1)}, u32[]{:S(2)}, u32[]{:S(2)}) collective-permute-start(bf16[32,2560]{1,0:T(8,128)(2,1)S(1)} %get-tuple-element.46), channel_id=1, source_target_pairs={{0,2},{1,3},{2,0},{3,1},{4,6},{5,7},{6,4},{7,5},{8,10},{9,11},{10,... | collective-permute-start | bytes 491528 | tf_op jit(solution)/shard_map/ppermute | solution.py:26
  7.0 1.7 %collective-permute-start.3 = (bf16[32,2560]{1,0:T(8,128)(2,1)S(1)}, bf16[32,2560]{1,0:T(8,128)(2,1)S(1)}, u32[]{:S(2)}, u32[]{:S(2)}) collective-permute-start(bf16[32,2560]{1,0:T(8,128)(2,1)S(1)} %get-tuple-element.45), channel_id=1, source_target_pairs={{0,2},{1,3},{2,0},{3,1},{4,6},{5,7},{6,4},{7,5},{8,10},{9,11},{10,... | collective-permute-start | bytes 491528 | tf_op jit(solution)/shard_map/ppermute | solution.py:26
  8.7 0.9 %slice.11 = bf16[16,2560]{1,0:T(8,128)(2,1)S(1)} slice(bf16[64,2560]{1,0:T(8,128)(2,1)} %refs_1_.1), slice={[48:64], [0:2560]} | slice | bytes 163840 | tf_op jit(solution)/shard_map/slice | solution.py:40
  9.6 0.7 collective-permute-start.5
  10.2 2.9 %copy-done = bf16[2560,1280]{1,0:T(8,128)(2,1)S(1)} copy-done((bf16[2560,1280]{1,0:T(8,128)(2,1)S(1)}, bf16[2560,1280]{1,0:T(8,128)(2,1)}, u32[]{:S(2)}) %copy-start) | copy-done | bytes 6553624
  13.1 1.3 %copy-done.1 = bf16[2560,256]{1,0:T(8,128)(2,1)S(1)} copy-done((bf16[2560,256]{1,0:T(8,128)(2,1)S(1)}, bf16[2560,256]{1,0:T(8,128)(2,1)}, u32[]{:S(2)}) %copy-start.1) | copy-done | bytes 1310744
  14.5 0.9 copy-done.2
  15.4 7.6 %collective-permute-start.4 = (bf16[16,2560]{1,0:T(8,128)(2,1)S(1)}, bf16[16,2560]{1,0:T(8,128)(2,1)S(1)}, u32[]{:S(2)}, u32[]{:S(2)}) collective-permute-start(bf16[16,2560]{1,0:T(8,128)(2,1)S(1)} %tail.1), channel_id=1, source_target_pairs={{0,4},{2,6},{3,7},{4,8},{6,10},{7,11},{8,12},{10,14},{11,15},{12,1... | collective-permute-start | bytes 245768 | tf_op jit(solution)/shard_map/ppermute | solution.py:63
  23.1 1.4 %collective-permute-done.4.refs_6_ = bf16[16,2560]{1,0:T(8,128)(2,1)S(1)} collective-permute-done((bf16[16,2560]{1,0:T(8,128)(2,1)S(1)}, bf16[16,2560]{1,0:T(8,128)(2,1)S(1)}, u32[]{:S(2)}, u32[]{:S(2)}) %collective-permute-start.4) | collective-permute-done | bytes 81952 | tf_op jit(solution)/shard_map/ppermute | solution.py:63
  24.5 5.8 %block.1 = (bf16[256,2560]{1,0:T(8,128)(2,1)S(1)}, bf16[32,8,768]{2,1,0:T(8,128)(2,1)S(1)}, bf16[256,1280]{1,0:T(8,128)(2,1)S(1)}, bf16[256,1280]{1,0:T(8,128)(2...) custom-call(s32[1,64]{1,0:T(1,128)S(1)} %bitcast.10, ...), custom_call_target="tpu_custom_call" | custom-call | tf_op jit(solution)/shard_map/block/pallas_call | solution.py:429
  30.4 3.6 %inside.1 = (f32[256,1280]{1,0:T(8,128)S(1)}, f32[256,1280]{1,0:T(8,128)S(1)}) custom-call(bf16[256,2560]{1,0:T(8,128)(2,1)S(1)} %get-tuple-element.26.refs_0_, bf16[256,1280]{1,0:T(8,128)(2,1)S(1)} %get-tuple-element.27.refs_1_, bf16[256,1280]{1,0:T(8,128)(2,1)S(1)} %get-tuple-element.28.refs_2_, bf16[256,128]{1,0:T(8,128)(2,1)S(1)} %get-tuple-element.29.refs_3_, ...), custom_call_target="tpu_custom_call" | custom-call | tf_op jit(solution)/shard_map/inside/pallas_call | solution.py:468
  34.0 18.4 %all_to_all.10.refs_0_ = bf16[32,8,768]{2,1,0:T(8,128)(2,1)S(1)} all-to-all(bf16[32,8,768]{2,1,0:T(8,128)(2,1)S(1)} %get-tuple-element.34), channel_id=1, replica_groups=mesh['seq'=32,'head'=4] {'seq'}, dimensions={0} | all-to-all | bytes 786432 | tf_op jit(solution)/shard_map/all_to_all | solution.py:479
  52.4 0.3 scan.1
  52.6 13.0 %all_to_all.11.refs_0_ = bf16[32,8,640]{2,1,0:T(8,128)(2,1)S(1)} all-to-all(bf16[32,8,640]{2,1,0:T(8,128)(2,1)S(1)} %scan.1), channel_id=1, replica_groups=mesh['seq'=32,'head'=4] {'seq'}, dimensions={0} | all-to-all | bytes 655360 | tf_op jit(solution)/shard_map/all_to_all | solution.py:489
  65.6 2.4 %out.1 = (bf16[64,2688]{1,0:T(8,128)(2,1)S(1)}, bf16[64,2688]{1,0:T(8,128)(2,1)S(1)}, bf16[32,2688]{1,0:T(8,128)(2,1)S(1)}, bf16[32,2688]{1,0:T(8,128)(2,1)S(1)}, bf16[64,2688]{1,0:T(8,128)(2,1)S(1)}) custom-call(bf16[32,8,640]{2,1,0:T(8,128)(2,1)S(1)} %all_to_all.11.refs_0_, bf16[256,128]{1,0:T(8,128)(2,1)S(1)} %get-tuple-element.35.refs_1_, ...), custom_call_target="tpu_custom_call" | custom-call | tf_op jit(solution)/shard_map/out/pallas_call | solution.py:493
  68.1 3.3 %collective-permute-start.9 = (bf16[64,2688]{1,0:T(8,128)(2,1)S(1)}, bf16[64,2688]{1,0:T(8,128)(2,1)S(1)}, u32[]{:S(2)}, u32[]{:S(2)}) collective-permute-start(bf16[64,2688]{1,0:T(8,128)(2,1)S(1)} %get-tuple-element.44), channel_id=1, source_target_pairs={{0,3},{1,0},{2,1},{3,2},{4,7},{5,4},{6,5},{7,6},{8,11},{9,8},{10,9... | collective-permute-start | bytes 1032200 | tf_op jit(solution)/shard_map/ppermute | solution.py:26
  71.4 1.1 %collective-permute-start.7 = (bf16[32,2688]{1,0:T(8,128)(2,1)S(1)}, bf16[32,2688]{1,0:T(8,128)(2,1)S(1)}, u32[]{:S(2)}, u32[]{:S(2)}) collective-permute-start(bf16[32,2688]{1,0:T(8,128)(2,1)S(1)} %get-tuple-element.42), channel_id=1, source_target_pairs={{0,2},{1,3},{2,0},{3,1},{4,6},{5,7},{6,4},{7,5},{8,10},{9,11},{10,... | collective-permute-start | bytes 516104 | tf_op jit(solution)/shard_map/ppermute | solution.py:26
  72.5 1.9 %collective-permute-start.8 = (bf16[32,2688]{1,0:T(8,128)(2,1)S(1)}, bf16[32,2688]{1,0:T(8,128)(2,1)S(1)}, u32[]{:S(2)}, u32[]{:S(2)}) collective-permute-start(bf16[32,2688]{1,0:T(8,128)(2,1)S(1)} %get-tuple-element.43), channel_id=1, source_target_pairs={{0,2},{1,3},{2,0},{3,1},{4,6},{5,7},{6,4},{7,5},{8,10},{9,11},{10,... | collective-permute-start | bytes 516104 | tf_op jit(solution)/shard_map/ppermute | solution.py:26
  74.4 10.0 %collective-permute-done.7.two = bf16[32,2688]{1,0:T(8,128)(2,1)S(1)} collective-permute-done((bf16[32,2688]{1,0:T(8,128)(2,1)S(1)}, bf16[32,2688]{1,0:T(8,128)(2,1)S(1)}, u32[]{:S(2)}, u32[]{:S(2)}) %collective-permute-start.7) | collective-permute-done | bytes 172064 | tf_op jit(solution)/shard_map/ppermute | solution.py:26
  84.4 3.7 %collective-permute-done.8.two_b = bf16[32,2688]{1,0:T(8,128)(2,1)S(1)} collective-permute-done((bf16[32,2688]{1,0:T(8,128)(2,1)S(1)}, bf16[32,2688]{1,0:T(8,128)(2,1)S(1)}, u32[]{:S(2)}, u32[]{:S(2)}) %collective-permute-start.8) | collective-permute-done | bytes 172064 | tf_op jit(solution)/shard_map/ppermute | solution.py:26
  88.1 1.0 %close.1 = bf16[64,2560]{1,0:T(8,128)(2,1)} custom-call(bf16[64,2688]{1,0:T(8,128)(2,1)S(1)} %get-tuple-element.40.own, bf16[64,2688]{1,0:T(8,128)(2,1)S(1)} %collective-permute-done.6.one, bf16[32,2688]{1,0:T(8,128)(2,1)S(1)} %collective-permute-done.7.two, bf16[32,2688]{1,0:T(8,128)(2,1)S(1)} %collective-permute-done.8.two_b, ...), custom_call_target="tpu_custom_call" | custom-call | tf_op jit(solution)/shard_map/close/pallas_call | solution.py:505
  (43 shorter events, 0.2 us)
Async XLA Ops:
  0.0 14.5 %collective-permute-start = (bf16[64,2560]{1,0:T(8,128)(2,1)}, bf16[64,2560]{1,0:T(8,128)(2,1)S(1)}, u32[]{:S(2)}, u32[]{:S(2)}) collective-permute-start(bf16[64,2560]{1,0:T(8,128)(2,1)} %refs_1_.1), channel_id=1, source_target_pairs={{0,1},{1,2},{2,3},{3,0},{4,5},{5,6},{6,7},{7,4},{8,9},{9,10},{10,1... | collective-permute-start | bytes 983048 | tf_op jit(solution)/shard_map/ppermute | solution.py:26
  2.5 12.0 %collective-permute-start.1 = (bf16[64,2560]{1,0:T(8,128)(2,1)}, bf16[64,2560]{1,0:T(8,128)(2,1)S(1)}, u32[]{:S(2)}, u32[]{:S(2)}) collective-permute-start(bf16[64,2560]{1,0:T(8,128)(2,1)} %refs_1_.1), channel_id=1, source_target_pairs={{0,3},{1,0},{2,1},{3,2},{4,7},{5,4},{6,5},{7,6},{8,11},{9,8},{10,9... | collective-permute-start | bytes 983048 | tf_op jit(solution)/shard_map/ppermute | solution.py:26
  5.6 17.5 %collective-permute-start.2 = (bf16[32,2560]{1,0:T(8,128)(2,1)S(1)}, bf16[32,2560]{1,0:T(8,128)(2,1)S(1)}, u32[]{:S(2)}, u32[]{:S(2)}) collective-permute-start(bf16[32,2560]{1,0:T(8,128)(2,1)S(1)} %get-tuple-element.46), channel_id=1, source_target_pairs={{0,2},{1,3},{2,0},{3,1},{4,6},{5,7},{6,4},{7,5},{8,10},{9,11},{10,... | collective-permute-start | bytes 491528 | tf_op jit(solution)/shard_map/ppermute | solution.py:26
  7.0 16.1 %collective-permute-start.3 = (bf16[32,2560]{1,0:T(8,128)(2,1)S(1)}, bf16[32,2560]{1,0:T(8,128)(2,1)S(1)}, u32[]{:S(2)}, u32[]{:S(2)}) collective-permute-start(bf16[32,2560]{1,0:T(8,128)(2,1)S(1)} %get-tuple-element.45), channel_id=1, source_target_pairs={{0,2},{1,3},{2,0},{3,1},{4,6},{5,7},{6,4},{7,5},{8,10},{9,11},{10,... | collective-permute-start | bytes 491528 | tf_op jit(solution)/shard_map/ppermute | solution.py:26
  9.6 13.5 %collective-permute-start.5 = (bf16[16,2560]{1,0:T(8,128)(2,1)S(1)}, bf16[16,2560]{1,0:T(8,128)(2,1)S(1)}, u32[]{:S(2)}, u32[]{:S(2)}) collective-permute-start(bf16[16,2560]{1,0:T(8,128)(2,1)S(1)} %slice.11), channel_id=1, source_target_pairs={{3,5},{7,9},{11,13},{15,17},{19,21},{23,25},{27,29},{31,33},{35,37... | collective-permute-start | bytes 245768 | tf_op jit(solution)/shard_map/ppermute | solution.py:40
  10.2 2.9 %copy-start = (bf16[2560,1280]{1,0:T(8,128)(2,1)S(1)}, bf16[2560,1280]{1,0:T(8,128)(2,1)}, u32[]{:S(2)}) copy-start(bf16[2560,1280]{1,0:T(8,128)(2,1)} %refs_15_.1) | copy-start | bytes 19660804
  14.4 8.6 %copy-start.10 = (f32[2560]{0:T(1024)S(1)}, f32[2560]{0:T(1024)}, u32[]{:S(2)}) copy-start(f32[2560]{0:T(1024)} %param.15) | copy-start | bytes 30724
  14.4 8.6 %copy-start.11 = (f32[1280]{0:T(1024)S(1)}, f32[1280]{0:T(1024)}, u32[]{:S(2)}) copy-start(f32[1280]{0:T(1024)} %param.25) | copy-start | bytes 15364
  14.4 10.1 %copy-start.3 = (bf16[2560,20]{0,1:T(8,128)(2,1)S(1)}, bf16[2560,20]{0,1:T(8,128)(2,1)}, u32[]{:S(2)}) copy-start(bf16[2560,20]{0,1:T(8,128)(2,1)} %param.19) | copy-start | bytes 307204
  14.4 10.1 %copy-start.4 = (f32[4,1280]{1,0:T(4,128)S(1)}, f32[4,1280]{1,0:T(4,128)}, u32[]{:S(2)}) copy-start(f32[4,1280]{1,0:T(4,128)} %refs_13_.1) | copy-start | bytes 61444
  14.4 10.1 %copy-start.5 = (f32[4,256]{1,0:T(4,128)S(1)}, f32[4,256]{1,0:T(4,128)}, u32[]{:S(2)}) copy-start(f32[4,256]{1,0:T(4,128)} %refs_12_.1) | copy-start | bytes 12292
  14.4 10.1 %copy-start.6 = (s32[64]{0:T(128)S(1)}, s32[64]{0:T(128)}, u32[]{:S(2)}) copy-start(s32[64]{0:T(128)} %param.27) | copy-start | bytes 772
  14.4 10.0 %copy-start.7 = (f32[20]{0:T(128)S(1)}, f32[20]{0:T(128)}, u32[]{:S(2)}) copy-start(f32[20]{0:T(128)} %param.20) | copy-start | bytes 244
  14.5 10.0 %copy-start.8 = (s32[20]{0:T(128)S(1)}, s32[20]{0:T(128)}, u32[]{:S(2)}) copy-start(s32[20]{0:T(128)} %param.21) | copy-start | bytes 244
  14.5 15.8 %slice-start = ((s8[6553600]{0:T(1024)(128)(4,1)}), s8[4194304]{0:T(1024)(128)(4,1)S(1)}, s32[]{:S(2)}) async-start(s8[6553600]{0:T(1024)(128)(4,1)} %bitcast.5), calls=%async_computation.2 | async-start | bytes 8388608
  15.4 9.1 %collective-permute-start.4 = (bf16[16,2560]{1,0:T(8,128)(2,1)S(1)}, bf16[16,2560]{1,0:T(8,128)(2,1)S(1)}, u32[]{:S(2)}, u32[]{:S(2)}) collective-permute-start(bf16[16,2560]{1,0:T(8,128)(2,1)S(1)} %tail.1), channel_id=1, source_target_pairs={{0,4},{2,6},{3,7},{4,8},{6,10},{7,11},{8,12},{10,14},{11,15},{12,1... | collective-permute-start | bytes 245768 | tf_op jit(solution)/shard_map/ppermute | solution.py:63
  24.5 5.8 %slice-start.1 = ((s8[6553600]{0:T(1024)(128)(4,1)}), s8[2359296]{0:T(1024)(128)(4,1)S(1)}, s32[]{:S(2)}) async-start(s8[6553600]{0:T(1024)(128)(4,1)} %bitcast.5), calls=%async_computation.3 | async-start | bytes 4718592
  24.5 5.8 %copy-start.9 = (f32[20]{0:T(128)S(1)}, f32[20]{0:T(128)}, u32[]{:S(2)}) copy-start(f32[20]{0:T(128)} %param.24) | copy-start | bytes 244
  30.3 35.3 %slice-start.2 = ((s8[6553600]{0:T(1024)(128)(4,1)}), s8[4194304]{0:T(1024)(128)(4,1)S(1)}, s32[]{:S(2)}) async-start(s8[6553600]{0:T(1024)(128)(4,1)} %bitcast.7), calls=%async_computation.4 | async-start | bytes 8388608
  30.3 35.3 %slice-start.3 = ((s8[6553600]{0:T(1024)(128)(4,1)}), s8[2359296]{0:T(1024)(128)(4,1)S(1)}, s32[]{:S(2)}) async-start(s8[6553600]{0:T(1024)(128)(4,1)} %bitcast.7), calls=%async_computation.5 | async-start | bytes 4718592
  68.0 20.1 %collective-permute-start.6 = (bf16[64,2688]{1,0:T(8,128)(2,1)S(1)}, bf16[64,2688]{1,0:T(8,128)(2,1)S(1)}, u32[]{:S(2)}, u32[]{:S(2)}) collective-permute-start(bf16[64,2688]{1,0:T(8,128)(2,1)S(1)} %get-tuple-element.41), channel_id=1, source_target_pairs={{0,1},{1,2},{2,3},{3,0},{4,5},{5,6},{6,7},{7,4},{8,9},{9,10},{10,1... | collective-permute-start | bytes 1032200 | tf_op jit(solution)/shard_map/ppermute | solution.py:26
  68.1 20.0 %collective-permute-start.9 = (bf16[64,2688]{1,0:T(8,128)(2,1)S(1)}, bf16[64,2688]{1,0:T(8,128)(2,1)S(1)}, u32[]{:S(2)}, u32[]{:S(2)}) collective-permute-start(bf16[64,2688]{1,0:T(8,128)(2,1)S(1)} %get-tuple-element.44), channel_id=1, source_target_pairs={{0,3},{1,0},{2,1},{3,2},{4,7},{5,4},{6,5},{7,6},{8,11},{9,8},{10,9... | collective-permute-start | bytes 1032200 | tf_op jit(solution)/shard_map/ppermute | solution.py:26
  71.4 13.0 %collective-permute-start.7 = (bf16[32,2688]{1,0:T(8,128)(2,1)S(1)}, bf16[32,2688]{1,0:T(8,128)(2,1)S(1)}, u32[]{:S(2)}, u32[]{:S(2)}) collective-permute-start(bf16[32,2688]{1,0:T(8,128)(2,1)S(1)} %get-tuple-element.42), channel_id=1, source_target_pairs={{0,2},{1,3},{2,0},{3,1},{4,6},{5,7},{6,4},{7,5},{8,10},{9,11},{10,... | collective-permute-start | bytes 516104 | tf_op jit(solution)/shard_map/ppermute | solution.py:26
  72.5 15.6 %collective-permute-start.8 = (bf16[32,2688]{1,0:T(8,128)(2,1)S(1)}, bf16[32,2688]{1,0:T(8,128)(2,1)S(1)}, u32[]{:S(2)}, u32[]{:S(2)}) collective-permute-start(bf16[32,2688]{1,0:T(8,128)(2,1)S(1)} %get-tuple-element.43), channel_id=1, source_target_pairs={{0,2},{1,3},{2,0},{3,1},{4,6},{5,7},{6,4},{7,5},{8,10},{9,11},{10,... | collective-permute-start | bytes 516104 | tf_op jit(solution)/shard_map/ppermute | solution.py:26
  (2 other events, 2.3 us)

commit v7 on v6

--- a/solution.py
+++ b/solution.py
@@ -31,13 +31,11 @@
     blocks = lax.axis_size("seq")
     rows, width = tokens.shape
     half = rows // 2
-    below = around(tokens, "head", 1)
-    above = around(tokens, "head", heads - 1)
-    bottom = around(tokens[half:], "head", 2)
-    top = around(tokens[:half], "head", 2)
+    first = tokens[:half]
+    low = [around(first, "head", distance) for distance in (1, heads - 1, 2)]
     last = heads - 1
-    far = [(s * heads + last, (s + 1) * heads + 1) for s in range(blocks - 1)]
-    rim_far = lax.ppermute(tokens[rows - RIM :], ("seq", "head"), far)
+    route = [(s * heads + last, (s + 1) * heads) for s in range(blocks - 1)]
+    rim = lax.ppermute(tokens[rows - RIM // 2 :], ("seq", "head"), route)
     (near,) = call(
         near_kernel,
         "near",
@@ -46,21 +44,16 @@
         [],
         BLOCK_LIMIT,
     )(inner_weight, state_weight)
-    (tail,) = call(
-        tail_kernel,
-        "tail",
-        [vmem()] * 4,
-        [jax.ShapeDtypeStruct((RIM, width), tokens.dtype)],
+    (second,) = call(
+        join_kernel,
+        "join",
+        [vmem()] * 2,
+        [jax.ShapeDtypeStruct((half + RIM // 2, width), tokens.dtype)],
         [],
         SMALL_LIMIT,
-    )(below, above, tokens, near)
-    route = [
-        (s * heads + h, (s + 1) * heads + h)
-        for s in range(blocks - 1)
-        for h in range(heads)
-        if h != 1
-    ]
-    return below, above, top, bottom, lax.ppermute(tail, ("seq", "head"), route), rim_far
+    )(tokens, rim)
+    high = [around(second, "head", distance) for distance in (1, heads - 1, 2)]
+    return low, high, rim, near
 
 
 def split3(x):
@@ -98,10 +91,10 @@
     near[...] = inner_w[0:RIM, 0:LANES] + state_w[0:RIM, 0:LANES]
 
 
-def tail_kernel(below, above, own, near, tail):
-    here = lax.axis_index("head")
-    last = [x[x.shape[0] - RIM :, :] for x in (below, above, own)]
-    tail[...] = jnp.where(here == 0, last[0], jnp.where(here == 2, last[1], last[2]))
+def join_kernel(own, rim, second):
+    half = own.shape[0] // 2
+    second[0:half, :] = own[half:, :]
+    second[half:, :] = rim[...]
 
 
 def repeat_lanes(x):
@@ -116,12 +109,14 @@
 def block_kernel(
     lens_row,
     own,
-    below,
-    above,
-    top,
-    bottom,
+    below_low,
+    above_low,
+    far_low,
+    below_high,
+    above_high,
+    far_high,
     rim,
-    rim_far,
+    near,
     gain,
     step_w,
     step_bias,
@@ -160,12 +155,18 @@
 
     half = rows // 2
     put(here, 0, own[...])
-    put((here + 3) % 4, 0, below[...])
-    put((here + 1) % 4, 0, above[...])
-    far = (here + 2) % 4
-    put(far, 0, top[...])
-    put(far, half, bottom[...])
-    normed[0:RIM, :] = norm(rim[...] + rim_far[...])
+    for step, low, high in (
+        (3, below_low, below_high),
+        (1, above_low, above_high),
+        (2, far_low, far_high),
+    ):
+        owner = (here + step) % 4
+        put(owner, 0, low[...])
+        put(owner, half, high[0:half, :])
+    tail = rim[...].astype(F32)
+    for high in (below_high, above_high, far_high):
+        tail = tail + high[half:, :].astype(F32)
+    normed[0:RIM, :] = norm(jnp.concatenate([jnp.zeros_like(tail), tail], axis=0))
     normed_out[...] = normed[RIM:, :]
 
     passages = lens_row.shape[1]
@@ -421,7 +422,7 @@
     length = heads * rows
     passages = passage_lengths.shape[0]
     span = channels // 2
-    below, above, top, bottom, rim, rim_far = gather_tokens(tokens, inner_weight, state_weight)
+    low, high, rim, near = gather_tokens(tokens, inner_weight, state_weight)
 
     def shape(dims, kind):
         return jax.ShapeDtypeStruct(dims, kind)
@@ -429,7 +430,7 @@
     normed, sent, conv, scaled, cum, cum_rows, scores, maps, head_decay = call(
         lambda *refs: block_kernel(*refs, heads_here=heads_here),
         "block",
-        [vmem()] * 16,
+        [vmem()] * 18,
         [
             shape((length, width), BF16),
             shape((blocks, 8, span + LANES), BF16),
@@ -449,12 +450,10 @@
     )(
         passage_lengths[None],
         tokens,
-        below,
-        above,
-        top,
-        bottom,
+        *low,
+        *high,
         rim,
-        rim_far,
+        near,
         input_gain[None],
         step_weight.T,
         step_bias[None],

time: 89.4 us -> 96.5 us (1.079)
  waiting for transfers between devices: 15.1 us -> 25.9 us
  starting transfers between devices: 22.3 us -> 16 us
  local copies, waits for them, and re-layouts: 7.02 us -> 8.33 us
  blocking collectives: 31.4 us -> 32.6 us
    ppermute x2 -> x1, starting transfers between devices: 8.26 us -> 1.28 us  [gather_tokens(): rim = lax.ppermute(tokens[rows - RIM // 2:], ('seq', 'head'), route)]
    ppermute x8 -> x10, waiting for transfers between devices: 13.7 us -> 20.6 us  [around(): lax.ppermute(block, axis, [(i, (i + distance) % size) for i in range(size)])]
    ppermute x2 -> x1, waiting for transfers between devices: 1.38 us -> 5.23 us  [gather_tokens(): rim = lax.ppermute(tokens[rows - RIM // 2:], ('seq', 'head'), route)]
    all_to_all x1, blocking collectives: 18.4 us -> 19.6 us  [on_device(): got = lax.all_to_all(sent, 'seq', 0, 0, tiled=True)]
    ppermute x8 -> x10, starting transfers between devices: 14 us -> 14.7 us  [around(): lax.ppermute(block, axis, [(i, (i + distance) % size) for i in range(size)])]
    unnamed x32 -> x30, local copies, waits for them, and re-layouts: 5.1 us -> 5.21 us
  transfers between devices with their start and end apart: 10 -> 11, of which waited for: 3 -> 5; matrix products, arithmetic and copies ran while one was open for 2% -> 2% of each run, Pallas kernels for 0% -> 0%
where the time goes in v7:
time: 96.5 us; the launch traced here: 96.1 us
  blocking collectives  32.6 us (34%)
  waiting for transfers between devices  25.9 us (27%)
  starting transfers between devices  16 us (17%)
  Pallas kernels  13.1 us (14%)
  local copies, waits for them, and re-layouts  8.33 us (9%)
    ppermute x10, waiting for transfers between devices, around(): lax.ppermute(block, axis, [(i, (i + distance) % size) for i in range(size)])  20.6 us
    all_to_all x1, blocking collectives, on_device(): got = lax.all_to_all(sent, 'seq', 0, 0, tiled=True)  19.6 us
    ppermute x10, starting transfers between devices, around(): lax.ppermute(block, axis, [(i, (i + distance) % size) for i in range(size)])  14.7 us
    all_to_all x1, blocking collectives, on_device(): states = lax.all_to_all(back, 'seq', 0, 0, tiled=True)  13 us
    pallas_call x1, Pallas kernels, on_device(): call(lambda *refs: block_kernel(*refs, heads_here=heads_here), 'block', [...  5.83 us
    ppermute x1, waiting for transfers between devices, gather_tokens(): rim = lax.ppermute(tokens[rows - RIM // 2:], ('seq', 'head'), route)  5.23 us
    unnamed x30, local copies, waits for them, and re-layouts  5.21 us
    pallas_call x1, Pallas kernels, on_device(): call(lambda *refs: inside_kernel(*refs, heads_here=heads_here), 'inside',...  3.58 us
  transfers between devices with their start and end apart: 11, of which 5 were waited for; matrix products, arithmetic and copies ran while one was open for 2% of the time, Pallas kernels for 0%

profile of v7, /device:TPU:1, one launch (start us, length us, event | category | flops | bytes accessed | tf_op | source)
XLA Modules:
  0.0 96.1 jit_solution(4960689657374177398)
XLA Ops:
  0.0 0.9 slice.6
  0.9 2.5 %collective-permute-start = (bf16[32,2560]{1,0:T(8,128)(2,1)S(1)}, bf16[32,2560]{1,0:T(8,128)(2,1)S(1)}, u32[]{:S(2)}, u32[]{:S(2)}) collective-permute-start(bf16[32,2560]{1,0:T(8,128)(2,1)S(1)} %slice.6), channel_id=1, source_target_pairs={{0,1},{1,2},{2,3},{3,0},{4,5},{5,6},{6,7},{7,4},{8,9},{9,10},{10,1... | collective-permute-start | bytes 491528 | tf_op jit(solution)/shard_map/ppermute | solution.py:26
  3.5 0.8 slice.7
  4.2 1.3 %collective-permute-start.3 = (bf16[8,2560]{1,0:T(8,128)(2,1)S(1)}, bf16[8,2560]{1,0:T(8,128)(2,1)S(1)}, u32[]{:S(2)}, u32[]{:S(2)}) collective-permute-start(bf16[8,2560]{1,0:T(8,128)(2,1)S(1)} %slice.7), channel_id=1, source_target_pairs={{3,4},{7,8},{11,12},{15,16},{19,20},{23,24},{27,28},{31,32},{35,36... | collective-permute-start | bytes 122888 | tf_op jit(solution)/shard_map/ppermute | solution.py:38
  5.5 5.2 %collective-permute-done.3.rim.refs_8_ = bf16[8,2560]{1,0:T(8,128)(2,1)S(1)} collective-permute-done((bf16[8,2560]{1,0:T(8,128)(2,1)S(1)}, bf16[8,2560]{1,0:T(8,128)(2,1)S(1)}, u32[]{:S(2)}, u32[]{:S(2)}) %collective-permute-start.3) | collective-permute-done | bytes 40992 | tf_op jit(solution)/shard_map/ppermute | solution.py:38
  10.8 1.0 %copy-done.4 = bf16[64,2560]{1,0:T(8,128)(2,1)S(1)} copy-done((bf16[64,2560]{1,0:T(8,128)(2,1)S(1)}, bf16[64,2560]{1,0:T(8,128)(2,1)}, u32[]{:S(2)}) %copy-start.4) | copy-done | bytes 327704
  11.8 2.7 %collective-permute-start.5 = (bf16[40,2560]{1,0:T(8,128)(2,1)S(1)}, bf16[40,2560]{1,0:T(8,128)(2,1)S(1)}, u32[]{:S(2)}, u32[]{:S(2)}) collective-permute-start(bf16[40,2560]{1,0:T(8,128)(2,1)S(1)} %join.1), channel_id=1, source_target_pairs={{0,3},{1,0},{2,1},{3,2},{4,7},{5,4},{6,5},{7,6},{8,11},{9,8},{10,9... | collective-permute-start | bytes 614408 | tf_op jit(solution)/shard_map/ppermute | solution.py:26
  14.5 1.3 %collective-permute-start.1 = (bf16[32,2560]{1,0:T(8,128)(2,1)S(1)}, bf16[32,2560]{1,0:T(8,128)(2,1)S(1)}, u32[]{:S(2)}, u32[]{:S(2)}) collective-permute-start(bf16[32,2560]{1,0:T(8,128)(2,1)S(1)} %slice.6), channel_id=1, source_target_pairs={{0,3},{1,0},{2,1},{3,2},{4,7},{5,4},{6,5},{7,6},{8,11},{9,8},{10,9... | collective-permute-start | bytes 491528 | tf_op jit(solution)/shard_map/ppermute | solution.py:26
  15.8 1.7 %collective-permute-start.2 = (bf16[32,2560]{1,0:T(8,128)(2,1)S(1)}, bf16[32,2560]{1,0:T(8,128)(2,1)S(1)}, u32[]{:S(2)}, u32[]{:S(2)}) collective-permute-start(bf16[32,2560]{1,0:T(8,128)(2,1)S(1)} %slice.6), channel_id=1, source_target_pairs={{0,2},{1,3},{2,0},{3,1},{4,6},{5,7},{6,4},{7,5},{8,10},{9,11},{10,... | collective-permute-start | bytes 491528 | tf_op jit(solution)/shard_map/ppermute | solution.py:26
  18.9 2.9 %copy-done = bf16[2560,1280]{1,0:T(8,128)(2,1)S(1)} copy-done((bf16[2560,1280]{1,0:T(8,128)(2,1)S(1)}, bf16[2560,1280]{1,0:T(8,128)(2,1)}, u32[]{:S(2)}) %copy-start) | copy-done | bytes 6553624
  21.8 1.3 %copy-done.3 = bf16[2560,256]{1,0:T(8,128)(2,1)S(1)} copy-done((bf16[2560,256]{1,0:T(8,128)(2,1)S(1)}, bf16[2560,256]{1,0:T(8,128)(2,1)}, u32[]{:S(2)}) %copy-start.3) | copy-done | bytes 1310744
  23.1 5.6 %collective-permute-done.1.refs_3_ = bf16[32,2560]{1,0:T(8,128)(2,1)S(1)} collective-permute-done((bf16[32,2560]{1,0:T(8,128)(2,1)S(1)}, bf16[32,2560]{1,0:T(8,128)(2,1)S(1)}, u32[]{:S(2)}, u32[]{:S(2)}) %collective-permute-start.1) | collective-permute-done | bytes 163872 | tf_op jit(solution)/shard_map/ppermute | solution.py:26
  28.9 5.8 %block.1 = (bf16[256,2560]{1,0:T(8,128)(2,1)S(1)}, bf16[32,8,768]{2,1,0:T(8,128)(2,1)S(1)}, bf16[256,1280]{1,0:T(8,128)(2,1)S(1)}, bf16[256,1280]{1,0:T(8,128)(2...) custom-call(s32[1,64]{1,0:T(1,128)S(1)} %bitcast.8, ...), custom_call_target="tpu_custom_call" | custom-call | tf_op jit(solution)/shard_map/block/pallas_call | solution.py:430
  34.8 3.6 %inside.1 = (f32[256,1280]{1,0:T(8,128)S(1)}, f32[256,1280]{1,0:T(8,128)S(1)}) custom-call(bf16[256,2560]{1,0:T(8,128)(2,1)S(1)} %get-tuple-element.26.refs_0_, bf16[256,1280]{1,0:T(8,128)(2,1)S(1)} %get-tuple-element.27.refs_1_, bf16[256,1280]{1,0:T(8,128)(2,1)S(1)} %get-tuple-element.28.refs_2_, bf16[256,128]{1,0:T(8,128)(2,1)S(1)} %get-tuple-element.29.refs_3_, ...), custom_call_target="tpu_custom_call" | custom-call | tf_op jit(solution)/shard_map/inside/pallas_call | solution.py:467
  38.4 19.6 %all_to_all.10.refs_0_ = bf16[32,8,768]{2,1,0:T(8,128)(2,1)S(1)} all-to-all(bf16[32,8,768]{2,1,0:T(8,128)(2,1)S(1)} %get-tuple-element.34), channel_id=1, replica_groups=mesh['seq'=32,'head'=4] {'seq'}, dimensions={0} | all-to-all | bytes 786432 | tf_op jit(solution)/shard_map/all_to_all | solution.py:478
  58.3 13.0 %all_to_all.11.refs_0_ = bf16[32,8,640]{2,1,0:T(8,128)(2,1)S(1)} all-to-all(bf16[32,8,640]{2,1,0:T(8,128)(2,1)S(1)} %scan.1), channel_id=1, replica_groups=mesh['seq'=32,'head'=4] {'seq'}, dimensions={0} | all-to-all | bytes 655360 | tf_op jit(solution)/shard_map/all_to_all | solution.py:488
  71.2 2.4 %out.1 = (bf16[64,2688]{1,0:T(8,128)(2,1)S(1)}, bf16[64,2688]{1,0:T(8,128)(2,1)S(1)}, bf16[32,2688]{1,0:T(8,128)(2,1)S(1)}, bf16[32,2688]{1,0:T(8,128)(2,1)S(1)}, bf16[64,2688]{1,0:T(8,128)(2,1)S(1)}) custom-call(bf16[32,8,640]{2,1,0:T(8,128)(2,1)S(1)} %all_to_all.11.refs_0_, bf16[256,128]{1,0:T(8,128)(2,1)S(1)} %get-tuple-element.35.refs_1_, ...), custom_call_target="tpu_custom_call" | custom-call | tf_op jit(solution)/shard_map/out/pallas_call | solution.py:492
  73.6 3.5 %collective-permute-start.10 = (bf16[64,2688]{1,0:T(8,128)(2,1)S(1)}, bf16[64,2688]{1,0:T(8,128)(2,1)S(1)}, u32[]{:S(2)}, u32[]{:S(2)}) collective-permute-start(bf16[64,2688]{1,0:T(8,128)(2,1)S(1)} %get-tuple-element.44), channel_id=1, source_target_pairs={{0,3},{1,0},{2,1},{3,2},{4,7},{5,4},{6,5},{7,6},{8,11},{9,8},{10,9... | collective-permute-start | bytes 1032200 | tf_op jit(solution)/shard_map/ppermute | solution.py:26
  77.1 1.3 %collective-permute-start.8 = (bf16[32,2688]{1,0:T(8,128)(2,1)S(1)}, bf16[32,2688]{1,0:T(8,128)(2,1)S(1)}, u32[]{:S(2)}, u32[]{:S(2)}) collective-permute-start(bf16[32,2688]{1,0:T(8,128)(2,1)S(1)} %get-tuple-element.42), channel_id=1, source_target_pairs={{0,2},{1,3},{2,0},{3,1},{4,6},{5,7},{6,4},{7,5},{8,10},{9,11},{10,... | collective-permute-start | bytes 516104 | tf_op jit(solution)/shard_map/ppermute | solution.py:26
  78.4 1.7 %collective-permute-start.9 = (bf16[32,2688]{1,0:T(8,128)(2,1)S(1)}, bf16[32,2688]{1,0:T(8,128)(2,1)S(1)}, u32[]{:S(2)}, u32[]{:S(2)}) collective-permute-start(bf16[32,2688]{1,0:T(8,128)(2,1)S(1)} %get-tuple-element.43), channel_id=1, source_target_pairs={{0,2},{1,3},{2,0},{3,1},{4,6},{5,7},{6,4},{7,5},{8,10},{9,11},{10,... | collective-permute-start | bytes 516104 | tf_op jit(solution)/shard_map/ppermute | solution.py:26
  80.1 10.2 %collective-permute-done.8.two = bf16[32,2688]{1,0:T(8,128)(2,1)S(1)} collective-permute-done((bf16[32,2688]{1,0:T(8,128)(2,1)S(1)}, bf16[32,2688]{1,0:T(8,128)(2,1)S(1)}, u32[]{:S(2)}, u32[]{:S(2)}) %collective-permute-start.8) | collective-permute-done | bytes 172064 | tf_op jit(solution)/shard_map/ppermute | solution.py:26
  90.3 3.7 %collective-permute-done.9.two_b = bf16[32,2688]{1,0:T(8,128)(2,1)S(1)} collective-permute-done((bf16[32,2688]{1,0:T(8,128)(2,1)S(1)}, bf16[32,2688]{1,0:T(8,128)(2,1)S(1)}, u32[]{:S(2)}, u32[]{:S(2)}) %collective-permute-start.9) | collective-permute-done | bytes 172064 | tf_op jit(solution)/shard_map/ppermute | solution.py:26
  94.0 1.0 %collective-permute-done.7.one = bf16[64,2688]{1,0:T(8,128)(2,1)S(1)} collective-permute-done((bf16[64,2688]{1,0:T(8,128)(2,1)S(1)}, bf16[64,2688]{1,0:T(8,128)(2,1)S(1)}, u32[]{:S(2)}, u32[]{:S(2)}) %collective-permute-start.7) | collective-permute-done | bytes 344096 | tf_op jit(solution)/shard_map/ppermute | solution.py:26
  95.1 1.0 %close.1 = bf16[64,2560]{1,0:T(8,128)(2,1)} custom-call(bf16[64,2688]{1,0:T(8,128)(2,1)S(1)} %get-tuple-element.40.own, bf16[64,2688]{1,0:T(8,128)(2,1)S(1)} %collective-permute-done.7.one, bf16[32,2688]{1,0:T(8,128)(2,1)S(1)} %collective-permute-done.8.two, bf16[32,2688]{1,0:T(8,128)(2,1)S(1)} %collective-permute-done.9.two_b, ...), custom_call_target="tpu_custom_call" | custom-call | tf_op jit(solution)/shard_map/close/pallas_call | solution.py:504
  (42 shorter events, 1.9 us)
Async XLA Ops:
  0.9 14.8 %collective-permute-start = (bf16[32,2560]{1,0:T(8,128)(2,1)S(1)}, bf16[32,2560]{1,0:T(8,128)(2,1)S(1)}, u32[]{:S(2)}, u32[]{:S(2)}) collective-permute-start(bf16[32,2560]{1,0:T(8,128)(2,1)S(1)} %slice.6), channel_id=1, source_target_pairs={{0,1},{1,2},{2,3},{3,0},{4,5},{5,6},{6,7},{7,4},{8,9},{9,10},{10,1... | collective-permute-start | bytes 491528 | tf_op jit(solution)/shard_map/ppermute | solution.py:26
  4.2 6.5 %collective-permute-start.3 = (bf16[8,2560]{1,0:T(8,128)(2,1)S(1)}, bf16[8,2560]{1,0:T(8,128)(2,1)S(1)}, u32[]{:S(2)}, u32[]{:S(2)}) collective-permute-start(bf16[8,2560]{1,0:T(8,128)(2,1)S(1)} %slice.7), channel_id=1, source_target_pairs={{3,4},{7,8},{11,12},{15,16},{19,20},{23,24},{27,28},{31,32},{35,36... | collective-permute-start | bytes 122888 | tf_op jit(solution)/shard_map/ppermute | solution.py:38
  11.8 17.0 %collective-permute-start.4 = (bf16[40,2560]{1,0:T(8,128)(2,1)S(1)}, bf16[40,2560]{1,0:T(8,128)(2,1)S(1)}, u32[]{:S(2)}, u32[]{:S(2)}) collective-permute-start(bf16[40,2560]{1,0:T(8,128)(2,1)S(1)} %join.1), channel_id=1, source_target_pairs={{0,1},{1,2},{2,3},{3,0},{4,5},{5,6},{6,7},{7,4},{8,9},{9,10},{10,1... | collective-permute-start | bytes 614408 | tf_op jit(solution)/shard_map/ppermute | solution.py:26
  11.8 17.0 %collective-permute-start.5 = (bf16[40,2560]{1,0:T(8,128)(2,1)S(1)}, bf16[40,2560]{1,0:T(8,128)(2,1)S(1)}, u32[]{:S(2)}, u32[]{:S(2)}) collective-permute-start(bf16[40,2560]{1,0:T(8,128)(2,1)S(1)} %join.1), channel_id=1, source_target_pairs={{0,3},{1,0},{2,1},{3,2},{4,7},{5,4},{6,5},{7,6},{8,11},{9,8},{10,9... | collective-permute-start | bytes 614408 | tf_op jit(solution)/shard_map/ppermute | solution.py:26
  14.5 14.3 %collective-permute-start.6 = (bf16[40,2560]{1,0:T(8,128)(2,1)S(1)}, bf16[40,2560]{1,0:T(8,128)(2,1)S(1)}, u32[]{:S(2)}, u32[]{:S(2)}) collective-permute-start(bf16[40,2560]{1,0:T(8,128)(2,1)S(1)} %join.1), channel_id=1, source_target_pairs={{0,2},{1,3},{2,0},{3,1},{4,6},{5,7},{6,4},{7,5},{8,10},{9,11},{10,... | collective-permute-start | bytes 614408 | tf_op jit(solution)/shard_map/ppermute | solution.py:26
  14.5 14.3 %collective-permute-start.1 = (bf16[32,2560]{1,0:T(8,128)(2,1)S(1)}, bf16[32,2560]{1,0:T(8,128)(2,1)S(1)}, u32[]{:S(2)}, u32[]{:S(2)}) collective-permute-start(bf16[32,2560]{1,0:T(8,128)(2,1)S(1)} %slice.6), channel_id=1, source_target_pairs={{0,3},{1,0},{2,1},{3,2},{4,7},{5,4},{6,5},{7,6},{8,11},{9,8},{10,9... | collective-permute-start | bytes 491528 | tf_op jit(solution)/shard_map/ppermute | solution.py:26
  15.8 13.0 %collective-permute-start.2 = (bf16[32,2560]{1,0:T(8,128)(2,1)S(1)}, bf16[32,2560]{1,0:T(8,128)(2,1)S(1)}, u32[]{:S(2)}, u32[]{:S(2)}) collective-permute-start(bf16[32,2560]{1,0:T(8,128)(2,1)S(1)} %slice.6), channel_id=1, source_target_pairs={{0,2},{1,3},{2,0},{3,1},{4,6},{5,7},{6,4},{7,5},{8,10},{9,11},{10,... | collective-permute-start | bytes 491528 | tf_op jit(solution)/shard_map/ppermute | solution.py:26
  18.9 2.9 %copy-start = (bf16[2560,1280]{1,0:T(8,128)(2,1)S(1)}, bf16[2560,1280]{1,0:T(8,128)(2,1)}, u32[]{:S(2)}) copy-start(bf16[2560,1280]{1,0:T(8,128)(2,1)} %refs_17_.1) | copy-start | bytes 19660804
  23.1 5.7 %copy-start.1 = (bf16[2560,1280]{1,0:T(8,128)(2,1)S(1)}, bf16[2560,1280]{1,0:T(8,128)(2,1)}, u32[]{:S(2)}) copy-start(bf16[2560,1280]{1,0:T(8,128)(2,1)} %refs_17_.1) | copy-start | bytes 19660804
  23.1 5.7 %copy-start.5 = (bf16[64,2560]{1,0:T(8,128)(2,1)S(1)}, bf16[64,2560]{1,0:T(8,128)(2,1)}, u32[]{:S(2)}) copy-start(bf16[64,2560]{1,0:T(8,128)(2,1)} %refs_1_.1) | copy-start | bytes 983044
  23.1 5.8 %copy-start.6 = (bf16[2560,20]{0,1:T(8,128)(2,1)S(1)}, bf16[2560,20]{0,1:T(8,128)(2,1)}, u32[]{:S(2)}) copy-start(bf16[2560,20]{0,1:T(8,128)(2,1)} %param.19) | copy-start | bytes 307204
  23.1 5.8 %copy-start.7 = (f32[4,1280]{1,0:T(4,128)S(1)}, f32[4,1280]{1,0:T(4,128)}, u32[]{:S(2)}) copy-start(f32[4,1280]{1,0:T(4,128)} %refs_15_.1) | copy-start | bytes 61444
  23.1 5.8 %copy-start.8 = (f32[4,256]{1,0:T(4,128)S(1)}, f32[4,256]{1,0:T(4,128)}, u32[]{:S(2)}) copy-start(f32[4,256]{1,0:T(4,128)} %refs_14_.1) | copy-start | bytes 12292
  23.1 5.8 %copy-start.9 = (s32[64]{0:T(128)S(1)}, s32[64]{0:T(128)}, u32[]{:S(2)}) copy-start(s32[64]{0:T(128)} %param.27) | copy-start | bytes 772
  23.1 5.8 %copy-start.10 = (f32[20]{0:T(128)S(1)}, f32[20]{0:T(128)}, u32[]{:S(2)}) copy-start(f32[20]{0:T(128)} %param.20) | copy-start | bytes 244
  23.1 5.8 %copy-start.11 = (s32[20]{0:T(128)S(1)}, s32[20]{0:T(128)}, u32[]{:S(2)}) copy-start(s32[20]{0:T(128)} %param.21) | copy-start | bytes 244
  28.9 5.9 %copy-start.2 = (bf16[2560,1280]{1,0:T(8,128)(2,1)S(1)}, bf16[2560,1280]{1,0:T(8,128)(2,1)}, u32[]{:S(2)}) copy-start(bf16[2560,1280]{1,0:T(8,128)(2,1)} %refs_7_.1) | copy-start | bytes 19660804
  28.9 5.9 %copy-start.12 = (f32[20]{0:T(128)S(1)}, f32[20]{0:T(128)}, u32[]{:S(2)}) copy-start(f32[20]{0:T(128)} %param.24) | copy-start | bytes 244
  34.7 36.5 %slice-start = ((s8[6553600]{0:T(1024)(128)(4,1)}), s8[4194304]{0:T(1024)(128)(4,1)S(1)}, s32[]{:S(2)}) async-start(s8[6553600]{0:T(1024)(128)(4,1)} %bitcast.5), calls=%async_computation.2 | async-start | bytes 8388608
  34.8 36.5 %slice-start.1 = ((s8[6553600]{0:T(1024)(128)(4,1)}), s8[2359296]{0:T(1024)(128)(4,1)S(1)}, s32[]{:S(2)}) async-start(s8[6553600]{0:T(1024)(128)(4,1)} %bitcast.5), calls=%async_computation.3 | async-start | bytes 4718592
  73.6 20.4 %collective-permute-start.10 = (bf16[64,2688]{1,0:T(8,128)(2,1)S(1)}, bf16[64,2688]{1,0:T(8,128)(2,1)S(1)}, u32[]{:S(2)}, u32[]{:S(2)}) collective-permute-start(bf16[64,2688]{1,0:T(8,128)(2,1)S(1)} %get-tuple-element.44), channel_id=1, source_target_pairs={{0,3},{1,0},{2,1},{3,2},{4,7},{5,4},{6,5},{7,6},{8,11},{9,8},{10,9... | collective-permute-start | bytes 1032200 | tf_op jit(solution)/shard_map/ppermute | solution.py:26
  77.1 18.0 %collective-permute-start.7 = (bf16[64,2688]{1,0:T(8,128)(2,1)S(1)}, bf16[64,2688]{1,0:T(8,128)(2,1)S(1)}, u32[]{:S(2)}, u32[]{:S(2)}) collective-permute-start(bf16[64,2688]{1,0:T(8,128)(2,1)S(1)} %get-tuple-element.41), channel_id=1, source_target_pairs={{0,1},{1,2},{2,3},{3,0},{4,5},{5,6},{6,7},{7,4},{8,9},{9,10},{10,1... | collective-permute-start | bytes 1032200 | tf_op jit(solution)/shard_map/ppermute | solution.py:26
  77.1 13.2 %collective-permute-start.8 = (bf16[32,2688]{1,0:T(8,128)(2,1)S(1)}, bf16[32,2688]{1,0:T(8,128)(2,1)S(1)}, u32[]{:S(2)}, u32[]{:S(2)}) collective-permute-start(bf16[32,2688]{1,0:T(8,128)(2,1)S(1)} %get-tuple-element.42), channel_id=1, source_target_pairs={{0,2},{1,3},{2,0},{3,1},{4,6},{5,7},{6,4},{7,5},{8,10},{9,11},{10,... | collective-permute-start | bytes 516104 | tf_op jit(solution)/shard_map/ppermute | solution.py:26
  78.4 15.6 %collective-permute-start.9 = (bf16[32,2688]{1,0:T(8,128)(2,1)S(1)}, bf16[32,2688]{1,0:T(8,128)(2,1)S(1)}, u32[]{:S(2)}, u32[]{:S(2)}) collective-permute-start(bf16[32,2688]{1,0:T(8,128)(2,1)S(1)} %get-tuple-element.43), channel_id=1, source_target_pairs={{0,2},{1,3},{2,0},{3,1},{4,6},{5,7},{6,4},{7,5},{8,10},{9,11},{10,... | collective-permute-start | bytes 516104 | tf_op jit(solution)/shard_map/ppermute | solution.py:26
  (2 other events, 2.3 us)

commit v8 on v6

--- a/solution.py
+++ b/solution.py
@@ -26,7 +26,7 @@
     return lax.ppermute(block, axis, [(i, (i + distance) % size) for i in range(size)])
 
 
-def gather_tokens(tokens, inner_weight, state_weight):
+def gather_tokens(tokens, inner_weight, state_weight, gate_weight):
     heads = lax.axis_size("head")
     blocks = lax.axis_size("seq")
     rows, width = tokens.shape
@@ -41,11 +41,11 @@
     (near,) = call(
         near_kernel,
         "near",
-        [vmem()] * 2,
+        [vmem()] * 3,
         [jax.ShapeDtypeStruct((RIM, LANES), tokens.dtype)],
         [],
         BLOCK_LIMIT,
-    )(inner_weight, state_weight)
+    )(inner_weight, state_weight, gate_weight)
     (tail,) = call(
         tail_kernel,
         "tail",
@@ -94,8 +94,10 @@
     return jnp.dot(a, b, preferred_element_type=F32)
 
 
-def near_kernel(inner_w, state_w, near):
-    near[...] = inner_w[0:RIM, 0:LANES] + state_w[0:RIM, 0:LANES]
+def near_kernel(inner_w, state_w, gate_w, near):
+    near[...] = (
+        inner_w[0:RIM, 0:LANES] + state_w[0:RIM, 0:LANES] + gate_w[0:RIM, 0:LANES]
+    )
 
 
 def tail_kernel(below, above, own, near, tail):
@@ -113,24 +115,68 @@
     return sum(dot(part.astype(BF16), copies) for part in split3(x))
 
 
-def block_kernel(
-    lens_row,
+def norm_rows(x, gain):
+    x = x.astype(F32)
+    mean = jnp.mean(x * x, axis=-1, keepdims=True)
+    return (x * lax.rsqrt(mean + 1e-05) * gain).astype(BF16)
+
+
+def project_kernel(
     own,
     below,
     above,
     top,
     bottom,
+    gain,
+    step_w,
+    state_w,
+    inner_w,
+    gate_w,
+    step_raw,
+    state_raw,
+    inner_raw,
+    gate,
+    normed,
+):
+    rows = own.shape[0]
+    half = rows // 2
+    here = lax.axis_index("head")
+
+    def put(owner, offset, x):
+        start = pl.multiple_of(owner * rows + offset, half)
+        normed[pl.ds(start, x.shape[0]), :] = norm_rows(x[...], gain[...])
+
+    far = (here + 2) % 4
+    put(here, 0, own)
+    put((here + 3) % 4, 0, below)
+    put((here + 1) % 4, 0, above)
+    put(far, 0, top)
+    put(far, half, bottom)
+    step_raw[...] = lax.dot_general(
+        normed[...], step_w[...], (((1,), (1,)), ((), ())), preferred_element_type=F32
+    )
+    state_raw[...] = dot(normed[...], state_w[...]).astype(BF16)
+    inner_raw[...] = dot(normed[...], inner_w[...]).astype(BF16)
+    for c in range(gate.shape[1] // CHUNK):
+        cols = slice(c * CHUNK, (c + 1) * CHUNK)
+        vals = dot(normed[...], gate_w[:, cols]).astype(BF16).astype(F32)
+        gate[:, cols] = vals * jax.nn.sigmoid(vals)
+
+
+def block_kernel(
+    lens_row,
     rim,
     rim_far,
     gain,
-    step_w,
+    step_raw,
+    state_raw,
+    inner_raw,
     step_bias,
     rate,
     taps_state,
     taps_inner,
     state_w,
     inner_w,
-    normed_out,
     sent,
     conv_out,
     scaled_out,
@@ -139,34 +185,17 @@
     scores_out,
     maps_out,
     head_decay_out,
-    normed,
     local,
     *,
     heads_here,
 ):
-    rows = own.shape[0]
-    length = normed.shape[0] - RIM
-    here = lax.axis_index("head")
+    length = inner_raw.shape[0]
     first = lax.axis_index("seq") * length
-
-    def norm(x):
-        x = x.astype(F32)
-        mean = jnp.mean(x * x, axis=-1, keepdims=True)
-        return (x * lax.rsqrt(mean + 1e-05) * gain[...]).astype(BF16)
-
-    def put(owner, offset, x):
-        start = pl.multiple_of(RIM + owner * rows + offset, RIM)
-        normed[pl.ds(start, x.shape[0]), :] = norm(x)
-
-    half = rows // 2
-    put(here, 0, own[...])
-    put((here + 3) % 4, 0, below[...])
-    put((here + 1) % 4, 0, above[...])
-    far = (here + 2) % 4
-    put(far, 0, top[...])
-    put(far, half, bottom[...])
-    normed[0:RIM, :] = norm(rim[...] + rim_far[...])
-    normed_out[...] = normed[RIM:, :]
+    rim_rows = norm_rows(rim[...] + rim_far[...], gain[...])
+
+    def behind(weight, raw):
+        before = dot(rim_rows, weight[...]).astype(BF16).astype(F32)
+        return jnp.concatenate([before, raw[...].astype(F32)], axis=0)
 
     passages = lens_row.shape[1]
     up = lax.broadcasted_iota(jnp.int32, (passages, passages), 0)
@@ -200,12 +229,9 @@
             acc = acc + taps[lag : lag + 1] * moved * same
         return (acc * jax.nn.sigmoid(acc)).astype(BF16)
 
-    x = lax.dot_general(
-        normed[RIM:, :], step_w[...], (((1,), (1,)), ((), ())), preferred_element_type=F32
-    )
-    x = repeat_lanes(x + step_bias[...])
+    x = repeat_lanes(step_raw[...] + step_bias[...])
     rates = jnp.broadcast_to(rate[...].astype(F32) * 2.0 ** (-21), (8, rate.shape[1]))
-    raw = dot(normed[...], state_w[...]).astype(BF16).astype(F32)
+    raw = behind(state_w, state_raw)
     maps = conv(raw, taps_state[...])
     maps_in = maps[:, :N]
     maps_out[...] = maps[:, N:]
@@ -232,7 +258,7 @@
     cum_out[...] = by_lane(cum, heads_here)
     cum_rows[...] = cum.T
 
-    raw = dot(normed[...], inner_w[...]).astype(BF16).astype(F32)
+    raw = behind(inner_w, inner_raw)
     mixed = conv(raw, taps_inner[...])
     conv_out[...] = mixed
     spread = spread_matrix(0, local.shape[1], heads_here)
@@ -251,16 +277,13 @@
 
 
 def inside_kernel(
-    normed,
     scaled,
     conv,
     cum,
     cum_rows,
     scores,
     skip,
-    gate_w,
     inside,
-    gate,
     *,
     heads_here,
 ):
@@ -293,8 +316,6 @@
         inside[:, cols] = jnp.concatenate([upper, lower], axis=0) + (
             skips * conv[:, cols].astype(F32)
         )
-        vals = dot(normed[...], gate_w[:, cols]).astype(BF16).astype(F32)
-        gate[:, cols] = vals * jax.nn.sigmoid(vals)
 
 
 def scan_kernel(got, back, *, heads_here):
@@ -421,17 +442,43 @@
     length = heads * rows
     passages = passage_lengths.shape[0]
     span = channels // 2
-    below, above, top, bottom, rim, rim_far = gather_tokens(tokens, inner_weight, state_weight)
+    below, above, top, bottom, rim, rim_far = gather_tokens(
+        tokens, inner_weight, state_weight, gate_weight
+    )
 
     def shape(dims, kind):
         return jax.ShapeDtypeStruct(dims, kind)
 
-    normed, sent, conv, scaled, cum, cum_rows, scores, maps, head_decay = call(
+    gain = input_gain[None]
+    step_raw, state_raw, inner_raw, gate = call(
+        project_kernel,
+        "project",
+        [vmem()] * 10,
+        [
+            shape((length, heads_here), F32),
+            shape((length, 2 * N), BF16),
+            shape((length, channels), BF16),
+            shape((length, channels), F32),
+        ],
+        [pltpu.VMEM((length, width), BF16)],
+        BLOCK_LIMIT,
+    )(
+        tokens,
+        below,
+        above,
+        top,
+        bottom,
+        gain,
+        step_weight.T,
+        state_weight,
+        inner_weight,
+        gate_weight,
+    )
+    sent, conv, scaled, cum, cum_rows, scores, maps, head_decay = call(
         lambda *refs: block_kernel(*refs, heads_here=heads_here),
         "block",
-        [vmem()] * 16,
+        [vmem()] * 13,
         [
-            shape((length, width), BF16),
             shape((blocks, 8, span + LANES), BF16),
             shape((length, channels), BF16),
             shape((length, channels), BF16),
@@ -441,22 +488,16 @@
             shape((length, N), BF16),
             shape((length, LANES), BF16),
         ],
-        [
-            pltpu.VMEM((length + RIM, width), BF16),
-            pltpu.VMEM((N, channels), F32),
-        ],
+        [pltpu.VMEM((N, channels), F32)],
         BLOCK_LIMIT,
     )(
         passage_lengths[None],
-        tokens,
-        below,
-        above,
-        top,
-        bottom,
         rim,
         rim_far,
-        input_gain[None],
-        step_weight.T,
+        gain,
+        step_raw,
+        state_raw,
+        inner_raw,
         step_bias[None],
         decay_exponent[None],
         conv_state,
@@ -465,14 +506,14 @@
         inner_weight,
     )
 
-    inside, gate = call(
+    (inside,) = call(
         lambda *refs: inside_kernel(*refs, heads_here=heads_here),
         "inside",
-        [vmem()] * 8,
-        [shape((length, channels), F32), shape((length, channels), F32)],
+        [vmem()] * 6,
+        [shape((length, channels), F32)],
         [],
         INSIDE_LIMIT,
-    )(normed, scaled, conv, cum, cum_rows, scores, skip_gain[None], gate_weight)
+    )(scaled, conv, cum, cum_rows, scores, skip_gain[None])
     sent, inside, gate, out_gain = lax.optimization_barrier(
         (sent, inside, gate, norm_gain[None])
     )

time: 89.4 us -> 86.8 us (0.971)
  local copies, waits for them, and re-layouts: 7.02 us -> 9.94 us
  starting transfers between devices: 22.3 us -> 19.4 us
  blocking collectives: 31.4 us -> 30 us
  waiting for transfers between devices: 15.1 us -> 13.8 us
    pallas_call x1 -> x2, Pallas kernels: 0.01 us -> 4.89 us  [the longest x1 4.88 us: on_device(): call(project_kernel, 'project', [vmem()] * 10, [shape((length, heads_here...]
    pallas_call x1, Pallas kernels: 5.75 us -> 2.72 us  [on_device(): call(lambda *refs: block_kernel(*refs, heads_here=heads_here), 'block', [...]
    unnamed x32 -> x30, local copies, waits for them, and re-layouts: 5.1 us -> 8.02 us
    ppermute x1, starting transfers between devices: 7.61 us -> 4.75 us  [gather_tokens(): lax.ppermute(tail, ('seq', 'head'), route)]
    pallas_call x1, Pallas kernels: 3.61 us -> 1.73 us  [on_device(): call(lambda *refs: inside_kernel(*refs, heads_here=heads_here), 'inside',...]
    all_to_all x1, blocking collectives: 18.4 us -> 17 us  [on_device(): got = lax.all_to_all(sent, 'seq', 0, 0, tiled=True)]
    ppermute x1, waiting for transfers between devices: 1.38 us -> 0.01 us  [gather_tokens(): lax.ppermute(tail, ('seq', 'head'), route)]
  transfers between devices with their start and end apart: 10 -> 10, of which waited for: 3 -> 2; matrix products, arithmetic and copies ran while one was open for 2% -> 2% of each run, Pallas kernels for 0% -> 6%
where the time goes in v8:
time: 86.8 us; the launch traced here: 86.4 us
  blocking collectives  30 us (35%)
  starting transfers between devices  19.4 us (22%)
  waiting for transfers between devices  13.8 us (16%)
  Pallas kernels  13 us (15%)
  local copies, waits for them, and re-layouts  9.94 us (11%)
    all_to_all x1, blocking collectives, on_device(): got = lax.all_to_all(sent, 'seq', 0, 0, tiled=True)  17 us
    ppermute x8, starting transfers between devices, around(): lax.ppermute(block, axis, [(i, (i + distance) % size) for i in range(size)])  14 us
    ppermute x8, waiting for transfers between devices, around(): lax.ppermute(block, axis, [(i, (i + distance) % size) for i in range(size)])  13.7 us
    all_to_all x1, blocking collectives, on_device(): states = lax.all_to_all(back, 'seq', 0, 0, tiled=True)  13 us
    unnamed x30, local copies, waits for them, and re-layouts  8.02 us
    pallas_call x1, Pallas kernels, on_device(): call(project_kernel, 'project', [vmem()] * 10, [shape((length, heads_here...  4.88 us
    ppermute x1, starting transfers between devices, gather_tokens(): lax.ppermute(tail, ('seq', 'head'), route)  4.75 us
    pallas_call x1, Pallas kernels, on_device(): call(lambda *refs: block_kernel(*refs, heads_here=heads_here), 'block', [...  2.72 us
  transfers between devices with their start and end apart: 10, of which 2 were waited for; matrix products, arithmetic and copies ran while one was open for 2% of the time, Pallas kernels for 6%

profile of v8, /device:TPU:1, one launch (start us, length us, event | category | flops | bytes accessed | tf_op | source)
XLA Modules:
  0.0 86.4 jit_solution(2523634166918750788)
XLA Ops:
  0.0 2.5 %collective-permute-start = (bf16[64,2560]{1,0:T(8,128)(2,1)}, bf16[64,2560]{1,0:T(8,128)(2,1)S(1)}, u32[]{:S(2)}, u32[]{:S(2)}) collective-permute-start(bf16[64,2560]{1,0:T(8,128)(2,1)} %own.3), channel_id=1, source_target_pairs={{0,1},{1,2},{2,3},{3,0},{4,5},{5,6},{6,7},{7,4},{8,9},{9,10},{10,1... | collective-permute-start | bytes 983048 | tf_op jit(solution)/shard_map/ppermute | solution.py:26
  2.5 2.1 %collective-permute-start.1 = (bf16[64,2560]{1,0:T(8,128)(2,1)}, bf16[64,2560]{1,0:T(8,128)(2,1)S(1)}, u32[]{:S(2)}, u32[]{:S(2)}) collective-permute-start(bf16[64,2560]{1,0:T(8,128)(2,1)} %own.3), channel_id=1, source_target_pairs={{0,3},{1,0},{2,1},{3,2},{4,7},{5,4},{6,5},{7,6},{8,11},{9,8},{10,9... | collective-permute-start | bytes 983048 | tf_op jit(solution)/shard_map/ppermute | solution.py:26
  4.6 1.0 %fusion = (bf16[32,2560]{1,0:T(8,128)(2,1)S(1)}, bf16[32,2560]{1,0:T(8,128)(2,1)S(1)}) fusion(bf16[64,2560]{1,0:T(8,128)(2,1)} %own.3), kind=kLoop, calls=%fused_computation | loop fusion | bytes 655360 | tf_op jit(solution)/shard_map/slice | solution.py:36
  5.6 1.4 %collective-permute-start.4 = (bf16[32,2560]{1,0:T(8,128)(2,1)S(1)}, bf16[32,2560]{1,0:T(8,128)(2,1)S(1)}, u32[]{:S(2)}, u32[]{:S(2)}) collective-permute-start(bf16[32,2560]{1,0:T(8,128)(2,1)S(1)} %get-tuple-element.48), channel_id=1, source_target_pairs={{0,2},{1,3},{2,0},{3,1},{4,6},{5,7},{6,4},{7,5},{8,10},{9,11},{10,... | collective-permute-start | bytes 491528 | tf_op jit(solution)/shard_map/ppermute | solution.py:26
  7.0 1.7 %collective-permute-start.5 = (bf16[32,2560]{1,0:T(8,128)(2,1)S(1)}, bf16[32,2560]{1,0:T(8,128)(2,1)S(1)}, u32[]{:S(2)}, u32[]{:S(2)}) collective-permute-start(bf16[32,2560]{1,0:T(8,128)(2,1)S(1)} %get-tuple-element.47), channel_id=1, source_target_pairs={{0,2},{1,3},{2,0},{3,1},{4,6},{5,7},{6,4},{7,5},{8,10},{9,11},{10,... | collective-permute-start | bytes 491528 | tf_op jit(solution)/shard_map/ppermute | solution.py:26
  8.7 0.9 %slice.9 = bf16[16,2560]{1,0:T(8,128)(2,1)S(1)} slice(bf16[64,2560]{1,0:T(8,128)(2,1)} %own.3), slice={[48:64], [0:2560]} | slice | bytes 163840 | tf_op jit(solution)/shard_map/slice | solution.py:40
  9.6 0.7 collective-permute-start.3
  10.2 2.9 %copy-done = bf16[2560,1280]{1,0:T(8,128)(2,1)S(1)} copy-done((bf16[2560,1280]{1,0:T(8,128)(2,1)S(1)}, bf16[2560,1280]{1,0:T(8,128)(2,1)}, u32[]{:S(2)}) %copy-start) | copy-done | bytes 6553624
  13.1 2.9 %copy-done.1 = bf16[2560,1280]{1,0:T(8,128)(2,1)S(1)} copy-done((bf16[2560,1280]{1,0:T(8,128)(2,1)S(1)}, bf16[2560,1280]{1,0:T(8,128)(2,1)}, u32[]{:S(2)}) %copy-start.1) | copy-done | bytes 6553624
  15.9 1.3 %copy-done.2 = bf16[2560,256]{1,0:T(8,128)(2,1)S(1)} copy-done((bf16[2560,256]{1,0:T(8,128)(2,1)S(1)}, bf16[2560,256]{1,0:T(8,128)(2,1)}, u32[]{:S(2)}) %copy-start.2) | copy-done | bytes 1310744
  17.3 0.9 %copy-done.3 = bf16[64,2560]{1,0:T(8,128)(2,1)S(1)} copy-done((bf16[64,2560]{1,0:T(8,128)(2,1)S(1)}, bf16[64,2560]{1,0:T(8,128)(2,1)}, u32[]{:S(2)}) %copy-start.3) | copy-done | bytes 327704
  18.3 4.8 %collective-permute-start.2 = (bf16[16,2560]{1,0:T(8,128)(2,1)S(1)}, bf16[16,2560]{1,0:T(8,128)(2,1)S(1)}, u32[]{:S(2)}, u32[]{:S(2)}) collective-permute-start(bf16[16,2560]{1,0:T(8,128)(2,1)S(1)} %tail.1), channel_id=1, source_target_pairs={{0,4},{2,6},{3,7},{4,8},{6,10},{7,11},{8,12},{10,14},{11,15},{12,1... | collective-permute-start | bytes 245768 | tf_op jit(solution)/shard_map/ppermute | solution.py:63
  23.2 4.9 %project.1 = (f32[256,20]{1,0:T(8,128)S(1)}, bf16[256,256]{1,0:T(8,128)(2,1)S(1)}, bf16[256,1280]{1,0:T(8,128)(2,1)S(1)}, f32[256,1280]{1,0:T(8,128)S(1)}) custom-call(bf16[64,2560]{1,0:T(8,128)(2,1)S(1)} %copy-done.3, bf16[64,2560]{1,0:T(8,128)(2,1)S(1)} %collective-permute-done.below, bf16[64,2560]{1,0:T(8,128)(2,1)S(1)} %collective-permute-done.1.above, ...), custom_call_target="tpu_custom_call" | custom-call | tf_op jit(solution)/shard_map/project/pallas_call | solution.py:453
  28.1 2.7 %block.1 = (bf16[32,8,768]{2,1,0:T(8,128)(2,1)S(1)}, bf16[256,1280]{1,0:T(8,128)(2,1)S(1)}, bf16[256,1280]{1,0:T(8,128)(2,1)S(1)}, bf16[256,128]{1,0:T(8,128)(2,...) custom-call(s32[1,64]{1,0:T(1,128)S(1)} %bitcast.8, ...), custom_call_target="tpu_custom_call" | custom-call | tf_op jit(solution)/shard_map/block/pallas_call | solution.py:477
  30.9 1.7 %inside.1.refs_3_ = f32[256,1280]{1,0:T(8,128)S(1)} custom-call(bf16[256,1280]{1,0:T(8,128)(2,1)S(1)} %get-tuple-element.30.refs_0_, bf16[256,1280]{1,0:T(8,128)(2,1)S(1)} %get-tuple-element.31.refs_1_, bf16[256,128]{1,0:T(8,128)(2,1)S(1)} %get-tuple-element.32.refs_2_, f32[128,256]{1,0:T(8,128)S(1)} %get-tuple-element.33.refs_3_, ...), custom_call_target="tpu_custom_call" | custom-call | tf_op jit(solution)/shard_map/inside/pallas_call | solution.py:509
  32.6 17.0 %all_to_all.10.refs_0_ = bf16[32,8,768]{2,1,0:T(8,128)(2,1)S(1)} all-to-all(bf16[32,8,768]{2,1,0:T(8,128)(2,1)S(1)} %get-tuple-element.36), channel_id=1, replica_groups=mesh['seq'=32,'head'=4] {'seq'}, dimensions={0} | all-to-all | bytes 786432 | tf_op jit(solution)/shard_map/all_to_all | solution.py:520
  49.9 13.0 %all_to_all.11.refs_0_ = bf16[32,8,640]{2,1,0:T(8,128)(2,1)S(1)} all-to-all(bf16[32,8,640]{2,1,0:T(8,128)(2,1)S(1)} %scan.1), channel_id=1, replica_groups=mesh['seq'=32,'head'=4] {'seq'}, dimensions={0} | all-to-all | bytes 655360 | tf_op jit(solution)/shard_map/all_to_all | solution.py:530
  62.9 2.4 %out.1 = (bf16[64,2688]{1,0:T(8,128)(2,1)S(1)}, bf16[64,2688]{1,0:T(8,128)(2,1)S(1)}, bf16[32,2688]{1,0:T(8,128)(2,1)S(1)}, bf16[32,2688]{1,0:T(8,128)(2,1)S(1)}, bf16[64,2688]{1,0:T(8,128)(2,1)S(1)}) custom-call(bf16[32,8,640]{2,1,0:T(8,128)(2,1)S(1)} %all_to_all.11.refs_0_, bf16[256,128]{1,0:T(8,128)(2,1)S(1)} %get-tuple-element.37.refs_1_, ...), custom_call_target="tpu_custom_call" | custom-call | tf_op jit(solution)/shard_map/out/pallas_call | solution.py:534
  65.8 2.9 %collective-permute-start.9 = (bf16[64,2688]{1,0:T(8,128)(2,1)S(1)}, bf16[64,2688]{1,0:T(8,128)(2,1)S(1)}, u32[]{:S(2)}, u32[]{:S(2)}) collective-permute-start(bf16[64,2688]{1,0:T(8,128)(2,1)S(1)} %get-tuple-element.46), channel_id=1, source_target_pairs={{0,3},{1,0},{2,1},{3,2},{4,7},{5,4},{6,5},{7,6},{8,11},{9,8},{10,9... | collective-permute-start | bytes 1032200 | tf_op jit(solution)/shard_map/ppermute | solution.py:26
  68.7 1.1 %collective-permute-start.7 = (bf16[32,2688]{1,0:T(8,128)(2,1)S(1)}, bf16[32,2688]{1,0:T(8,128)(2,1)S(1)}, u32[]{:S(2)}, u32[]{:S(2)}) collective-permute-start(bf16[32,2688]{1,0:T(8,128)(2,1)S(1)} %get-tuple-element.44), channel_id=1, source_target_pairs={{0,2},{1,3},{2,0},{3,1},{4,6},{5,7},{6,4},{7,5},{8,10},{9,11},{10,... | collective-permute-start | bytes 516104 | tf_op jit(solution)/shard_map/ppermute | solution.py:26
  69.8 1.9 %collective-permute-start.8 = (bf16[32,2688]{1,0:T(8,128)(2,1)S(1)}, bf16[32,2688]{1,0:T(8,128)(2,1)S(1)}, u32[]{:S(2)}, u32[]{:S(2)}) collective-permute-start(bf16[32,2688]{1,0:T(8,128)(2,1)S(1)} %get-tuple-element.45), channel_id=1, source_target_pairs={{0,2},{1,3},{2,0},{3,1},{4,6},{5,7},{6,4},{7,5},{8,10},{9,11},{10,... | collective-permute-start | bytes 516104 | tf_op jit(solution)/shard_map/ppermute | solution.py:26
  71.7 10.0 %collective-permute-done.7.two = bf16[32,2688]{1,0:T(8,128)(2,1)S(1)} collective-permute-done((bf16[32,2688]{1,0:T(8,128)(2,1)S(1)}, bf16[32,2688]{1,0:T(8,128)(2,1)S(1)}, u32[]{:S(2)}, u32[]{:S(2)}) %collective-permute-start.7) | collective-permute-done | bytes 172064 | tf_op jit(solution)/shard_map/ppermute | solution.py:26
  81.7 3.7 %collective-permute-done.8.two_b = bf16[32,2688]{1,0:T(8,128)(2,1)S(1)} collective-permute-done((bf16[32,2688]{1,0:T(8,128)(2,1)S(1)}, bf16[32,2688]{1,0:T(8,128)(2,1)S(1)}, u32[]{:S(2)}, u32[]{:S(2)}) %collective-permute-start.8) | collective-permute-done | bytes 172064 | tf_op jit(solution)/shard_map/ppermute | solution.py:26
  85.4 1.0 %close.1 = bf16[64,2560]{1,0:T(8,128)(2,1)} custom-call(bf16[64,2688]{1,0:T(8,128)(2,1)S(1)} %get-tuple-element.42.own, bf16[64,2688]{1,0:T(8,128)(2,1)S(1)} %collective-permute-done.6.one, bf16[32,2688]{1,0:T(8,128)(2,1)S(1)} %collective-permute-done.7.two, bf16[32,2688]{1,0:T(8,128)(2,1)S(1)} %collective-permute-done.8.two_b, ...), custom_call_target="tpu_custom_call" | custom-call | tf_op jit(solution)/shard_map/close/pallas_call | solution.py:546
  (41 shorter events, 0.9 us)
Async XLA Ops:
  0.0 17.3 %collective-permute-start = (bf16[64,2560]{1,0:T(8,128)(2,1)}, bf16[64,2560]{1,0:T(8,128)(2,1)S(1)}, u32[]{:S(2)}, u32[]{:S(2)}) collective-permute-start(bf16[64,2560]{1,0:T(8,128)(2,1)} %own.3), channel_id=1, source_target_pairs={{0,1},{1,2},{2,3},{3,0},{4,5},{5,6},{6,7},{7,4},{8,9},{9,10},{10,1... | collective-permute-start | bytes 983048 | tf_op jit(solution)/shard_map/ppermute | solution.py:26
  2.5 14.8 %collective-permute-start.1 = (bf16[64,2560]{1,0:T(8,128)(2,1)}, bf16[64,2560]{1,0:T(8,128)(2,1)S(1)}, u32[]{:S(2)}, u32[]{:S(2)}) collective-permute-start(bf16[64,2560]{1,0:T(8,128)(2,1)} %own.3), channel_id=1, source_target_pairs={{0,3},{1,0},{2,1},{3,2},{4,7},{5,4},{6,5},{7,6},{8,11},{9,8},{10,9... | collective-permute-start | bytes 983048 | tf_op jit(solution)/shard_map/ppermute | solution.py:26
  5.6 17.5 %collective-permute-start.4 = (bf16[32,2560]{1,0:T(8,128)(2,1)S(1)}, bf16[32,2560]{1,0:T(8,128)(2,1)S(1)}, u32[]{:S(2)}, u32[]{:S(2)}) collective-permute-start(bf16[32,2560]{1,0:T(8,128)(2,1)S(1)} %get-tuple-element.48), channel_id=1, source_target_pairs={{0,2},{1,3},{2,0},{3,1},{4,6},{5,7},{6,4},{7,5},{8,10},{9,11},{10,... | collective-permute-start | bytes 491528 | tf_op jit(solution)/shard_map/ppermute | solution.py:26
  7.0 16.1 %collective-permute-start.5 = (bf16[32,2560]{1,0:T(8,128)(2,1)S(1)}, bf16[32,2560]{1,0:T(8,128)(2,1)S(1)}, u32[]{:S(2)}, u32[]{:S(2)}) collective-permute-start(bf16[32,2560]{1,0:T(8,128)(2,1)S(1)} %get-tuple-element.47), channel_id=1, source_target_pairs={{0,2},{1,3},{2,0},{3,1},{4,6},{5,7},{6,4},{7,5},{8,10},{9,11},{10,... | collective-permute-start | bytes 491528 | tf_op jit(solution)/shard_map/ppermute | solution.py:26
  9.6 18.5 %collective-permute-start.3 = (bf16[16,2560]{1,0:T(8,128)(2,1)S(1)}, bf16[16,2560]{1,0:T(8,128)(2,1)S(1)}, u32[]{:S(2)}, u32[]{:S(2)}) collective-permute-start(bf16[16,2560]{1,0:T(8,128)(2,1)S(1)} %slice.9), channel_id=1, source_target_pairs={{3,5},{7,9},{11,13},{15,17},{19,21},{23,25},{27,29},{31,33},{35,37... | collective-permute-start | bytes 245768 | tf_op jit(solution)/shard_map/ppermute | solution.py:40
  10.2 2.9 %copy-start = (bf16[2560,1280]{1,0:T(8,128)(2,1)S(1)}, bf16[2560,1280]{1,0:T(8,128)(2,1)}, u32[]{:S(2)}) copy-start(bf16[2560,1280]{1,0:T(8,128)(2,1)} %refs_12_.1) | copy-start | bytes 19660804
  13.1 2.9 %copy-start.1 = (bf16[2560,1280]{1,0:T(8,128)(2,1)S(1)}, bf16[2560,1280]{1,0:T(8,128)(2,1)}, u32[]{:S(2)}) copy-start(bf16[2560,1280]{1,0:T(8,128)(2,1)} %gate_w.3) | copy-start | bytes 19660804
  15.9 1.3 %copy-start.2 = (bf16[2560,256]{1,0:T(8,128)(2,1)S(1)}, bf16[2560,256]{1,0:T(8,128)(2,1)}, u32[]{:S(2)}) copy-start(bf16[2560,256]{1,0:T(8,128)(2,1)} %refs_11_.1) | copy-start | bytes 3932164
  17.3 5.8 %copy-start.11 = (f32[2560]{0:T(1024)S(1)}, f32[2560]{0:T(1024)}, u32[]{:S(2)}) copy-start(f32[2560]{0:T(1024)} %param.15) | copy-start | bytes 30724
  17.3 5.8 %copy-start.12 = (f32[1280]{0:T(1024)S(1)}, f32[1280]{0:T(1024)}, u32[]{:S(2)}) copy-start(f32[1280]{0:T(1024)} %param.25) | copy-start | bytes 15364
  17.3 5.8 %copy-start.4 = (bf16[2560,20]{0,1:T(8,128)(2,1)S(1)}, bf16[2560,20]{0,1:T(8,128)(2,1)}, u32[]{:S(2)}) copy-start(bf16[2560,20]{0,1:T(8,128)(2,1)} %param.19) | copy-start | bytes 307204
  18.3 9.8 %collective-permute-start.2 = (bf16[16,2560]{1,0:T(8,128)(2,1)S(1)}, bf16[16,2560]{1,0:T(8,128)(2,1)S(1)}, u32[]{:S(2)}, u32[]{:S(2)}) collective-permute-start(bf16[16,2560]{1,0:T(8,128)(2,1)S(1)} %tail.1), channel_id=1, source_target_pairs={{0,4},{2,6},{3,7},{4,8},{6,10},{7,11},{8,12},{10,14},{11,15},{12,1... | collective-permute-start | bytes 245768 | tf_op jit(solution)/shard_map/ppermute | solution.py:63
  23.1 5.0 %copy-start.5 = (f32[4,1280]{1,0:T(4,128)S(1)}, f32[4,1280]{1,0:T(4,128)}, u32[]{:S(2)}) copy-start(f32[4,1280]{1,0:T(4,128)} %refs_10_.1) | copy-start | bytes 61444
  23.1 5.0 %copy-start.6 = (f32[4,256]{1,0:T(4,128)S(1)}, f32[4,256]{1,0:T(4,128)}, u32[]{:S(2)}) copy-start(f32[4,256]{1,0:T(4,128)} %refs_9_.1) | copy-start | bytes 12292
  23.1 5.0 %copy-start.7 = (s32[64]{0:T(128)S(1)}, s32[64]{0:T(128)}, u32[]{:S(2)}) copy-start(s32[64]{0:T(128)} %param.27) | copy-start | bytes 772
  23.1 5.0 %copy-start.8 = (f32[20]{0:T(128)S(1)}, f32[20]{0:T(128)}, u32[]{:S(2)}) copy-start(f32[20]{0:T(128)} %param.20) | copy-start | bytes 244
  23.1 5.0 %copy-start.9 = (s32[20]{0:T(128)S(1)}, s32[20]{0:T(128)}, u32[]{:S(2)}) copy-start(s32[20]{0:T(128)} %param.21) | copy-start | bytes 244
  28.0 2.8 %copy-start.10 = (f32[20]{0:T(128)S(1)}, f32[20]{0:T(128)}, u32[]{:S(2)}) copy-start(f32[20]{0:T(128)} %param.24) | copy-start | bytes 244
  28.1 34.8 %slice-start = ((s8[6553600]{0:T(1024)(128)(4,1)}), s8[4194304]{0:T(1024)(128)(4,1)S(1)}, s32[]{:S(2)}) async-start(s8[6553600]{0:T(1024)(128)(4,1)} %bitcast.5), calls=%async_computation.2 | async-start | bytes 8388608
  28.1 34.8 %slice-start.1 = ((s8[6553600]{0:T(1024)(128)(4,1)}), s8[2359296]{0:T(1024)(128)(4,1)S(1)}, s32[]{:S(2)}) async-start(s8[6553600]{0:T(1024)(128)(4,1)} %bitcast.5), calls=%async_computation.3 | async-start | bytes 4718592
  65.3 20.1 %collective-permute-start.6 = (bf16[64,2688]{1,0:T(8,128)(2,1)S(1)}, bf16[64,2688]{1,0:T(8,128)(2,1)S(1)}, u32[]{:S(2)}, u32[]{:S(2)}) collective-permute-start(bf16[64,2688]{1,0:T(8,128)(2,1)S(1)} %get-tuple-element.43), channel_id=1, source_target_pairs={{0,1},{1,2},{2,3},{3,0},{4,5},{5,6},{6,7},{7,4},{8,9},{9,10},{10,1... | collective-permute-start | bytes 1032200 | tf_op jit(solution)/shard_map/ppermute | solution.py:26
  65.8 19.6 %collective-permute-start.9 = (bf16[64,2688]{1,0:T(8,128)(2,1)S(1)}, bf16[64,2688]{1,0:T(8,128)(2,1)S(1)}, u32[]{:S(2)}, u32[]{:S(2)}) collective-permute-start(bf16[64,2688]{1,0:T(8,128)(2,1)S(1)} %get-tuple-element.46), channel_id=1, source_target_pairs={{0,3},{1,0},{2,1},{3,2},{4,7},{5,4},{6,5},{7,6},{8,11},{9,8},{10,9... | collective-permute-start | bytes 1032200 | tf_op jit(solution)/shard_map/ppermute | solution.py:26
  68.7 13.0 %collective-permute-start.7 = (bf16[32,2688]{1,0:T(8,128)(2,1)S(1)}, bf16[32,2688]{1,0:T(8,128)(2,1)S(1)}, u32[]{:S(2)}, u32[]{:S(2)}) collective-permute-start(bf16[32,2688]{1,0:T(8,128)(2,1)S(1)} %get-tuple-element.44), channel_id=1, source_target_pairs={{0,2},{1,3},{2,0},{3,1},{4,6},{5,7},{6,4},{7,5},{8,10},{9,11},{10,... | collective-permute-start | bytes 516104 | tf_op jit(solution)/shard_map/ppermute | solution.py:26
  69.8 15.6 %collective-permute-start.8 = (bf16[32,2688]{1,0:T(8,128)(2,1)S(1)}, bf16[32,2688]{1,0:T(8,128)(2,1)S(1)}, u32[]{:S(2)}, u32[]{:S(2)}) collective-permute-start(bf16[32,2688]{1,0:T(8,128)(2,1)S(1)} %get-tuple-element.45), channel_id=1, source_target_pairs={{0,2},{1,3},{2,0},{3,1},{4,6},{5,7},{6,4},{7,5},{8,10},{9,11},{10,... | collective-permute-start | bytes 516104 | tf_op jit(solution)/shard_map/ppermute | solution.py:26
  (1 other events, 1.0 us)

commit v9 on v8

--- a/solution.py
+++ b/solution.py
@@ -340,21 +340,13 @@
     gate,
     norm_gain,
     out_w,
-    out0,
-    out1,
-    out2,
-    out2b,
-    out3,
+    part,
     states,
     x,
-    sums,
     *,
     heads_here,
 ):
     length = inside.shape[0]
-    rows = length // 4
-    half = rows // 2
-    here = lax.axis_index("head")
     span = got.shape[2]
     for piece in range(got.shape[0]):
         group, side = piece // 2, piece % 2
@@ -368,38 +360,26 @@
         carried = dot(maps[...], states[:, cols].astype(BF16)) * dot(head_decay[...], spread)
         gated = (inside[:, cols] + carried) * gate[:, cols]
         total = total + jnp.sum(gated * gated, axis=1, keepdims=True)
-        ready = (gated * norm_gain[:, cols]).astype(BF16)
-        for b in range(4):
-            start = pl.multiple_of(((b + 4 - here) % 4) * rows, rows)
-            x[pl.ds(start, rows), cols] = ready[b * rows : (b + 1) * rows]
-    packed = by_lane(jnp.broadcast_to(total, (length, LANES)), 1)
-    for b in range(4):
-        start = pl.multiple_of(((b + 4 - here) % 4) * rows, rows)
-        sums[pl.ds(start, rows), :] = packed[b * rows : (b + 1) * rows]
-
-    def put(cols, part):
-        out0[:, cols] = part[0:rows]
-        out1[:, cols] = part[rows : 2 * rows]
-        out2[:, cols] = part[2 * rows : 2 * rows + half]
-        out2b[:, cols] = part[2 * rows + half : 3 * rows]
-        out3[:, cols] = part[3 * rows :]
-
+        x[:, cols] = (gated * norm_gain[:, cols]).astype(BF16)
     width = out_w.shape[1]
     for c in range(width // WIDE):
         cols = slice(c * WIDE, (c + 1) * WIDE)
-        put(cols, dot(x[...], out_w[:, cols]).astype(BF16))
-    put(slice(width, width + LANES), sums[...])
-
-
-def close_kernel(own, one, two, two_b, three, mixed):
-    width = mixed.shape[1]
-    half = two.shape[0]
-    for i, far in enumerate((two, two_b)):
-        rows = slice(i * half, (i + 1) * half)
-        total = own[rows, :].astype(F32) + one[rows, :].astype(F32)
-        total = total + far[...].astype(F32) + three[rows, :].astype(F32)
+        part[:, cols] = dot(x[...], out_w[:, cols]).astype(BF16)
+    part[:, width:] = by_lane(jnp.broadcast_to(total, (length, LANES)), 1)
+
+
+def close_kernel(parts, mixed):
+    rows, width = mixed.shape
+    half = rows // 2
+    for start in (0, half):
+        total = sum(
+            parts[peer * rows + start : peer * rows + start + half, :].astype(F32)
+            for peer in range(parts.shape[0] // rows)
+        )
         mean = jnp.sum(total[:, width:], axis=1, keepdims=True) / (H * P_SIZE)
-        mixed[rows, :] = (total[:, :width] * lax.rsqrt(mean + 1e-05)).astype(BF16)
+        mixed[start : start + half, :] = (
+            total[:, :width] * lax.rsqrt(mean + 1e-05)
+        ).astype(BF16)
 
 
 def vmem():
@@ -531,32 +511,25 @@
 
     out_width = out_weight.shape[1]
     packed = out_width + LANES
-    own, one, two, two_b, three = call(
+    (part,) = call(
         lambda *refs: out_kernel(*refs, heads_here=heads_here),
         "out",
         [vmem()] * 7,
-        [shape((n, packed), BF16) for n in (rows, rows, rows // 2, rows // 2, rows)],
+        [shape((length, packed), BF16)],
         [
             pltpu.VMEM((N, channels), F32),
             pltpu.VMEM((length, channels), BF16),
-            pltpu.VMEM((length, LANES), BF16),
         ],
         OUT_LIMIT,
     )(states, maps, head_decay, inside, gate, out_gain, out_weight)
     (mixed,) = call(
         close_kernel,
         "close",
-        [vmem()] * 5,
+        [vmem()],
         [shape((rows, out_width), BF16)],
         [],
         SMALL_LIMIT,
-    )(
-        own,
-        around(one, "head", 1),
-        around(two, "head", 2),
-        around(two_b, "head", 2),
-        around(three, "head", 3),
-    )
+    )(lax.all_to_all(part, "head", 0, 0, tiled=True))
     return mixed
 
 

time: 86.8 us -> 89.3 us (1.029)
  blocking collectives: 30 us -> 52.5 us
  waiting for transfers between devices: 13.8 us -> 0.02 us
  starting transfers between devices: 19.4 us -> 13.3 us
    all_to_all x0 -> x1, blocking collectives: none -> 22.5 us  [on_device(): lax.all_to_all(part, 'head', 0, 0, tiled=True)]
    ppermute x8 -> x4, waiting for transfers between devices: 13.7 us -> 0.01 us  [around(): lax.ppermute(block, axis, [(i, (i + distance) % size) for i in range(size)])]
    ppermute x8 -> x4, starting transfers between devices: 14 us -> 7.64 us  [around(): lax.ppermute(block, axis, [(i, (i + distance) % size) for i in range(size)])]
  transfers between devices with their start and end apart: 10 -> 6, of which waited for: 2 -> 0; matrix products, arithmetic and copies ran while one was open for 2% -> 2% of each run, Pallas kernels for 6% -> 6%
where the time goes in v9:
time: 89.3 us; the launch traced here: 88.9 us
  blocking collectives  52.5 us (59%)
  starting transfers between devices  13.3 us (15%)
  Pallas kernels  12.9 us (14%)
  local copies, waits for them, and re-layouts  9.94 us (11%)
    all_to_all x1, blocking collectives, on_device(): lax.all_to_all(part, 'head', 0, 0, tiled=True)  22.5 us
    all_to_all x1, blocking collectives, on_device(): got = lax.all_to_all(sent, 'seq', 0, 0, tiled=True)  17 us
    all_to_all x1, blocking collectives, on_device(): states = lax.all_to_all(back, 'seq', 0, 0, tiled=True)  13 us
    unnamed x30, local copies, waits for them, and re-layouts  8.02 us
    ppermute x4, starting transfers between devices, around(): lax.ppermute(block, axis, [(i, (i + distance) % size) for i in range(size)])  7.64 us
    ppermute x1, starting transfers between devices, gather_tokens(): lax.ppermute(tail, ('seq', 'head'), route)  5.01 us
    pallas_call x1, Pallas kernels, on_device(): call(project_kernel, 'project', [vmem()] * 10, [shape((length, heads_here...  4.89 us
    pallas_call x1, Pallas kernels, on_device(): call(lambda *refs: block_kernel(*refs, heads_here=heads_here), 'block', [...  2.7 us
  transfers between devices with their start and end apart: 6, of which 0 were waited for; matrix products, arithmetic and copies ran while one was open for 2% of the time, Pallas kernels for 6%

profile of v9, /device:TPU:1, one launch (start us, length us, event | category | flops | bytes accessed | tf_op | source)
XLA Modules:
  0.0 88.9 jit_solution(17006897055872320167)
XLA Ops:
  0.0 2.5 %collective-permute-start = (bf16[64,2560]{1,0:T(8,128)(2,1)}, bf16[64,2560]{1,0:T(8,128)(2,1)S(1)}, u32[]{:S(2)}, u32[]{:S(2)}) collective-permute-start(bf16[64,2560]{1,0:T(8,128)(2,1)} %own.3), channel_id=1, source_target_pairs={{0,1},{1,2},{2,3},{3,0},{4,5},{5,6},{6,7},{7,4},{8,9},{9,10},{10,1... | collective-permute-start | bytes 983048 | tf_op jit(solution)/shard_map/ppermute | solution.py:26
  2.5 2.1 %collective-permute-start.1 = (bf16[64,2560]{1,0:T(8,128)(2,1)}, bf16[64,2560]{1,0:T(8,128)(2,1)S(1)}, u32[]{:S(2)}, u32[]{:S(2)}) collective-permute-start(bf16[64,2560]{1,0:T(8,128)(2,1)} %own.3), channel_id=1, source_target_pairs={{0,3},{1,0},{2,1},{3,2},{4,7},{5,4},{6,5},{7,6},{8,11},{9,8},{10,9... | collective-permute-start | bytes 983048 | tf_op jit(solution)/shard_map/ppermute | solution.py:26
  4.6 1.0 %fusion = (bf16[32,2560]{1,0:T(8,128)(2,1)S(1)}, bf16[32,2560]{1,0:T(8,128)(2,1)S(1)}) fusion(bf16[64,2560]{1,0:T(8,128)(2,1)} %own.3), kind=kLoop, calls=%fused_computation | loop fusion | bytes 655360 | tf_op jit(solution)/shard_map/slice | solution.py:36
  5.6 1.4 %collective-permute-start.4 = (bf16[32,2560]{1,0:T(8,128)(2,1)S(1)}, bf16[32,2560]{1,0:T(8,128)(2,1)S(1)}, u32[]{:S(2)}, u32[]{:S(2)}) collective-permute-start(bf16[32,2560]{1,0:T(8,128)(2,1)S(1)} %get-tuple-element.38), channel_id=1, source_target_pairs={{0,2},{1,3},{2,0},{3,1},{4,6},{5,7},{6,4},{7,5},{8,10},{9,11},{10,... | collective-permute-start | bytes 491528 | tf_op jit(solution)/shard_map/ppermute | solution.py:26
  7.0 1.7 %collective-permute-start.5 = (bf16[32,2560]{1,0:T(8,128)(2,1)S(1)}, bf16[32,2560]{1,0:T(8,128)(2,1)S(1)}, u32[]{:S(2)}, u32[]{:S(2)}) collective-permute-start(bf16[32,2560]{1,0:T(8,128)(2,1)S(1)} %get-tuple-element.37), channel_id=1, source_target_pairs={{0,2},{1,3},{2,0},{3,1},{4,6},{5,7},{6,4},{7,5},{8,10},{9,11},{10,... | collective-permute-start | bytes 491528 | tf_op jit(solution)/shard_map/ppermute | solution.py:26
  8.7 0.9 %slice.9 = bf16[16,2560]{1,0:T(8,128)(2,1)S(1)} slice(bf16[64,2560]{1,0:T(8,128)(2,1)} %own.3), slice={[48:64], [0:2560]} | slice | bytes 163840 | tf_op jit(solution)/shard_map/slice | solution.py:40
  9.6 0.7 collective-permute-start.3
  10.2 2.9 %copy-done = bf16[2560,1280]{1,0:T(8,128)(2,1)S(1)} copy-done((bf16[2560,1280]{1,0:T(8,128)(2,1)S(1)}, bf16[2560,1280]{1,0:T(8,128)(2,1)}, u32[]{:S(2)}) %copy-start) | copy-done | bytes 6553624
  13.1 2.9 %copy-done.1 = bf16[2560,1280]{1,0:T(8,128)(2,1)S(1)} copy-done((bf16[2560,1280]{1,0:T(8,128)(2,1)S(1)}, bf16[2560,1280]{1,0:T(8,128)(2,1)}, u32[]{:S(2)}) %copy-start.1) | copy-done | bytes 6553624
  15.9 1.3 %copy-done.2 = bf16[2560,256]{1,0:T(8,128)(2,1)S(1)} copy-done((bf16[2560,256]{1,0:T(8,128)(2,1)S(1)}, bf16[2560,256]{1,0:T(8,128)(2,1)}, u32[]{:S(2)}) %copy-start.2) | copy-done | bytes 1310744
  17.3 0.9 %copy-done.3 = bf16[64,2560]{1,0:T(8,128)(2,1)S(1)} copy-done((bf16[64,2560]{1,0:T(8,128)(2,1)S(1)}, bf16[64,2560]{1,0:T(8,128)(2,1)}, u32[]{:S(2)}) %copy-start.3) | copy-done | bytes 327704
  18.3 5.0 %collective-permute-start.2 = (bf16[16,2560]{1,0:T(8,128)(2,1)S(1)}, bf16[16,2560]{1,0:T(8,128)(2,1)S(1)}, u32[]{:S(2)}, u32[]{:S(2)}) collective-permute-start(bf16[16,2560]{1,0:T(8,128)(2,1)S(1)} %tail.1), channel_id=1, source_target_pairs={{0,4},{2,6},{3,7},{4,8},{6,10},{7,11},{8,12},{10,14},{11,15},{12,1... | collective-permute-start | bytes 245768 | tf_op jit(solution)/shard_map/ppermute | solution.py:63
  23.4 0.0 copy-start.6
  23.4 0.0 copy-start.7
  23.4 0.0 slice-start.1
  23.4 4.9 %project.1 = (f32[256,20]{1,0:T(8,128)S(1)}, bf16[256,256]{1,0:T(8,128)(2,1)S(1)}, bf16[256,1280]{1,0:T(8,128)(2,1)S(1)}, f32[256,1280]{1,0:T(8,128)S(1)}) custom-call(bf16[64,2560]{1,0:T(8,128)(2,1)S(1)} %copy-done.3, bf16[64,2560]{1,0:T(8,128)(2,1)S(1)} %collective-permute-done.below, bf16[64,2560]{1,0:T(8,128)(2,1)S(1)} %collective-permute-done.1.above, ...), custom_call_target="tpu_custom_call" | custom-call | tf_op jit(solution)/shard_map/project/pallas_call | solution.py:433
  28.4 2.7 %block.1 = (bf16[32,8,768]{2,1,0:T(8,128)(2,1)S(1)}, bf16[256,1280]{1,0:T(8,128)(2,1)S(1)}, bf16[256,1280]{1,0:T(8,128)(2,1)S(1)}, bf16[256,128]{1,0:T(8,128)(2,...) custom-call(s32[1,64]{1,0:T(1,128)S(1)} %bitcast.12, ...), custom_call_target="tpu_custom_call" | custom-call | tf_op jit(solution)/shard_map/block/pallas_call | solution.py:457
  31.1 1.7 %inside.1.refs_3_ = f32[256,1280]{1,0:T(8,128)S(1)} custom-call(bf16[256,1280]{1,0:T(8,128)(2,1)S(1)} %get-tuple-element.25.refs_0_, bf16[256,1280]{1,0:T(8,128)(2,1)S(1)} %get-tuple-element.26.refs_1_, bf16[256,128]{1,0:T(8,128)(2,1)S(1)} %get-tuple-element.27.refs_2_, f32[128,256]{1,0:T(8,128)S(1)} %get-tuple-element.28.refs_3_, ...), custom_call_target="tpu_custom_call" | custom-call | tf_op jit(solution)/shard_map/inside/pallas_call | solution.py:489
  32.9 17.0 %all_to_all.21.refs_0_ = bf16[32,8,768]{2,1,0:T(8,128)(2,1)S(1)} all-to-all(bf16[32,8,768]{2,1,0:T(8,128)(2,1)S(1)} %get-tuple-element.31), channel_id=1, replica_groups=mesh['seq'=32,'head'=4] {'seq'}, dimensions={0} | all-to-all | bytes 786432 | tf_op jit(solution)/shard_map/all_to_all | solution.py:500
  49.9 0.3 scan.1
  50.1 13.0 %all_to_all.22.refs_0_ = bf16[32,8,640]{2,1,0:T(8,128)(2,1)S(1)} all-to-all(bf16[32,8,640]{2,1,0:T(8,128)(2,1)S(1)} %scan.1), channel_id=1, replica_groups=mesh['seq'=32,'head'=4] {'seq'}, dimensions={0} | all-to-all | bytes 655360 | tf_op jit(solution)/shard_map/all_to_all | solution.py:510
  63.1 2.3 %out.1 = bf16[256,2688]{1,0:T(8,128)(2,1)S(1)} custom-call(bf16[32,8,640]{2,1,0:T(8,128)(2,1)S(1)} %all_to_all.22.refs_0_, bf16[256,128]{1,0:T(8,128)(2,1)S(1)} %get-tuple-element.32.refs_1_, bf16[256,128]{1,0:T(8,128)(2,1)S(1)} %get-tuple-element.33.refs_2_, f32[256,1280]{1,0:T(8,128)S(1)} %inside.1.refs_3_, f32[256,1280]{1,0:T(8,128)S(1)} %get-tuple-element.35.refs_4_, ...), custom_call_target="tpu_custom_call" | custom-call | tf_op jit(solution)/shard_map/out/pallas_call | solution.py:514
  65.4 22.5 %all_to_all.23 = bf16[4,64,2688]{2,1,0:T(8,128)(2,1)S(1)} all-to-all(bf16[4,64,2688]{2,1,0:T(8,128)(2,1)S(1)} %bitcast.10), channel_id=1, replica_groups=mesh['seq'=32,'head'=4] {'head'}, dimensions={0} | all-to-all | bytes 2752512 | tf_op jit(solution)/shard_map/all_to_all | solution.py:532
  87.9 1.0 %close.1 = bf16[64,2560]{1,0:T(8,128)(2,1)} custom-call(bf16[256,2688]{1,0:T(8,128)(2,1)S(1)} %bitcast.9), custom_call_target="tpu_custom_call" | custom-call | tf_op jit(solution)/shard_map/close/pallas_call | solution.py:525
  (34 shorter events, 0.1 us)
Async XLA Ops:
  0.0 17.3 %collective-permute-start = (bf16[64,2560]{1,0:T(8,128)(2,1)}, bf16[64,2560]{1,0:T(8,128)(2,1)S(1)}, u32[]{:S(2)}, u32[]{:S(2)}) collective-permute-start(bf16[64,2560]{1,0:T(8,128)(2,1)} %own.3), channel_id=1, source_target_pairs={{0,1},{1,2},{2,3},{3,0},{4,5},{5,6},{6,7},{7,4},{8,9},{9,10},{10,1... | collective-permute-start | bytes 983048 | tf_op jit(solution)/shard_map/ppermute | solution.py:26
  2.5 14.8 %collective-permute-start.1 = (bf16[64,2560]{1,0:T(8,128)(2,1)}, bf16[64,2560]{1,0:T(8,128)(2,1)S(1)}, u32[]{:S(2)}, u32[]{:S(2)}) collective-permute-start(bf16[64,2560]{1,0:T(8,128)(2,1)} %own.3), channel_id=1, source_target_pairs={{0,3},{1,0},{2,1},{3,2},{4,7},{5,4},{6,5},{7,6},{8,11},{9,8},{10,9... | collective-permute-start | bytes 983048 | tf_op jit(solution)/shard_map/ppermute | solution.py:26
  5.6 17.7 %collective-permute-start.4 = (bf16[32,2560]{1,0:T(8,128)(2,1)S(1)}, bf16[32,2560]{1,0:T(8,128)(2,1)S(1)}, u32[]{:S(2)}, u32[]{:S(2)}) collective-permute-start(bf16[32,2560]{1,0:T(8,128)(2,1)S(1)} %get-tuple-element.38), channel_id=1, source_target_pairs={{0,2},{1,3},{2,0},{3,1},{4,6},{5,7},{6,4},{7,5},{8,10},{9,11},{10,... | collective-permute-start | bytes 491528 | tf_op jit(solution)/shard_map/ppermute | solution.py:26
  7.0 16.3 %collective-permute-start.5 = (bf16[32,2560]{1,0:T(8,128)(2,1)S(1)}, bf16[32,2560]{1,0:T(8,128)(2,1)S(1)}, u32[]{:S(2)}, u32[]{:S(2)}) collective-permute-start(bf16[32,2560]{1,0:T(8,128)(2,1)S(1)} %get-tuple-element.37), channel_id=1, source_target_pairs={{0,2},{1,3},{2,0},{3,1},{4,6},{5,7},{6,4},{7,5},{8,10},{9,11},{10,... | collective-permute-start | bytes 491528 | tf_op jit(solution)/shard_map/ppermute | solution.py:26
  9.6 18.8 %collective-permute-start.3 = (bf16[16,2560]{1,0:T(8,128)(2,1)S(1)}, bf16[16,2560]{1,0:T(8,128)(2,1)S(1)}, u32[]{:S(2)}, u32[]{:S(2)}) collective-permute-start(bf16[16,2560]{1,0:T(8,128)(2,1)S(1)} %slice.9), channel_id=1, source_target_pairs={{3,5},{7,9},{11,13},{15,17},{19,21},{23,25},{27,29},{31,33},{35,37... | collective-permute-start | bytes 245768 | tf_op jit(solution)/shard_map/ppermute | solution.py:40
  10.2 2.9 %copy-start = (bf16[2560,1280]{1,0:T(8,128)(2,1)S(1)}, bf16[2560,1280]{1,0:T(8,128)(2,1)}, u32[]{:S(2)}) copy-start(bf16[2560,1280]{1,0:T(8,128)(2,1)} %refs_12_.1) | copy-start | bytes 19660804
  13.1 2.9 %copy-start.1 = (bf16[2560,1280]{1,0:T(8,128)(2,1)S(1)}, bf16[2560,1280]{1,0:T(8,128)(2,1)}, u32[]{:S(2)}) copy-start(bf16[2560,1280]{1,0:T(8,128)(2,1)} %gate_w.3) | copy-start | bytes 19660804
  15.9 1.3 %copy-start.2 = (bf16[2560,256]{1,0:T(8,128)(2,1)S(1)}, bf16[2560,256]{1,0:T(8,128)(2,1)}, u32[]{:S(2)}) copy-start(bf16[2560,256]{1,0:T(8,128)(2,1)} %refs_11_.1) | copy-start | bytes 3932164
  17.3 1.0 %copy-start.3 = (bf16[64,2560]{1,0:T(8,128)(2,1)S(1)}, bf16[64,2560]{1,0:T(8,128)(2,1)}, u32[]{:S(2)}) copy-start(bf16[64,2560]{1,0:T(8,128)(2,1)} %own.3) | copy-start | bytes 983044
  17.3 6.0 %copy-start.11 = (f32[2560]{0:T(1024)S(1)}, f32[2560]{0:T(1024)}, u32[]{:S(2)}) copy-start(f32[2560]{0:T(1024)} %param.15) | copy-start | bytes 30724
  17.3 6.0 %copy-start.12 = (f32[1280]{0:T(1024)S(1)}, f32[1280]{0:T(1024)}, u32[]{:S(2)}) copy-start(f32[1280]{0:T(1024)} %param.25) | copy-start | bytes 15364
  17.3 6.1 %copy-start.4 = (bf16[2560,20]{0,1:T(8,128)(2,1)S(1)}, bf16[2560,20]{0,1:T(8,128)(2,1)}, u32[]{:S(2)}) copy-start(bf16[2560,20]{0,1:T(8,128)(2,1)} %param.19) | copy-start | bytes 307204
  18.2 44.9 %slice-start = ((s8[6553600]{0:T(1024)(128)(4,1)}), s8[4194304]{0:T(1024)(128)(4,1)S(1)}, s32[]{:S(2)}) async-start(s8[6553600]{0:T(1024)(128)(4,1)} %bitcast.7), calls=%async_computation.3 | async-start | bytes 8388608
  18.3 10.1 %collective-permute-start.2 = (bf16[16,2560]{1,0:T(8,128)(2,1)S(1)}, bf16[16,2560]{1,0:T(8,128)(2,1)S(1)}, u32[]{:S(2)}, u32[]{:S(2)}) collective-permute-start(bf16[16,2560]{1,0:T(8,128)(2,1)S(1)} %tail.1), channel_id=1, source_target_pairs={{0,4},{2,6},{3,7},{4,8},{6,10},{7,11},{8,12},{10,14},{11,15},{12,1... | collective-permute-start | bytes 245768 | tf_op jit(solution)/shard_map/ppermute | solution.py:63
  23.4 5.0 %copy-start.5 = (f32[4,1280]{1,0:T(4,128)S(1)}, f32[4,1280]{1,0:T(4,128)}, u32[]{:S(2)}) copy-start(f32[4,1280]{1,0:T(4,128)} %refs_10_.1) | copy-start | bytes 61444
  23.4 5.0 %copy-start.6 = (f32[4,256]{1,0:T(4,128)S(1)}, f32[4,256]{1,0:T(4,128)}, u32[]{:S(2)}) copy-start(f32[4,256]{1,0:T(4,128)} %refs_9_.1) | copy-start | bytes 12292
  23.4 5.0 %copy-start.7 = (s32[64]{0:T(128)S(1)}, s32[64]{0:T(128)}, u32[]{:S(2)}) copy-start(s32[64]{0:T(128)} %param.27) | copy-start | bytes 772
  23.4 5.0 %copy-start.8 = (f32[20]{0:T(128)S(1)}, f32[20]{0:T(128)}, u32[]{:S(2)}) copy-start(f32[20]{0:T(128)} %param.20) | copy-start | bytes 244
  23.4 5.0 %copy-start.9 = (s32[20]{0:T(128)S(1)}, s32[20]{0:T(128)}, u32[]{:S(2)}) copy-start(s32[20]{0:T(128)} %param.21) | copy-start | bytes 244
  23.4 39.7 %slice-start.1 = ((s8[6553600]{0:T(1024)(128)(4,1)}), s8[2359296]{0:T(1024)(128)(4,1)S(1)}, s32[]{:S(2)}) async-start(s8[6553600]{0:T(1024)(128)(4,1)} %bitcast.7), calls=%async_computation.4 | async-start | bytes 4718592
  28.4 2.7 %copy-start.10 = (f32[20]{0:T(128)S(1)}, f32[20]{0:T(128)}, u32[]{:S(2)}) copy-start(f32[20]{0:T(128)} %param.24) | copy-start | bytes 244
